TPU v7x, 128 devices: a whole 4x4x4 slice. The times are simulated.
128 devices in a mesh: seq: 32 (over x, y, core), head: 4 (over z).
Axes of the slice: x: 4, y: 4, z: 4, core: 2. Of those that a mesh axis runs over, the one named last changes fastest.
Arguments:
- q2: bfloat16 [8192, 4096], P('seq', 'head'), may hold values from -128 to 128
- k2: bfloat16 [8192, 512], P('seq', 'head'), may hold values from -6 to 6
- v2: bfloat16 [8192, 512], P('seq', 'head'), may hold values from -6 to 6
- hidden: bfloat16 [8192, 8192], P('seq', 'head'), may hold values from -120 to 120
- w_query: bfloat16 [8192, 4096], P(None, 'head'), may hold values from -0.0625 to 0.0625
- b_query: float32 [4096], P('head'), may hold values from -3 to 3
- w_key: bfloat16 [8192, 512], P(None, 'head'), may hold values from -0.0625 to 0.0625
- b_key: float32 [512], P('head'), may hold values from -3 to 3
- w_value: bfloat16 [8192, 512], P(None, 'head'), may hold values from -0.0625 to 0.0625
- b_value: float32 [512], P('head'), may hold values from -3 to 3
- kept_index: int32 [8192], P('seq'), may hold values from 0 to 127, as said below
- block_count: int32 [64], P('seq'), may hold values from 0 to 128, as said below
- text_rows: int32 [256], replicated, may hold values from 0 to 8191, as said below
Outputs:
- attn2: bfloat16 [8192, 4096], P('seq', 'head')
- importance: float32 [8192], P('seq')
- attn3: bfloat16 [4224, 4096], P('seq', 'head')
Inputs may be any that keep to these rules, and one draw needn't show every extreme that they name: `kept_index`: in each aligned block of 128 rows, the first block_count entries are the in-block indices of that block's kept rows in ascending order; the other entries are the block's remaining indices. `block_count`: every text row is kept, and exactly 4224 rows are kept in all. For every k, the rows 2 * k * 256 to (2 * k + 2) * 256 - 1 hold exactly 264 kept rows together. `text_rows`: Distinct, in ascending order.
All inputs are finite; a program needn't handle non-finite values.
Results may differ from a plain program's by a relative error of at most 0.0093.
Values may be sent and summed in bfloat16 or wider, within the bound.
No kernel may reach another device: no remote copies, remote signals or barrier semaphores. Data moves between devices by JAX's collectives and lax.ppermute only.
A program may use at most 128 MiB of HBM per device.

v0:
```python
import math

import jax
import jax.numpy as jnp
from jax import lax
from jax.sharding import PartitionSpec as P

HD = 128
GROUP = 8
BLOCK = 128
TEXT = 256


def side_by_side(arrays, axis, dim, along):
    ends, at = ([], 0)
    for a in arrays[:-1]:
        at += a.shape[along]
        ends.append(at)
    both = jnp.concatenate(arrays, axis=along)
    return tuple(jnp.split(lax.all_gather(both, axis, axis=dim, tiled=True), ends, axis=along))


def copy_for_each(x, axis):
    count = lax.axis_size(axis)
    return lax.all_to_all(jnp.broadcast_to(x[None], (count, *x.shape)), axis, 0, 0, tiled=True)


def over_copies(x, axis):
    everything = copy_for_each(x, axis)
    return jnp.sum(everything, axis=0)


def folded_in_pairs(pieces, combine):
    while len(jax.tree.leaves(pieces)[0]) > 1:
        pieces = jax.vmap(combine)(*(pieces[side::2] for side in (0, 1)))
    return pieces[0]


def prefix(x, axis, combine, identity):
    count, index = (lax.axis_size(axis), lax.axis_index(axis))
    passed = jnp.arange(count) < index

    def kept(part, zero, own):
        part = jnp.where(
            passed.reshape(-1, *(1 for _ in own.shape)), part, jnp.asarray(zero, own.dtype)
        )
        return part

    pieces = copy_for_each(x, axis)
    return folded_in_pairs(kept(pieces, identity, x), combine)


def shifted(block, axis, distance):
    devices = range(lax.axis_size(axis))
    route = [(i - distance, i) for i in devices if i - distance in devices]
    return lax.ppermute(block, axis, route)


def in_order(pieces, dim):
    lengths = list(pieces.shape[1:])
    lengths[dim] *= pieces.shape[0]
    return jnp.moveaxis(pieces, 0, dim).reshape(lengths)


def collect(x, axis, dim):
    pieces = copy_for_each(x, axis)
    return in_order(pieces, dim)


def rotate(values, positions):
    half = values.shape[-1] // 2
    freqs = 1000000.0 ** (-(jnp.arange(half, dtype=jnp.float32) * 2.0) / values.shape[-1])
    angles = positions.astype(jnp.float32)[:, None] * freqs[None, :]
    cosine = jnp.cos(angles)[:, None, :]
    sine = jnp.sin(angles)[:, None, :]
    first = values[..., :half]
    second = values[..., half:]
    return jnp.concatenate(
        [first * cosine - second * sine, second * cosine + first * sine], axis=-1
    )


def start_carry(count):
    return (
        jnp.full((GROUP, count), -1e30, jnp.float32),
        jnp.zeros((GROUP, count), jnp.float32),
        jnp.zeros((count, GROUP, HD), jnp.float32),
    )


def finish(carry):
    _, total, summed = carry
    return (summed / total.T[:, :, None]).reshape(summed.shape[0], -1).astype(jnp.bfloat16)


def attend(carry, queries, keys, values, query_pos, key_pos, key_live):
    count = keys.shape[0]
    width = 512 if count % 512 == 0 else count
    scale = 1.0 / math.sqrt(HD)

    def step(state, block):
        top, total, summed = state
        key_block, value_block, place_block, live_block = block
        scores = (
            jnp.einsum("qgd,kd->gqk", queries, key_block, preferred_element_type=jnp.float32)
            * scale
        )
        allowed = ((place_block[None, :] <= query_pos[:, None]) & live_block[None, :])[None]
        new_top = jnp.maximum(top, jnp.max(jnp.where(allowed, scores, -1e30), axis=-1))
        rescale = jnp.exp(top - new_top)
        weights = jnp.where(allowed, jnp.exp(scores - new_top[..., None]), 0.0)
        total = total * rescale + jnp.sum(weights, axis=-1)
        summed = summed * rescale.T[:, :, None] + jnp.einsum(
            "gqk,kd->qgd",
            weights.astype(jnp.bfloat16),
            value_block,
            preferred_element_type=jnp.float32,
        )
        return ((new_top, total, summed), None)

    blocks = count // width
    pieces = (
        keys.reshape(blocks, width, -1),
        values.reshape(blocks, width, -1),
        key_pos.reshape(blocks, width),
        key_live.reshape(blocks, width),
    )
    carry, _ = lax.scan(step, carry, pieces)
    return carry


def project(inputs, positions, w_query, b_query, w_key, b_key, w_value, b_value):
    count = inputs.shape[0]
    query_part = jnp.dot(inputs, w_query, preferred_element_type=jnp.float32) + b_query
    query_part = rotate(query_part.reshape(count, -1, HD), positions).astype(jnp.bfloat16)
    key_part = jnp.dot(inputs, w_key, preferred_element_type=jnp.float32) + b_key
    key_part = (
        rotate(key_part.reshape(count, 1, HD), positions).reshape(count, HD).astype(jnp.bfloat16)
    )
    value_part = (jnp.dot(inputs, w_value, preferred_element_type=jnp.float32) + b_value).astype(
        jnp.bfloat16
    )
    return (query_part, key_part, value_part)


def pick_rows(table, valid, source):
    return jnp.where(valid[:, None], jnp.take(table, source, axis=0), jnp.zeros((), table.dtype))


def body(
    q2,
    k2,
    v2,
    hidden,
    w_query,
    b_query,
    w_key,
    b_key,
    w_value,
    b_value,
    kept_index,
    block_count,
    text_rows,
):
    rows = q2.shape[0]
    seq_count = lax.axis_size("seq")
    head_count = lax.axis_size("head")
    seq_rank = lax.axis_index("seq")
    first_row = seq_rank * rows
    query_pos = first_row + jnp.arange(rows, dtype=jnp.int32)
    queries = q2.reshape(rows, GROUP, HD)
    keys, values = side_by_side((k2, v2), "seq", 0, 1)
    key_pos = jnp.arange(keys.shape[0], dtype=jnp.int32)
    carry = attend(
        start_carry(rows),
        queries,
        keys,
        values,
        query_pos,
        key_pos,
        jnp.ones((keys.shape[0],), jnp.bool_),
    )
    top, total, _ = carry
    attn2 = finish(carry)
    selector = text_rows[:, None] == query_pos[None, :]
    picked = jnp.dot(selector.astype(jnp.bfloat16), q2, preferred_element_type=jnp.float32)
    picked_top = jnp.dot(selector.astype(jnp.float32), top.T)
    picked_total = jnp.dot(selector.astype(jnp.float32), total.T)
    text_queries, text_top, text_total = (
        lax.psum(picked.astype(jnp.bfloat16), "seq").astype(jnp.float32),
        lax.psum(picked_top.astype(jnp.bfloat16), "seq").astype(jnp.float32),
        lax.psum(picked_total.astype(jnp.bfloat16), "seq").astype(jnp.float32),
    )
    text_block = text_queries.astype(jnp.bfloat16).reshape(TEXT, GROUP, HD)
    scores = jnp.einsum("tgd,kd->gtk", text_block, k2, preferred_element_type=jnp.float32) * (
        1.0 / math.sqrt(HD)
    )
    allowed = (query_pos[None, :] <= text_rows[:, None])[None]
    probs = jnp.where(
        allowed, jnp.exp(scores - text_top.T[:, :, None]) / text_total.T[:, :, None], 0.0
    )
    partial_value = jnp.sum(probs, axis=(0, 1))
    head_total = over_copies(partial_value, "head")
    importance = head_total * (rows * seq_count / (GROUP * head_count * TEXT))
    blocks = rows // BLOCK
    kept_count = jnp.sum(block_count)
    ends = jnp.cumsum(block_count)
    begins = ends - block_count
    ranks = jnp.arange(rows, dtype=jnp.int32)
    owner = jnp.minimum(
        jnp.sum((ranks[:, None] >= ends[None, :]).astype(jnp.int32), axis=1), blocks - 1
    )
    within = jnp.clip(ranks - begins[owner], 0, BLOCK - 1)
    compact = owner * BLOCK + kept_index[owner * BLOCK + within]
    per_device = (rows * seq_count + TEXT) // (2 * seq_count)
    offset = prefix(kept_count, "seq", lambda earlier, later: earlier + later, jnp.int32(0))

    def window(delta):
        place = (seq_rank + delta) * per_device + jnp.arange(per_device, dtype=jnp.int32) - offset
        near_valid = (place >= 0) & (place < kept_count)
        return (near_valid, compact[jnp.clip(place, 0, rows - 1)])

    own_valid, own_source = window(0)
    gathered = pick_rows(hidden, own_valid, own_source).astype(jnp.float32)
    kept_pos = jnp.where(own_valid, first_row + own_source, 0)
    for delta in (1, -1):
        near_valid, near_source = window(delta)
        sent = pick_rows(hidden, near_valid, near_source)
        gathered = gathered + shifted(sent, "seq", delta).astype(jnp.float32)
        near_places = jnp.where(near_valid, first_row + near_source, 0)
        kept_pos = kept_pos + shifted(near_places, "seq", delta)
    kept_rows = gathered.astype(jnp.bfloat16)
    full_rows = collect(kept_rows, "head", 1)
    queries3, keys3, values3 = project(
        full_rows, kept_pos, w_query, b_query, w_key, b_key, w_value, b_value
    )
    order_pos = seq_rank * per_device + jnp.arange(per_device, dtype=jnp.int32)
    keys = collect(keys3, "seq", 0)
    values = collect(values3, "seq", 0)
    key_pos = jnp.arange(keys.shape[0], dtype=jnp.int32)
    state = attend(
        start_carry(per_device),
        queries3,
        keys,
        values,
        order_pos,
        key_pos,
        jnp.ones((keys.shape[0],), jnp.bool_),
    )
    attn3 = finish(state)
    return (attn2, importance, attn3)


def solution(mesh):
    placed = (
        P("seq", "head"),
        P("seq", "head"),
        P("seq", "head"),
        P("seq", "head"),
        P(None, "head"),
        P("head"),
        P(None, "head"),
        P("head"),
        P(None, "head"),
        P("head"),
        P("seq"),
        P("seq"),
        P(),
    )
    return jax.shard_map(
        body,
        mesh=mesh,
        in_specs=placed,
        out_specs=(P("seq", "head"), P("seq"), P("seq", "head")),
        check_vma=False,
    )
```

profile of v0, /device:TPU:1, one launch (start us, length us, event | category | flops | bytes accessed | tf_op | source)
XLA Modules:
  0.0 336.5 jit_solution(15182808153986926871)
XLA Ops:
  7.2 1.7 pad_maximum_fusion
  12.3 8.6 %all-to-all-start.1 = ((s32[32,1,1]{2,1,0:T(1,128)}), s32[32,1,1]{2,1,0:T(1,128)S(1)}, u32[]{:S(2)}, u32[]{:S(2)}) async-start(s32[32,1,1]{2,1,0:T(1,128)} %broadcast_in_dim.195), calls=%async_computation.1 | async-start | bytes 32768 | tf_op jit(solution)/shard_map/all_to_all | solution.py:25
  25.3 1.9 gather_fusion
  37.5 3.1 collective-permute-start.2
  40.6 1.9 collective-permute-start.3
  42.5 1.8 gather_fusion.6
  44.3 1.8 gather_fusion.5
  46.0 2.0 select_select_fusion.1
  48.1 3.6 %collective-permute-start = (bf16[132,2048]{1,0:T(8,128)(2,1)}, bf16[132,2048]{1,0:T(8,128)(2,1)}, u32[]{:S(2)}, u32[]{:S(2)}) collective-permute-start(bf16[132,2048]{1,0:T(8,128)(2,1)} %select_select_fusion.1), channel_id=1, source_target_pairs={{0,4},{4,8},{8,12},{12,16},{16,20},{20,24},{24,28},{28,32},{32,36}... | collective-permute-start | bytes 1622024 | tf_op jit(solution)/shard_map/ppermute | solution.py:56
  51.7 2.0 select_select_fusion
  53.8 1.9 collective-permute-start.1
  56.4 1.8 gather_fusion.4
  58.1 2.7 collective-permute-done
  60.9 4.0 %collective-permute-done.1 = bf16[132,2048]{1,0:T(8,128)(2,1)} collective-permute-done((bf16[132,2048]{1,0:T(8,128)(2,1)}, bf16[132,2048]{1,0:T(8,128)(2,1)}, u32[]{:S(2)}, u32[]{:S(2)}) %collective-permute-start.1) | collective-permute-done | bytes 540704 | tf_op jit(solution)/shard_map/ppermute | solution.py:56
  64.9 1.8 add_convert_fusion
  68.4 5.1 %all-to-all-start.2 = ((bf16[4,132,2048]{2,1,0:T(8,128)(2,1)}), bf16[4,132,2048]{2,1,0:T(8,128)(2,1)}, u32[]{:S(2)}, u32[]{:S(2)}) async-start(bf16[4,132,2048]{2,1,0:T(8,128)(2,1)} %broadcast_in_dim.201), calls=%async_computation.2 | async-start | bytes 4456448 | tf_op jit(solution)/shard_map/all_to_all | solution.py:25
  74.6 2.1 copy.62
  79.5 16.1 %all-to-all-done.2 = bf16[4,132,2048]{2,1,0:T(8,128)(2,1)} async-done(((bf16[4,132,2048]{2,1,0:T(8,128)(2,1)}), bf16[4,132,2048]{2,1,0:T(8,128)(2,1)}, u32[]{:S(2)}, u32[]{:S(2)}) %all-to-all-start.2) | async-done | bytes 2162720 | tf_op jit(solution)/shard_map/all_to_all | solution.py:25
  95.7 3.3 copy.67
  104.3 12.7 %all-to-all-start.3 = ((bf16[32,132,128]{2,1,0:T(8,128)(2,1)}), bf16[32,132,128]{2,1,0:T(8,128)(2,1)S(1)}, u32[]{:S(2)}, u32[]{:S(2)}) async-start(bf16[32,132,128]{2,1,0:T(8,128)(2,1)} %broadcast_in_dim.202), calls=%async_computation.3 | async-start | bytes 2228224 | tf_op jit(solution)/shard_map/all_to_all | solution.py:25
  117.0 9.0 %convolution_add_fusion = f32[132,1024]{1,0:T(8,128)S(1)} fusion(bf16[132,8192]{1,0:T(8,128)(2,1)} %bitcast.156, bf16[8192,1024]{1,0:T(8,128)(2,1)} %param.21, f32[1024]{0:T(1024)S(1)} %copy-done.13), kind=kOutput, calls=%fused_computation.56 | convolution fusion | flops 2214727680 | bytes 19484672 | tf_op jit(solution)/shard_map/dot_general | solution.py:134
  129.0 5.7 %all-to-all-done.3 = bf16[32,132,128]{2,1,0:T(8,128)(2,1)S(1)} async-done(((bf16[32,132,128]{2,1,0:T(8,128)(2,1)}), bf16[32,132,128]{2,1,0:T(8,128)(2,1)S(1)}, u32[]{:S(2)}, u32[]{:S(2)}) %all-to-all-start.3) | async-done | bytes 1081376 | tf_op jit(solution)/shard_map/all_to_all | solution.py:25
  135.9 4.8 %all-to-all-start.4 = ((bf16[32,132,128]{2,1,0:T(8,128)(2,1)}), bf16[32,132,128]{2,1,0:T(8,128)(2,1)}, u32[]{:S(2)}, u32[]{:S(2)}) async-start(bf16[32,132,128]{2,1,0:T(8,128)(2,1)} %broadcast_in_dim.204), calls=%async_computation.4 | async-start | bytes 2228224 | tf_op jit(solution)/shard_map/all_to_all | solution.py:25
  141.9 9.5 %fusion.27 = (f32[8,132]{1,0:T(8,128)S(1)}, f32[4224,132,8]{0,1,2:T(8,128)}) fusion(pred[132,4224]{1,0:T(8,128)(4,1)S(1)} %copy-done.7, bf16[4224,128,1]{1,0,2:T(8,128)(2,1)} %reshape.515, bf16[132,8,64]{2,0,1:T(8,128)(2,1)S(1)} %get-tuple-element.194, bf16[132,8,64]{2,0,1:T(8,128)(2,1)S(1)} %get-tuple-element.193), kind=kOutput, calls=%fused_computation.39 | convolution fusion | flops 1155820544 | bytes 19755648 | tf_op jit(solution)/shard_map/while/body/eval_jaxpr/qgd,kd->gqk/dot_general | solution.py:105
  151.5 10.7 %fusion.30 = f32[8,132]{1,0:T(8,128)S(1)} fusion(f32[4224,132,8]{0,1,2:T(8,128)} %get-tuple-element.213, f32[8,132]{1,0:T(8,128)S(1)} %get-tuple-element.200, pred[132,4224]{1,0:T(8,128)(4,1)S(1)} %copy-done.7), kind=kLoop, calls=%fused_computation.42 | loop fusion | flops 17841120 | bytes 18408192 | tf_op jit(solution)/shard_map/while/body/eval_jaxpr/reduce_sum | solution.py:112
  163.6 8.2 %fusion.53 = bf16[132,8,128]{2,0,1:T(8,128)(2,1)S(1)} fusion(bf16[4224,128,1]{1,0,2:T(8,128)(2,1)S(1)} %reshape.516, f32[4224,132,8]{0,1,2:T(8,128)} %get-tuple-element.213, f32[8,132]{1,0:T(8,128)S(1)} %get-tuple-element.200, pred[132,4224]{1,0:T(8,128)(4,1)S(1)} %copy-done.7, f32[132,8]{0,1:T(8,128)S(1)} %bitcast_add_fusion, ...), kind=kOutput, calls=%fused_computation.68 | convolution fusion | flops 1160146944 | bytes 19764096 | tf_op jit(solution)/shard_map/while/body/eval_jaxpr/gqk,kd->qgd/dot_general | solution.py:113
  172.6 4.5 %fusion.83 = (bf16[8192,128]{1,0:T(8,128)(2,1)}, bf16[8192,128]{1,0:T(8,128)(2,1)}) fusion(bf16[8192,256]{1,0:T(8,128)(2,1)} %all-gather.2.cloned.1.call-done), kind=kLoop, calls=%fused_computation.146 | loop fusion | bytes 8388608 | tf_op jit(solution)/shard_map/split | solution.py:20
  177.1 78.1 %while.3 = (s32[]{:T(128)}, f32[8,256]{1,0:T(8,128)S(1)}, f32[8,256]{1,0:T(8,128)S(1)}, f32[256,8,128]{0,2,1:T(8,128)S(1)}, s32[16,512]{1,0:T(8,128)S(1)}, /*ind...) while((s32[]{:T(128)}, f32[8,256]{1,0:T(8,128)S(1)}, ...), condition=%wide.region_3.4_spmd.clone, body=%wide.region_0.3_spmd.clone.sunk | while | flops 549335296 | bytes 16130193 | solution.py:128
  177.5 1.7 fusion.112
  180.1 2.1 fusion.116
  182.4 1.7 fusion.112
  185.0 2.1 fusion.116
  187.3 1.7 fusion.112
  189.8 2.1 fusion.116
  192.1 1.7 fusion.112
  194.7 2.1 fusion.116
  197.0 1.7 fusion.112
  199.6 2.1 fusion.116
  201.9 1.7 fusion.112
  204.4 2.1 fusion.116
  206.7 1.7 fusion.112
  209.3 2.1 fusion.116
  211.6 1.7 fusion.112
  214.2 2.1 fusion.116
  216.5 1.7 fusion.112
  219.0 2.1 fusion.116
  221.3 1.7 fusion.112
  223.9 2.1 fusion.116
  226.2 1.7 fusion.112
  228.8 2.1 fusion.116
  231.1 1.7 fusion.112
  233.7 2.1 fusion.116
  235.9 1.7 fusion.112
  238.5 2.1 fusion.116
  240.8 1.7 fusion.112
  243.4 2.1 fusion.116
  245.7 1.7 fusion.112
  248.3 2.1 fusion.116
  250.5 1.7 fusion.112
  253.1 2.1 fusion.116
  255.7 63.4 %all-reduce = (bf16[8,256]{1,0:T(8,128)(2,1)S(1)}, bf16[8,256]{1,0:T(8,128)(2,1)S(1)}) all-reduce(bf16[8,256]{1,0:T(8,128)(2,1)S(1)} %fusion.49, bf16[8,256]{1,0:T(8,128)(2,1)S(1)} %fusion.48), channel_id=1, replica_groups=mesh['seq'=32,'head'=4] {'seq'}, use_global_device_ids=true, to_apply=%region_6.7 | all-reduce | flops 4096 | bytes 16384 | tf_op jit(solution)/shard_map/psum | solution.py:192
  319.2 2.0 fusion.38
  321.8 3.2 all-to-all-start
  325.9 2.0 copy.72
  (238 shorter events, 56.2 us)
Async XLA Ops:
  7.2 94.5 %copy-start = (bf16[8192,128]{1,0:T(8,128)(2,1)S(1)}, bf16[8192,128]{1,0:T(8,128)(2,1)}, u32[]{:S(2)}) copy-start(bf16[8192,128]{1,0:T(8,128)(2,1)} %param.23) | copy-start | bytes 6291460
  7.2 18.1 %copy-start.2 = (s32[256]{0:T(256)S(1)}, s32[256]{0:T(256)}, u32[]{:S(2)}) copy-start(s32[256]{0:T(256)} %param.27) | copy-start | bytes 3076
  7.2 165.4 %all-gather.2.cloned.1.call-start = ((), (), s32[]{:S(2)}) async-start(), calls=%async_computation.5 | async-start | bytes 4325376 | tf_op jit(solution)/shard_map/all_gather | solution.py:20
  12.3 15.5 %all-to-all-start.1 = ((s32[32,1,1]{2,1,0:T(1,128)}), s32[32,1,1]{2,1,0:T(1,128)S(1)}, u32[]{:S(2)}, u32[]{:S(2)}) async-start(s32[32,1,1]{2,1,0:T(1,128)} %broadcast_in_dim.195), calls=%async_computation.1 | async-start | bytes 32768 | tf_op jit(solution)/shard_map/all_to_all | solution.py:25
  20.9 298.2 %all-reduce.3.cloned.1.call-start = ((), (), s32[]{:S(2)}) async-start(), calls=%async_computation.6 | async-start | bytes 1048576 | tf_op jit(solution)/shard_map/psum | solution.py:190
  23.3 19.2 %copy-start.3 = (bf16[256,2048]{1,0:T(8,128)(2,1)S(1)}, bf16[256,2048]{1,0:T(8,128)(2,1)}, u32[]{:S(2)}) copy-start(bf16[256,2048]{1,0:T(8,128)(2,1)} %param.20) | copy-start | bytes 3145732
  37.5 18.2 %collective-permute-start.2 = (s32[132]{0:T(256)S(1)}, s32[132]{0:T(256)S(1)}, u32[]{:S(2)}, u32[]{:S(2)}) collective-permute-start(s32[132]{0:T(256)S(1)} %get-tuple-element.185), channel_id=1, source_target_pairs={{0,4},{4,8},{8,12},{12,16},{16,20},{20,24},{24,28},{28,32},{32,36}... | collective-permute-start | bytes 1592 | tf_op jit(solution)/shard_map/ppermute | solution.py:56
  40.6 15.1 %collective-permute-start.3 = (s32[132]{0:T(256)S(1)}, s32[132]{0:T(256)S(1)}, u32[]{:S(2)}, u32[]{:S(2)}) collective-permute-start(s32[132]{0:T(256)S(1)} %get-tuple-element.187), channel_id=1, source_target_pairs={{4,0},{8,4},{12,8},{16,12},{20,16},{24,20},{28,24},{32,28},{36,32}... | collective-permute-start | bytes 1592 | tf_op jit(solution)/shard_map/ppermute | solution.py:56
  48.1 12.8 %collective-permute-start = (bf16[132,2048]{1,0:T(8,128)(2,1)}, bf16[132,2048]{1,0:T(8,128)(2,1)}, u32[]{:S(2)}, u32[]{:S(2)}) collective-permute-start(bf16[132,2048]{1,0:T(8,128)(2,1)} %select_select_fusion.1), channel_id=1, source_target_pairs={{0,4},{4,8},{8,12},{12,16},{16,20},{20,24},{24,28},{28,32},{32,36}... | collective-permute-start | bytes 1622024 | tf_op jit(solution)/shard_map/ppermute | solution.py:56
  53.8 11.2 %collective-permute-start.1 = (bf16[132,2048]{1,0:T(8,128)(2,1)}, bf16[132,2048]{1,0:T(8,128)(2,1)}, u32[]{:S(2)}, u32[]{:S(2)}) collective-permute-start(bf16[132,2048]{1,0:T(8,128)(2,1)} %select_select_fusion), channel_id=1, source_target_pairs={{4,0},{8,4},{12,8},{16,12},{20,16},{24,20},{28,24},{32,28},{36,32}... | collective-permute-start | bytes 1622024 | tf_op jit(solution)/shard_map/ppermute | solution.py:56
  68.4 5.2 %copy-start.9 = (bf16[256,1024]{1,0:T(8,128)(2,1)S(1)}, bf16[256,1024]{1,0:T(8,128)(2,1)}, u32[]{:S(2)}) copy-start(bf16[256,1024]{1,0:T(8,128)(2,1)} %param.17) | copy-start | bytes 1572868
  68.4 8.3 %copy-start.14 = (s32[256]{0:T(256)S(1)}, s32[256]{0:T(256)}, u32[]{:S(2)}) copy-start(s32[256]{0:T(256)} %param.29) | copy-start | bytes 3076
  68.4 27.3 %all-to-all-start.2 = ((bf16[4,132,2048]{2,1,0:T(8,128)(2,1)}), bf16[4,132,2048]{2,1,0:T(8,128)(2,1)}, u32[]{:S(2)}, u32[]{:S(2)}) async-start(bf16[4,132,2048]{2,1,0:T(8,128)(2,1)} %broadcast_in_dim.201), calls=%async_computation.2 | async-start | bytes 4456448 | tf_op jit(solution)/shard_map/all_to_all | solution.py:25
  100.1 1.6 copy-start.16
  101.7 1.4 copy-start.4
  102.5 14.4 %copy-start.13 = (f32[1024]{0:T(1024)S(1)}, f32[1024]{0:T(1024)}, u32[]{:S(2)}) copy-start(f32[1024]{0:T(1024)} %param.22) | copy-start | bytes 12292
  104.3 30.5 %all-to-all-start.3 = ((bf16[32,132,128]{2,1,0:T(8,128)(2,1)}), bf16[32,132,128]{2,1,0:T(8,128)(2,1)S(1)}, u32[]{:S(2)}, u32[]{:S(2)}) async-start(bf16[32,132,128]{2,1,0:T(8,128)(2,1)} %broadcast_in_dim.202), calls=%async_computation.3 | async-start | bytes 2228224 | tf_op jit(solution)/shard_map/all_to_all | solution.py:25
  126.0 0.9 copy-start.10
  126.0 1.7 copy-start.5
  126.0 2.3 copy-start.8
  126.0 2.3 copy-start.15
  135.9 6.0 %copy-start.7 = (pred[132,4224]{1,0:T(8,128)(4,1)S(1)}, pred[132,4224]{1,0:T(8,128)(4,1)}, u32[]{:S(2)}) copy-start(pred[132,4224]{1,0:T(8,128)(4,1)} %iota_compare_fusion) | copy-start | bytes 1672708
  135.9 26.3 %all-to-all-start.4 = ((bf16[32,132,128]{2,1,0:T(8,128)(2,1)}), bf16[32,132,128]{2,1,0:T(8,128)(2,1)}, u32[]{:S(2)}, u32[]{:S(2)}) async-start(bf16[32,132,128]{2,1,0:T(8,128)(2,1)} %broadcast_in_dim.204), calls=%async_computation.4 | async-start | bytes 2228224 | tf_op jit(solution)/shard_map/all_to_all | solution.py:25
  172.6 4.5 %copy-start.6 = (bf16[256,8,128]{2,0,1:T(8,128)(2,1)S(1)}, bf16[256,8,128]{2,0,1:T(8,128)(2,1)}, u32[]{:S(2)}) copy-start(bf16[256,8,128]{2,0,1:T(8,128)(2,1)} %copy.62) | copy-start | bytes 1572868
  177.1 142.1 %copy-start.11 = (pred[256,256]{1,0:T(8,128)(4,1)S(1)}, pred[256,256]{1,0:T(8,128)(4,1)}, u32[]{:S(2)}) copy-start(pred[256,256]{1,0:T(8,128)(4,1)} %broadcast_compare_fusion.1) | copy-start | bytes 196612
  177.1 142.1 %copy-start.12 = (bf16[256,128]{1,0:T(8,128)(2,1)S(1)}, bf16[256,128]{1,0:T(8,128)(2,1)}, u32[]{:S(2)}) copy-start(bf16[256,128]{1,0:T(8,128)(2,1)} %param.18) | copy-start | bytes 196612
  319.2 10.5 %copy-start.1 = (bf16[8192,128]{1,0:T(8,128)(2,1)S(1)}, bf16[8192,128]{1,0:T(8,128)(2,1)}, u32[]{:S(2)}) copy-start(bf16[8192,128]{1,0:T(8,128)(2,1)} %param.23) | copy-start | bytes 6291460
  321.8 7.3 %all-to-all-start = ((f32[4,1,256]{2,1,0:T(1,128)}), f32[4,1,256]{2,1,0:T(1,128)S(1)}, u32[]{:S(2)}, u32[]{:S(2)}) async-start(f32[4,1,256]{2,1,0:T(1,128)} %broadcast_in_dim.191), calls=%async_computation | async-start | bytes 8192 | tf_op jit(solution)/shard_map/all_to_all | solution.py:25
Sparse Core Ops, SparseCore 0:
  10.3 49.5 all-gather.1
  63.1 106.4 all-reduce.2
where the time goes:
time: 343 us; the launch traced here: 337 us
  matrix products  91.9 us (27%)
  blocking collectives  63.4 us (18%)
  other arithmetic  46.2 us (13%)
  starting transfers between devices  45.1 us (13%)
  local copies, waits for them, and re-layouts  42.2 us (12%)
  waiting for transfers between devices  30.3 us (9%)
  between operations  16 us (5%)
    psum x1, blocking collectives, body(): lax.psum(picked_total.astype(jnp.bfloat16), 'seq').astype(jnp.float32)  63.4 us
    dot_general x17, matrix products, step(): jnp.einsum('gqk,kd->qgd', weights.astype(jnp.bfloat16), value_block, pref...  41 us
    dot_general x17, matrix products, step(): jnp.einsum('qgd,kd->gqk', queries, key_block, preferred_element_type=jnp....  36.5 us
    all_to_all x5, starting transfers between devices, copy_for_each(): lax.all_to_all(jnp.broadcast_to(x[None], (count, *x.shape)), axis, 0, 0,...  34.5 us
    reduce_sum x17, other arithmetic, step(): total = total * rescale + jnp.sum(weights, axis=-1)  24.6 us
    all_to_all x5, waiting for transfers between devices, copy_for_each(): lax.all_to_all(jnp.broadcast_to(x[None], (count, *x.shape)), axis, 0, 0,...  23.5 us
    ppermute x4, starting transfers between devices, shifted(): return lax.ppermute(block, axis, route)  10.5 us
    dot_general x1, matrix products, project(): jnp.dot(inputs, w_query, preferred_element_type=jnp.float32) + b_query  8.98 us
  transfers between devices with their start and end apart: 11, of which 6 were waited for; matrix products, arithmetic and copies ran while one was open for 52% of the time, Pallas kernels for 0%

commit v1 on v0

v1 whole, which is shorter than its diff:
```python
import math

import jax
import jax.numpy as jnp
from jax import lax
from jax.experimental import pallas as pl
from jax.experimental.pallas import tpu as pltpu
from jax.sharding import PartitionSpec as P

HD = 128
GROUP = 8
BLOCK = 128
ROWS = 256
SHARE = 132
PAD = 136
WIDE = 1024
FACTOR = math.log2(math.e) / math.sqrt(HD)
LOW = -1e30
BF = jnp.bfloat16
F32 = jnp.float32


def dot(a, b):
    return jnp.dot(a, b, preferred_element_type=F32)


def dot_t(a, b):
    return lax.dot_general(a, b, (((1,), (1,)), ((), ())), preferred_element_type=F32)


def whole(shape):
    return pl.BlockSpec(shape, lambda *_: (0,) * len(shape))


def smem():
    return pl.BlockSpec(memory_space=pltpu.SMEM)


def pick_kernel(info, index_ref, hidden_ref, own_ref, send_ref):
    core, first, before, live0, live1 = (info[i] for i in range(5))
    count = live0 + live1
    start = jnp.where(core == 0, 0, 2 * SHARE - count)
    lane = lax.broadcasted_iota(jnp.int32, (PAD, ROWS), 1)
    place = lax.broadcasted_iota(jnp.int32, (PAD, ROWS), 0)
    second = lane >= BLOCK
    within = jnp.where(second, lane - BLOCK, lane)
    rank = jnp.where(second, within + live0, within)
    live = within < jnp.where(second, live1, live0)
    row = index_ref[...] + jnp.where(second, BLOCK, 0)
    column = lax.broadcasted_iota(jnp.int32, (PAD, BLOCK), 1)
    for out_ref, base in ((own_ref, SHARE * core), (send_ref, SHARE * (1 - core))):
        wanted = place + (base - start)
        match = (rank == wanted) & live & (place < SHARE)
        source = jnp.sum(jnp.where(match, (row + 1).astype(F32), 0.0), axis=1, keepdims=True)
        source = source.astype(jnp.int32) - 1
        select = jnp.where(lane == source, 1.0, 0.0).astype(BF)
        out_ref[:, : hidden_ref.shape[1]] = dot(select, hidden_ref[...]).astype(BF)
        position = jnp.where(source >= 0, source + first, 0)
        high = jnp.where(column == 0, position >> 7, 0)
        marks = jnp.where(column == 1, position & 127, high)
        out_ref[:, hidden_ref.shape[1] :] = marks.astype(F32).astype(BF)


def pick_rows(info, kept_index, hidden):
    width = hidden.shape[1] + BLOCK
    shape = jax.ShapeDtypeStruct((PAD, width), BF)
    return pl.pallas_call(
        pick_kernel,
        out_shape=(shape, shape),
        in_specs=[smem(), pl.BlockSpec(memory_space=pltpu.VMEM), pl.BlockSpec(memory_space=pltpu.VMEM)],
        out_specs=(pl.BlockSpec(memory_space=pltpu.VMEM),) * 2,
        compiler_params=pltpu.CompilerParams(vmem_limit_bytes=24 << 20),
        cost_estimate=pl.CostEstimate(
            flops=4 * PAD * ROWS * width, transcendentals=0, bytes_accessed=4 * ROWS * width
        ),
        name="pick_rows",
    )(info, kept_index.reshape(1, ROWS), hidden)


def rotated(u, cosine, sine):
    return u * cosine + pltpu.roll(u, HD // 2, 1) * sine


def project_kernel(pieces, last, blocks, *refs):
    x_refs = refs[:pieces]
    wq, wk, wv = refs[pieces : pieces + 3]
    rest = refs[pieces + 3 :]
    if last:
        q_in, kv_in, bq, bk, bv, cosine, sine, q_out, kv_out, q_acc, kv_acc = rest
    else:
        q_out, kv_out, q_acc, kv_acc = rest
    piece, tile = pl.program_id(0), pl.program_id(1)
    tiles = pl.num_programs(1)
    at = pl.ds(pl.multiple_of(tile * 256, 256), 256)
    for p in range(pieces):

        @pl.when(piece == p)
        def _(p=p):
            x = x_refs[p][...]
            got = dot(x, wq[...])
            if p > 0:
                got = got + q_acc[:, at]
            elif last:
                got = got + q_in[:, at]
            q_acc[:, at] = got

            @pl.when(tile == 0)
            def _():
                k, v = (dot(x, wk[...]), dot(x, wv[...]))
                if p > 0:
                    k, v = (k + kv_acc[:, :HD], v + kv_acc[:, HD:])
                elif last:
                    k, v = (k + kv_in[:, :HD], v + kv_in[:, HD:])
                kv_acc[:, :HD] = k
                kv_acc[:, HD:] = v

    @pl.when((piece == pieces - 1) & (tile == tiles - 1))
    def _():
        if last:
            c, s = (cosine[...], sine[...])
            for h in range(GROUP):
                part = slice(h * HD, (h + 1) * HD)
                q_out[:, part] = rotated(q_acc[:, part] + bq[:, part], c, s).astype(BF)
            kv_out[:, :HD] = rotated(kv_acc[:, :HD] + bk[...], c, s).astype(BF)
            kv_out[:, HD:] = (kv_acc[:, HD:] + bv[...]).astype(BF)
        else:
            q_out[...] = q_acc[...]
            kv_out[...] = kv_acc[...]


def project(blocks, xs, weights, extra):
    pieces = len(xs)
    last = bool(extra)
    depth = xs[0].shape[1]
    wq, wk, wv = weights
    columns = wq.shape[1]
    kind = BF if last else F32
    spec = pltpu.PrefetchScalarGridSpec(
        num_scalar_prefetch=1,
        grid=(pieces, columns // 256),
        in_specs=[whole(x.shape) for x in xs]
        + [
            pl.BlockSpec((depth, 256), lambda p, n, b: (b[p], n)),
            pl.BlockSpec((depth, HD), lambda p, n, b: (b[p], 0)),
            pl.BlockSpec((depth, HD), lambda p, n, b: (b[p], 0)),
        ]
        + [whole(e.shape) for e in extra],
        out_specs=(whole((PAD, columns)), whole((PAD, 2 * HD))),
        scratch_shapes=[pltpu.VMEM((PAD, columns), F32), pltpu.VMEM((PAD, 2 * HD), F32)],
    )

    def kernel(*refs):
        project_kernel(pieces, last, *refs)

    return pl.pallas_call(
        kernel,
        out_shape=(
            jax.ShapeDtypeStruct((PAD, columns), kind),
            jax.ShapeDtypeStruct((PAD, 2 * HD), kind),
        ),
        grid_spec=spec,
        compiler_params=pltpu.CompilerParams(vmem_limit_bytes=32 << 20),
        cost_estimate=pl.CostEstimate(
            flops=2 * pieces * PAD * depth * (columns + 2 * HD),
            transcendentals=0,
            bytes_accessed=2 * pieces * depth * (columns + 2 * HD),
        ),
        name="project_rest" if last else "project_own",
    )(blocks, *xs, wq, wk, wv, *extra)


def attend_kernel(info, q_ref, kv_ref, out_ref, q_s, top_s, sum_s, v_s, bias_s):
    step = pl.program_id(0)
    rank = info[0]
    last = (rank * ROWS) // WIDE

    @pl.when(step == 0)
    def _():
        for h in range(GROUP):
            q_s[h] = q_ref[:, h * HD : (h + 1) * HD]
        top_s[...] = jnp.full_like(top_s, LOW)
        sum_s[...] = jnp.zeros_like(sum_s)
        v_s[:, HD:] = jnp.ones((WIDE, HD), BF)

    def run(masked):
        keys = kv_ref[:, :HD]
        v_s[:, :HD] = kv_ref[:, HD:]
        if masked:
            key = lax.broadcasted_iota(jnp.int32, (ROWS, WIDE), 1)
            query = lax.broadcasted_iota(jnp.int32, (ROWS, WIDE), 0)
            shift = rank * ROWS - last * WIDE
            bias_s[...] = jnp.where(key <= query + shift, 0.0, LOW)

        def heads(i, carry):
            for h in (2 * i, 2 * i + 1):
                scores = dot_t(q_s[h], keys)
                if masked:
                    scores = scores + bias_s[...]
                before = top_s[h]
                top = jnp.maximum(before, jnp.max(scores, axis=1, keepdims=True))
                top_s[h] = top
                weights = jnp.exp2((scores - top[:, :1]) * FACTOR).astype(BF)
                fade = jnp.exp2((before - top) * FACTOR)
                fade = jnp.concatenate([fade, fade], axis=1)
                sum_s[h] = sum_s[h] * fade + dot(weights, v_s[...])
            return carry

        lax.fori_loop(0, GROUP // 2, heads, 0)

    @pl.when(step < last)
    def _():
        run(False)

    @pl.when(step == last)
    def _():
        run(True)
        for h in range(GROUP):
            total = sum_s[h]
            out_ref[:, h * HD : (h + 1) * HD] = (total[:, :HD] / total[:, HD:]).astype(BF)


def attend(info, q2, kv2):
    tokens = kv2.shape[0]
    spec = pltpu.PrefetchScalarGridSpec(
        num_scalar_prefetch=1,
        grid=(tokens // WIDE,),
        in_specs=[
            whole(q2.shape),
            pl.BlockSpec((WIDE, 2 * HD), lambda i, info: (jnp.minimum(i, info[0] * ROWS // WIDE), 0)),
        ],
        out_specs=whole(q2.shape),
        scratch_shapes=[
            pltpu.VMEM((GROUP, ROWS, HD), BF),
            pltpu.VMEM((GROUP, ROWS, HD), F32),
            pltpu.VMEM((GROUP, ROWS, 2 * HD), F32),
            pltpu.VMEM((WIDE, 2 * HD), BF),
            pltpu.VMEM((ROWS, WIDE), F32),
        ],
    )
    return pl.pallas_call(
        attend_kernel,
        out_shape=jax.ShapeDtypeStruct(q2.shape, BF),
        grid_spec=spec,
        compiler_params=pltpu.CompilerParams(vmem_limit_bytes=40 << 20),
        cost_estimate=pl.CostEstimate(
            flops=6 * GROUP * ROWS * tokens * HD,
            transcendentals=GROUP * ROWS * tokens,
            bytes_accessed=4 * tokens * HD,
        ),
        name="attend2",
    )(info, q2, kv2)


CHUNK = 8


def text_kernel(info, text, q_ref, kv_ref, out_ref, score_s):
    rank, low, count = (info[i] for i in range(3))
    first = rank * ROWS
    blocks = (first // WIDE) + 1
    out_ref[...] = jnp.zeros_like(out_ref)
    rows = GROUP * CHUNK

    def chunk(c, carry):
        place = jnp.zeros((CHUNK, ROWS), jnp.int32)
        sub = lax.broadcasted_iota(jnp.int32, (CHUNK, ROWS), 0)
        for i in range(CHUNK):
            n = c * CHUNK + i
            at = text[jnp.minimum(low + n, text.shape[0] - 1)] - first
            place = jnp.where(sub == i, jnp.where(n < count, at, -1), place)
        lane = lax.broadcasted_iota(jnp.int32, (CHUNK, ROWS), 1)
        select = jnp.where(lane == place, 1.0, 0.0).astype(BF)
        picked = dot(select, q_ref[...]).astype(BF)
        queries = jnp.concatenate(
            [picked[:, h * HD : (h + 1) * HD] for h in range(GROUP)], axis=0
        )
        place = jnp.concatenate([place[:, :HD]] * GROUP, axis=0)[:, :1]
        limit = first + jnp.maximum(place, 0)
        key = lax.broadcasted_iota(jnp.int32, (rows, WIDE), 1)

        def scored(b, top):
            at = pl.ds(pl.multiple_of(b * WIDE, WIDE), WIDE)
            scores = dot_t(queries, kv_ref[at, :HD])
            scores = jnp.where(key + b * WIDE <= limit, scores, LOW)
            score_s[:, at] = scores
            return jnp.maximum(top, jnp.max(scores, axis=1, keepdims=True))

        top = lax.fori_loop(0, blocks, scored, jnp.full((rows, 1), LOW, F32))

        def weighed(b, total):
            at = pl.ds(pl.multiple_of(b * WIDE, WIDE), WIDE)
            weights = jnp.exp2((score_s[:, at] - top) * FACTOR)
            score_s[:, at] = weights
            return total + jnp.sum(weights, axis=1, keepdims=True)

        total = lax.fori_loop(0, blocks, weighed, jnp.zeros((rows, 1), F32))
        share = jnp.where(place >= 0, 1.0 / total, 0.0)

        def summed(b, carry):
            at = pl.ds(pl.multiple_of(b * WIDE, WIDE), WIDE)
            out_ref[pl.ds(b, 1), :] += jnp.sum(score_s[:, at] * share, axis=0, keepdims=True)
            return carry

        lax.fori_loop(0, blocks, summed, 0)
        return carry

    lax.fori_loop(0, (count + CHUNK - 1) // CHUNK, chunk, 0)


def text_sums(info, text_rows, q2, kv2):
    tokens = kv2.shape[0]
    vmem = pl.BlockSpec(memory_space=pltpu.VMEM)
    return pl.pallas_call(
        text_kernel,
        out_shape=jax.ShapeDtypeStruct((tokens // WIDE, WIDE), F32),
        in_specs=[smem(), smem(), vmem, vmem],
        out_specs=vmem,
        scratch_shapes=[pltpu.VMEM((GROUP * CHUNK, tokens), F32)],
        compiler_params=pltpu.CompilerParams(vmem_limit_bytes=24 << 20),
        cost_estimate=pl.CostEstimate(
            flops=2 * GROUP * CHUNK * tokens * HD,
            transcendentals=GROUP * CHUNK * tokens,
            bytes_accessed=4 * tokens * HD,
        ),
        name="text_sums",
    )(info, text_rows, q2, kv2)


def attend3_kernel(info, q_ref, mine_ref, other_ref, out_ref, q_s, out_s, v_s, bias_s):
    chip, core = info[0], info[1]
    half = mine_ref.shape[0]
    for h in range(GROUP):
        q_s[h] = q_ref[:, h * HD : (h + 1) * HD]
    v_s[:half, :HD] = mine_ref[:, HD:]
    v_s[half:, :HD] = other_ref[:, HD:]
    v_s[:, HD:] = jnp.ones((2 * half, HD), BF)
    row = lax.broadcasted_iota(jnp.int32, (1, half), 1)
    rest = row % PAD
    live = rest < SHARE
    query = lax.broadcasted_iota(jnp.int32, (PAD, half), 0)
    start = chip * PAD
    own = (row - start <= query) & live
    bias_s[:, :half] = jnp.where(own, 0.0, LOW)
    earlier = (row < start + core * PAD) & live
    bias_s[:, half:] = jnp.where(earlier & (query >= 0), 0.0, LOW)

    def heads(h, carry):
        q = q_s[h]
        left = dot_t(q, mine_ref[:, :HD]) + bias_s[:, :half]
        right = dot_t(q, other_ref[:, :HD]) + bias_s[:, half:]
        top = jnp.maximum(
            jnp.max(left, axis=1, keepdims=True), jnp.max(right, axis=1, keepdims=True)
        )
        left = jnp.exp2((left - top) * FACTOR).astype(BF)
        right = jnp.exp2((right - top) * FACTOR).astype(BF)
        total = dot(left, v_s[:half]) + dot(right, v_s[half:])
        out_s[h] = total[:, :HD] / total[:, HD:]
        return carry

    lax.fori_loop(0, GROUP, heads, 0)
    for h in range(GROUP):
        out_ref[:, h * HD : (h + 1) * HD] = out_s[h][:SHARE].astype(BF)


def attend3(info, q3, mine, other):
    vmem = pl.BlockSpec(memory_space=pltpu.VMEM)
    keys = 2 * mine.shape[0]
    return pl.pallas_call(
        attend3_kernel,
        out_shape=jax.ShapeDtypeStruct((SHARE, q3.shape[1]), BF),
        in_specs=[smem(), vmem, vmem, vmem],
        out_specs=vmem,
        scratch_shapes=[
            pltpu.VMEM((GROUP, PAD, HD), BF),
            pltpu.VMEM((GROUP, PAD, HD), F32),
            pltpu.VMEM((keys, 2 * HD), BF),
            pltpu.VMEM((PAD, keys), F32),
        ],
        compiler_params=pltpu.CompilerParams(vmem_limit_bytes=40 << 20),
        cost_estimate=pl.CostEstimate(
            flops=6 * GROUP * PAD * keys * HD,
            transcendentals=GROUP * PAD * keys,
            bytes_accessed=4 * keys * HD,
        ),
        name="attend3",
    )(info, q3, mine, other)


def from_core(x):
    count = lax.axis_size("seq")
    return lax.ppermute(x, "seq", [(i ^ 1, i) for i in range(count)])


def from_head(x, distance):
    count = lax.axis_size("head")
    return lax.ppermute(x, "head", [((i + distance) % count, i) for i in range(count)])


def over_chips(x):
    count = lax.axis_size("seq")
    groups = [[i for i in range(count) if i % 2 == core] for core in range(2)]
    many = jnp.broadcast_to(x[None], (count // 2, *x.shape))
    return lax.all_to_all(many, "seq", 0, 0, axis_index_groups=groups, tiled=True)


def body(
    q2,
    k2,
    v2,
    hidden,
    w_query,
    b_query,
    w_key,
    b_key,
    w_value,
    b_value,
    kept_index,
    block_count,
    text_rows,
):
    rank = lax.axis_index("seq")
    head = lax.axis_index("head")
    seq_count = lax.axis_size("seq")
    head_count = lax.axis_size("head")
    core = rank % 2
    chip = rank // 2
    first = rank * ROWS
    depth = hidden.shape[1]

    kv2 = lax.all_gather(jnp.concatenate([k2, v2], axis=1), "seq", axis=0, tiled=True)

    numbers = jnp.stack([core, first, 0, block_count[0], block_count[1]])
    own, sent = pick_rows(numbers, kept_index, hidden)
    x = own + from_core(sent)
    marks = x[:, depth : depth + 2].astype(jnp.int32)
    positions = marks[:, 0] * 128 + marks[:, 1]
    x = x[:, :depth]
    freqs = 1000000.0 ** (-(jnp.arange(HD // 2, dtype=F32) * 2.0) / HD)
    angles = positions.astype(F32)[:, None] * freqs[None, :]
    cosine, sine = (jnp.cos(angles), jnp.sin(angles))
    cosine = jnp.concatenate([cosine, cosine], axis=1)
    sine = jnp.concatenate([-sine, sine], axis=1)

    distances = (-1, 1, 2)
    pieces = [from_head(x, d) for d in distances]
    weights = (w_query, w_key, w_value)
    partial = project(head[None].astype(jnp.int32), [x], weights, ())
    blocks = jnp.stack([(head + d) % head_count for d in distances]).astype(jnp.int32)
    biases = tuple(b[None, :] for b in (b_query, b_key, b_value))
    q3, kv3 = project(blocks, pieces, weights, (*partial, *biases, cosine, sine))
    mine = over_chips(kv3).reshape(-1, 2 * HD)
    other = from_core(mine)

    low = jnp.sum((text_rows < first).astype(jnp.int32))
    count = jnp.sum((text_rows < first + ROWS).astype(jnp.int32)) - low
    partial_sums = text_sums(jnp.stack([rank, low, count]), text_rows, q2, kv2)
    partial_sums = partial_sums.reshape(seq_count, 1, ROWS)
    many = jnp.broadcast_to(partial_sums, (seq_count, head_count, ROWS))
    many = many.reshape(seq_count * head_count, ROWS)
    arrived = lax.all_to_all(many, ("seq", "head"), 0, 0, tiled=True)
    tokens = seq_count * ROWS
    importance = jnp.sum(arrived, axis=0) * (tokens / (GROUP * head_count * text_rows.shape[0]))

    attn2 = attend(rank[None], q2, kv2)
    attn3 = attend3(jnp.stack([chip, core]), q3, mine, other)
    return (attn2, importance, attn3)


def solution(mesh):
    placed = (
        P("seq", "head"),
        P("seq", "head"),
        P("seq", "head"),
        P("seq", "head"),
        P(None, "head"),
        P("head"),
        P(None, "head"),
        P("head"),
        P(None, "head"),
        P("head"),
        P("seq"),
        P("seq"),
        P(),
    )
    return jax.shard_map(
        body,
        mesh=mesh,
        in_specs=placed,
        out_specs=(P("seq", "head"), P("seq"), P("seq", "head")),
        check_vma=False,
    )
```

time: 343 us -> 169 us (0.49)
  the two profiles are of different devices: /device:TPU:1 before, /device:TPU:23 now
where the time goes in v1:
time: 169 us
  Pallas kernels  82 us (49%)
  blocking collectives  19.8 us (12%)
  waiting for transfers between devices  16.8 us (10%)
  between operations  15.5 us (9%)
  starting transfers between devices  14.9 us (9%)
  local copies, waits for them, and re-layouts  13.2 us (8%)
  other arithmetic  6.47 us (4%)
    pallas_call x1, Pallas kernels, attend(): pl.pallas_call(attend_kernel, out_shape=jax.ShapeDtypeStruct(q2.shape, BF...  43.2 us
    all_to_all x1, blocking collectives, over_chips(): lax.all_to_all(many, 'seq', 0, 0, axis_index_groups=groups, tiled=True)  19.8 us
    pallas_call x1, Pallas kernels, attend3(): pl.pallas_call(attend3_kernel, out_shape=jax.ShapeDtypeStruct((SHARE, q3....  18.2 us
    ppermute x3, waiting for transfers between devices, from_head(): lax.ppermute(x, 'head', [((i + distance) % count, i) for i in range(count)])  15.1 us
    pallas_call x2, Pallas kernels, project(): pl.pallas_call(kernel, out_shape=(jax.ShapeDtypeStruct((PAD, columns), ki...  14.7 us
    unnamed x24, local copies, waits for them, and re-layouts  12.3 us
    all_to_all x1, starting transfers between devices, body(): arrived = lax.all_to_all(many, ('seq', 'head'), 0, 0, tiled=True)  6.8 us
    ppermute x3, starting transfers between devices, from_head(): lax.ppermute(x, 'head', [((i + distance) % count, i) for i in range(count)])  5.14 us
  transfers between devices with their start and end apart: 7, of which 3 were waited for; matrix products, arithmetic and copies ran while one was open for 3% of the time, Pallas kernels for 46%

profile of v1, /device:TPU:23, one launch (start us, length us, event | category | flops | bytes accessed | tf_op | source)
XLA Modules:
  0.0 168.7 jit_solution(10006770385125113376)
XLA Ops:
  7.2 0.0 all-gather.2.cloned.1.call-start
  7.2 1.5 pad_maximum_fusion
  8.8 0.0 all-gather.2.cloned.1.call-update
  8.8 0.7 pad_add_fusion.3.info
  9.5 0.0 copy-start.10
  9.5 1.2 copy-done.10
  10.8 0.0 copy-start.11
  10.8 0.7 copy-done.11
  11.4 0.0 copy-start.1
  11.4 1.1 pick_rows.1
  12.5 0.8 collective-permute-start
  13.3 0.0 copy-start.2
  13.3 0.1 pad_add_fusion.2.refs_0_
  13.4 1.7 collective-permute-done
  15.1 1.2 add.41
  16.3 0.1 slice.19.refs_1_
  16.3 1.7 %collective-permute-start.1 = (bf16[136,2048]{1,0:T(8,128)(2,1)S(1)}, bf16[136,2048]{1,0:T(8,128)(2,1)S(1)}, u32[]{:S(2)}, u32[]{:S(2)}) collective-permute-start(bf16[136,2048]{1,0:T(8,128)(2,1)S(1)} %slice.19.refs_1_), channel_id=1, source_target_pairs={{3,0},{0,1},{1,2},{2,3},{7,4},{4,5},{5,6},{6,7},{11,8},{8,9},{9,10... | collective-permute-start | bytes 1671176 | tf_op jit(solution)/shard_map/ppermute | solution.py:396
  18.0 2.2 %collective-permute-start.2 = (bf16[136,2048]{1,0:T(8,128)(2,1)S(1)}, bf16[136,2048]{1,0:T(8,128)(2,1)S(1)}, u32[]{:S(2)}, u32[]{:S(2)}) collective-permute-start(bf16[136,2048]{1,0:T(8,128)(2,1)S(1)} %slice.19.refs_1_), channel_id=1, source_target_pairs={{1,0},{2,1},{3,2},{0,3},{5,4},{6,5},{7,6},{4,7},{9,8},{10,9},{11,1... | collective-permute-start | bytes 1671176 | tf_op jit(solution)/shard_map/ppermute | solution.py:396
  20.2 1.2 collective-permute-start.3
  21.5 0.0 copy-done.1
  21.5 0.0 copy-done.2
  21.5 0.0 copy-start
  21.5 6.0 %copy-done = bf16[8192,1024]{1,0:T(8,128)(2,1)S(1)} copy-done((bf16[8192,1024]{1,0:T(8,128)(2,1)S(1)}, bf16[8192,1024]{1,0:T(8,128)(2,1)}, u32[]{:S(2)}) %copy-start) | copy-done | bytes 16777240
  27.5 0.0 copy-start.6
  27.5 0.0 copy-start.8
  27.5 0.0 copy-start.9
  27.5 2.5 %project_own.1 = (f32[136,1024]{1,0:T(8,128)S(1)}, f32[136,256]{1,0:T(8,128)S(1)}) custom-call(s32[1]{0:T(128)} %bitcast.10.refs_0_, bf16[136,2048]{1,0:T(8,128)(2,1)S(1)} %slice.19.refs_1_, bf16[8192,1024]{1,0:T(8,128)(2,1)S(1)} %copy-done, bf16[8192,128]{1,0:T(8,128)(2,1)S(1)} %copy-done.1, bf16[8192,128]{1,0:T(8,128)(2,1)S(1)} %copy-done.2), custom_call_target="tpu_custom_call" | custom-call | flops 713031680 | bytes 5242880 | tf_op jit(solution)/shard_map/project_own/pallas_call | solution.py:155
  29.9 0.2 fusion.1
  30.1 0.3 fusion.2
  30.5 0.1 pad_maximum_fusion.1
  30.6 2.4 %collective-permute-done.1.refs_1_ = bf16[136,2048]{1,0:T(8,128)(2,1)S(1)} collective-permute-done((bf16[136,2048]{1,0:T(8,128)(2,1)S(1)}, bf16[136,2048]{1,0:T(8,128)(2,1)S(1)}, u32[]{:S(2)}, u32[]{:S(2)}) %collective-permute-start.1) | collective-permute-done | bytes 557088 | tf_op jit(solution)/shard_map/ppermute | solution.py:396
  32.9 0.0 collective-permute-done.2.refs_2_
  32.9 12.7 %collective-permute-done.3.refs_3_ = bf16[136,2048]{1,0:T(8,128)(2,1)S(1)} collective-permute-done((bf16[136,2048]{1,0:T(8,128)(2,1)S(1)}, bf16[136,2048]{1,0:T(8,128)(2,1)S(1)}, u32[]{:S(2)}, u32[]{:S(2)}) %collective-permute-start.3) | collective-permute-done | bytes 557088 | tf_op jit(solution)/shard_map/ppermute | solution.py:396
  45.6 0.0 copy-done.6
  45.6 0.0 copy-done.8
  45.6 0.0 copy-done.9
  45.7 12.2 %project_rest.1 = (bf16[136,1024]{1,0:T(8,128)(2,1)S(1)}, bf16[136,256]{1,0:T(8,128)(2,1)S(1)}) custom-call(s32[3]{0:T(128)S(1)} %pad_add_fusion.2.refs_0_, bf16[136,2048]{1,0:T(8,128)(2,1)S(1)} %collective-permute-done.1.refs_1_, bf16[136,2048]{1,0:T(8,128)(2,1)S(1)} %collective-permute-done.2.refs_2_, ...), custom_call_target="tpu_custom_call" | custom-call | flops 2139095040 | bytes 15728640 | tf_op jit(solution)/shard_map/project_rest/pallas_call | solution.py:155
  57.9 0.0 copy-start.7
  57.9 0.1 broadcast_in_dim.37
  58.0 19.8 %all_to_all.14 = bf16[16,136,256]{2,1,0:T(8,128)(2,1)S(1)} all-to-all(bf16[16,136,256]{2,1,0:T(8,128)(2,1)S(1)} %broadcast_in_dim.37), channel_id=1, replica_groups={{0,8,16,24,32,40,48,56,64,72,80,88,96,104,112,120},{4,12,20,28,36,44,52..., dimensions={0} | all-to-all | bytes 2228224 | tf_op jit(solution)/shard_map/all_to_all | solution.py:403
  77.8 2.2 %collective-permute-start.4 = (bf16[2176,256]{1,0:T(8,128)(2,1)S(1)}, bf16[2176,256]{1,0:T(8,128)(2,1)S(1)}, u32[]{:S(2)}, u32[]{:S(2)}) collective-permute-start(bf16[2176,256]{1,0:T(8,128)(2,1)S(1)} %bitcast.15), channel_id=1, source_target_pairs={{4,0},{0,4},{12,8},{8,12},{20,16},{16,20},{28,24},{24,28},{36,32},... | collective-permute-start | bytes 3342344 | tf_op jit(solution)/shard_map/ppermute | solution.py:391
  80.0 0.0 copy-done.7
  80.0 0.7 fusion.3
  82.0 0.1 pad_add_fusion.1.info
  82.1 0.8 pad_add_fusion.info
  82.9 0.0 collective-permute-done.4.other_ref
  82.9 0.0 copy-start.5
  82.9 18.2 %attend3.1 = bf16[132,1024]{1,0:T(8,128)(2,1)} custom-call(s32[2]{0:T(128)S(1)} %pad_add_fusion.1.info, bf16[136,1024]{1,0:T(8,128)(2,1)S(1)} %get-tuple-element.13.q_ref, bf16[2176,256]{1,0:T(8,128)(2,1)S(1)} %bitcast.16, bf16[2176,256]{1,0:T(8,128)(2,1)S(1)} %collective-permute-done.4.other_ref), custom_call_target="tpu_custom_call" | custom-call | flops 3636461568 | bytes 2228224 | tf_op jit(solution)/shard_map/attend3/pallas_call | solution.py:368
  101.0 0.0 all-gather.2.cloned.1.call-done.kv_ref
  101.0 0.0 copy-done.5
  101.0 0.0 copy-start.3
  101.0 2.2 %copy-done.3 = bf16[8192,256]{1,0:T(8,128)(2,1)S(1)} copy-done((bf16[8192,256]{1,0:T(8,128)(2,1)S(1)}, bf16[8192,256]{1,0:T(8,128)(2,1)}, u32[]{:S(2)}) %copy-start.3) | copy-done | bytes 4194328
  103.2 4.9 %text_sums.1 = f32[8,1024]{1,0:T(8,128)S(1)} custom-call(s32[3]{0:T(128)S(1)} %pad_add_fusion.info, s32[256]{0:T(256)S(1)} %copy-done.7, bf16[256,1024]{1,0:T(8,128)(2,1)S(1)} %copy-done.5, bf16[8192,256]{1,0:T(8,128)(2,1)S(1)} %copy-done.3), custom_call_target="tpu_custom_call" | custom-call | flops 134217728 | bytes 4194304 | tf_op jit(solution)/shard_map/text_sums/pallas_call | solution.py:313
  108.1 0.8 all_to_all.9
  109.0 6.8 %all-to-all-start = ((f32[128,1,256]{2,1,0:T(1,128)}), f32[128,1,256]{2,1,0:T(1,128)S(1)}, u32[]{:S(2)}, u32[]{:S(2)}) async-start(f32[128,1,256]{2,1,0:T(1,128)} %all_to_all.9), calls=%async_computation | async-start | bytes 262144 | tf_op jit(solution)/shard_map/all_to_all | solution.py:460
  115.8 0.0 copy-start.4
  115.8 2.2 %copy-done.4 = bf16[8192,256]{1,0:T(8,128)(2,1)S(1)} copy-done((bf16[8192,256]{1,0:T(8,128)(2,1)S(1)}, bf16[8192,256]{1,0:T(8,128)(2,1)}, u32[]{:S(2)}) %copy-start.4) | copy-done | bytes 4194328
  118.0 43.2 %attend2.1 = bf16[256,1024]{1,0:T(8,128)(2,1)} custom-call(s32[1]{0:T(128)} %bitcast.info, bf16[256,1024]{1,0:T(8,128)(2,1)S(1)} %copy-done.5, bf16[8192,256]{1,0:T(8,128)(2,1)S(1)} %copy-done.4), custom_call_target="tpu_custom_call" | custom-call | flops 12884901888 | bytes 4194304 | tf_op jit(solution)/shard_map/attend2/pallas_call | solution.py:240
  161.1 0.0 all-to-all-done
  161.2 0.7 reduce_sum.29
  (4 shorter events, 0.1 us)
Async XLA Ops:
  7.2 93.9 %all-gather.2.cloned.1.call-start = ((), (), s32[]{:S(2)}) async-start(), calls=%async_computation.2 | async-start | bytes 4325376 | tf_op jit(solution)/shard_map/all_gather | solution.py:430
  9.5 1.2 copy-start.10
  10.8 0.7 copy-start.11
  11.4 10.0 %copy-start.1 = (bf16[8192,128]{1,0:T(8,128)(2,1)S(1)}, bf16[8192,128]{1,0:T(8,128)(2,1)}, u32[]{:S(2)}) copy-start(bf16[8192,128]{1,0:T(8,128)(2,1)} %refs_5_.1) | copy-start | bytes 6291460
  12.5 2.5 %collective-permute-start = (bf16[136,2176]{1,0:T(8,128)(2,1)S(1)}, bf16[136,2176]{1,0:T(8,128)(2,1)}, u32[]{:S(2)}, u32[]{:S(2)}) collective-permute-start(bf16[136,2176]{1,0:T(8,128)(2,1)S(1)} %get-tuple-element.10), channel_id=1, source_target_pairs={{4,0},{0,4},{12,8},{8,12},{20,16},{16,20},{28,24},{24,28},{36,32},... | collective-permute-start | bytes 1775624 | tf_op jit(solution)/shard_map/ppermute | solution.py:391
  13.3 8.2 %copy-start.2 = (bf16[8192,128]{1,0:T(8,128)(2,1)S(1)}, bf16[8192,128]{1,0:T(8,128)(2,1)}, u32[]{:S(2)}) copy-start(bf16[8192,128]{1,0:T(8,128)(2,1)} %refs_6_.1) | copy-start | bytes 6291460
  16.3 16.6 %collective-permute-start.1 = (bf16[136,2048]{1,0:T(8,128)(2,1)S(1)}, bf16[136,2048]{1,0:T(8,128)(2,1)S(1)}, u32[]{:S(2)}, u32[]{:S(2)}) collective-permute-start(bf16[136,2048]{1,0:T(8,128)(2,1)S(1)} %slice.19.refs_1_), channel_id=1, source_target_pairs={{3,0},{0,1},{1,2},{2,3},{7,4},{4,5},{5,6},{6,7},{11,8},{8,9},{9,10... | collective-permute-start | bytes 1671176 | tf_op jit(solution)/shard_map/ppermute | solution.py:396
  18.0 14.9 %collective-permute-start.2 = (bf16[136,2048]{1,0:T(8,128)(2,1)S(1)}, bf16[136,2048]{1,0:T(8,128)(2,1)S(1)}, u32[]{:S(2)}, u32[]{:S(2)}) collective-permute-start(bf16[136,2048]{1,0:T(8,128)(2,1)S(1)} %slice.19.refs_1_), channel_id=1, source_target_pairs={{1,0},{2,1},{3,2},{0,3},{5,4},{6,5},{7,6},{4,7},{9,8},{10,9},{11,1... | collective-permute-start | bytes 1671176 | tf_op jit(solution)/shard_map/ppermute | solution.py:396
  20.2 25.4 %collective-permute-start.3 = (bf16[136,2048]{1,0:T(8,128)(2,1)S(1)}, bf16[136,2048]{1,0:T(8,128)(2,1)S(1)}, u32[]{:S(2)}, u32[]{:S(2)}) collective-permute-start(bf16[136,2048]{1,0:T(8,128)(2,1)S(1)} %slice.19.refs_1_), channel_id=1, source_target_pairs={{2,0},{3,1},{0,2},{1,3},{6,4},{7,5},{4,6},{5,7},{10,8},{11,9},{8,1... | collective-permute-start | bytes 1671176 | tf_op jit(solution)/shard_map/ppermute | solution.py:396
  21.5 6.0 %copy-start = (bf16[8192,1024]{1,0:T(8,128)(2,1)S(1)}, bf16[8192,1024]{1,0:T(8,128)(2,1)}, u32[]{:S(2)}) copy-start(bf16[8192,1024]{1,0:T(8,128)(2,1)} %refs_4_.3) | copy-start | bytes 50331652
  27.5 18.2 %copy-start.6 = (f32[1024]{0:T(1024)S(1)}, f32[1024]{0:T(1024)}, u32[]{:S(2)}) copy-start(f32[1024]{0:T(1024)} %param.18) | copy-start | bytes 12292
  27.5 18.2 %copy-start.8 = (f32[128]{0:T(128)S(1)}, f32[128]{0:T(128)}, u32[]{:S(2)}) copy-start(f32[128]{0:T(128)} %param.20) | copy-start | bytes 1540
  27.5 18.2 %copy-start.9 = (f32[128]{0:T(128)S(1)}, f32[128]{0:T(128)}, u32[]{:S(2)}) copy-start(f32[128]{0:T(128)} %param.22) | copy-start | bytes 1540
  57.9 22.1 %copy-start.7 = (s32[256]{0:T(256)S(1)}, s32[256]{0:T(256)}, u32[]{:S(2)}) copy-start(s32[256]{0:T(256)} %text.1) | copy-start | bytes 3076
  77.8 5.1 %collective-permute-start.4 = (bf16[2176,256]{1,0:T(8,128)(2,1)S(1)}, bf16[2176,256]{1,0:T(8,128)(2,1)S(1)}, u32[]{:S(2)}, u32[]{:S(2)}) collective-permute-start(bf16[2176,256]{1,0:T(8,128)(2,1)S(1)} %bitcast.15), channel_id=1, source_target_pairs={{4,0},{0,4},{12,8},{8,12},{20,16},{16,20},{28,24},{24,28},{36,32},... | collective-permute-start | bytes 3342344 | tf_op jit(solution)/shard_map/ppermute | solution.py:391
  82.9 18.2 %copy-start.5 = (bf16[256,1024]{1,0:T(8,128)(2,1)S(1)}, bf16[256,1024]{1,0:T(8,128)(2,1)}, u32[]{:S(2)}) copy-start(bf16[256,1024]{1,0:T(8,128)(2,1)} %q_ref.3) | copy-start | bytes 1572868
  101.0 2.2 %copy-start.3 = (bf16[8192,256]{1,0:T(8,128)(2,1)S(1)}, bf16[8192,256]{1,0:T(8,128)(2,1)}, u32[]{:S(2)}) copy-start(bf16[8192,256]{1,0:T(8,128)(2,1)} %all-gather.2.cloned.1.call-done.kv_ref) | copy-start | bytes 12582916
  109.0 52.2 %all-to-all-start = ((f32[128,1,256]{2,1,0:T(1,128)}), f32[128,1,256]{2,1,0:T(1,128)S(1)}, u32[]{:S(2)}, u32[]{:S(2)}) async-start(f32[128,1,256]{2,1,0:T(1,128)} %all_to_all.9), calls=%async_computation | async-start | bytes 262144 | tf_op jit(solution)/shard_map/all_to_all | solution.py:460
  115.8 2.2 %copy-start.4 = (bf16[8192,256]{1,0:T(8,128)(2,1)S(1)}, bf16[8192,256]{1,0:T(8,128)(2,1)}, u32[]{:S(2)}) copy-start(bf16[8192,256]{1,0:T(8,128)(2,1)} %all-gather.2.cloned.1.call-done.kv_ref) | copy-start | bytes 12582916
Sparse Core Ops, SparseCore 0:
  10.8 46.6 all-gather.1

commit v2 on v1

v2 whole, which is shorter than its diff:
```python
import math

import jax
import jax.numpy as jnp
from jax import lax
from jax.experimental import pallas as pl
from jax.experimental.pallas import tpu as pltpu
from jax.sharding import PartitionSpec as P

HD = 128
GROUP = 8
BLOCK = 128
ROWS = 256
SHARE = 132
PAD = 136
WIDE = 2048
TILE = 512
FACTOR = math.log2(math.e) / math.sqrt(HD)
LOW = -1e30
BF = jnp.bfloat16
F32 = jnp.float32


def dot(a, b):
    return jnp.dot(a, b, preferred_element_type=F32)


def dot_t(a, b):
    return lax.dot_general(a, b, (((1,), (1,)), ((), ())), preferred_element_type=F32)


def whole(shape):
    return pl.BlockSpec(shape, lambda *_: (0,) * len(shape))


def smem():
    return pl.BlockSpec(memory_space=pltpu.SMEM)


def pick_kernel(info, index_ref, hidden_ref, own_ref, send_ref):
    core, first, before, live0, live1 = (info[i] for i in range(5))
    count = live0 + live1
    start = jnp.where(core == 0, 0, 2 * SHARE - count)
    lane = lax.broadcasted_iota(jnp.int32, (PAD, ROWS), 1)
    place = lax.broadcasted_iota(jnp.int32, (PAD, ROWS), 0)
    second = lane >= BLOCK
    within = jnp.where(second, lane - BLOCK, lane)
    rank = jnp.where(second, within + live0, within)
    live = within < jnp.where(second, live1, live0)
    row = index_ref[...] + jnp.where(second, BLOCK, 0)
    column = lax.broadcasted_iota(jnp.int32, (PAD, BLOCK), 1)
    for out_ref, base in ((own_ref, SHARE * core), (send_ref, SHARE * (1 - core))):
        wanted = place + (base - start)
        match = (rank == wanted) & live & (place < SHARE)
        source = jnp.sum(jnp.where(match, (row + 1).astype(F32), 0.0), axis=1, keepdims=True)
        source = source.astype(jnp.int32) - 1
        select = jnp.where(lane == source, 1.0, 0.0).astype(BF)
        out_ref[:, : hidden_ref.shape[1]] = dot(select, hidden_ref[...]).astype(BF)
        position = jnp.where(source >= 0, source + first, 0)
        high = jnp.where(column == 0, position >> 7, 0)
        marks = jnp.where(column == 1, position & 127, high)
        out_ref[:, hidden_ref.shape[1] :] = marks.astype(F32).astype(BF)


def pick_rows(info, kept_index, hidden):
    width = hidden.shape[1] + BLOCK
    shape = jax.ShapeDtypeStruct((PAD, width), BF)
    return pl.pallas_call(
        pick_kernel,
        out_shape=(shape, shape),
        in_specs=[smem(), pl.BlockSpec(memory_space=pltpu.VMEM), pl.BlockSpec(memory_space=pltpu.VMEM)],
        out_specs=(pl.BlockSpec(memory_space=pltpu.VMEM),) * 2,
        compiler_params=pltpu.CompilerParams(vmem_limit_bytes=24 << 20),
        cost_estimate=pl.CostEstimate(
            flops=4 * PAD * ROWS * width, transcendentals=0, bytes_accessed=4 * ROWS * width
        ),
        name="pick_rows",
    )(info, kept_index.reshape(1, ROWS), hidden)


def rotated(u, cosine, sine):
    return u * cosine + pltpu.roll(u, HD // 2, 1) * sine


def project_kernel(pieces, last, blocks, *refs):
    x_refs = refs[:pieces]
    wq, wk, wv = refs[pieces : pieces + 3]
    rest = refs[pieces + 3 :]
    if last:
        q_in, kv_in, bq, bk, bv, cosine, sine, q_out, kv_out = rest
        c, s = (cosine[...], sine[...])
    else:
        q_out, kv_out = rest
    depth = x_refs[0].shape[1]

    def product(w, part):
        total = None
        for p in range(pieces):
            at = pl.ds(pl.multiple_of(blocks[p] * depth, depth), depth)
            got = dot(x_refs[p][...], w[at, part])
            total = got if total is None else total + got
        return total

    every = slice(0, HD)
    key, value = (product(wk, every), product(wv, every))
    if last:
        key = key + kv_in[:, :HD] + bk[...]
        kv_out[:, :HD] = rotated(key, c, s).astype(BF)
        kv_out[:, HD:] = (value + kv_in[:, HD:] + bv[...]).astype(BF)
    else:
        kv_out[:, :HD] = key
        kv_out[:, HD:] = value
    columns = wq.shape[1]
    for n in range(0, columns, TILE):
        part = slice(n, n + TILE)
        query = product(wq, part)
        if last:
            query = query + q_in[:, part] + bq[:, part]
            for h in range(0, TILE, HD):
                q_out[:, n + h : n + h + HD] = rotated(query[:, h : h + HD], c, s).astype(BF)
        else:
            q_out[:, part] = query


def project(blocks, xs, weights, extra):
    pieces = len(xs)
    last = bool(extra)
    depth = xs[0].shape[1]
    columns = weights[0].shape[1]
    kind = BF if last else F32
    vmem = pl.BlockSpec(memory_space=pltpu.VMEM)

    def kernel(*refs):
        project_kernel(pieces, last, *refs)

    return pl.pallas_call(
        kernel,
        out_shape=(
            jax.ShapeDtypeStruct((PAD, columns), kind),
            jax.ShapeDtypeStruct((PAD, 2 * HD), kind),
        ),
        in_specs=[smem()] + [vmem] * (pieces + 3 + len(extra)),
        out_specs=(vmem, vmem),
        compiler_params=pltpu.CompilerParams(vmem_limit_bytes=32 << 20),
        cost_estimate=pl.CostEstimate(
            flops=2 * pieces * PAD * depth * (columns + 2 * HD),
            transcendentals=0,
            bytes_accessed=2 * pieces * depth * (columns + 2 * HD),
        ),
        name="project_rest" if last else "project_own",
    )(blocks, *xs, *weights, *extra)


def in_turn(heads, scored, weighed):
    ahead = scored(heads[0])
    for at, h in enumerate(heads):
        scores = ahead
        if at + 1 < len(heads):
            ahead = scored(heads[at + 1])
        weighed(h, scores)


def attend_kernel(heads, info, q_ref, mine_ref, other_ref, *refs):
    out_ref, q_s, top_s, sum_s, k_s, v_s, bias_s = refs[-7:]
    step = pl.program_id(0)
    half = pl.num_programs(0) // 2
    chip, core = info[0], info[1]
    mine = step < half
    at = jnp.where(mine, step, step - half)
    limit = (jnp.where(mine, chip, chip + core)) * ROWS - at * WIDE
    ends = jnp.where(mine, limit + ROWS, limit)

    @pl.when(step == 0)
    def _():
        for h in range(heads):
            q_s[h] = q_ref[:, h * HD : (h + 1) * HD]
        top_s[...] = jnp.full_like(top_s, LOW)
        sum_s[...] = jnp.zeros_like(sum_s)
        v_s[:, HD:] = jnp.ones((WIDE, HD), BF)

    for chosen, ref in ((mine, mine_ref), (jnp.logical_not(mine), other_ref)):

        @pl.when(chosen & (ends > 0))
        def _(ref=ref):
            k_s[...] = ref[:, :HD]
            v_s[:, :HD] = ref[:, HD:]

    def run(masked):
        if masked:
            key = lax.broadcasted_iota(jnp.int32, (ROWS, WIDE), 1)
            query = lax.broadcasted_iota(jnp.int32, (ROWS, WIDE), 0)
            bound = jnp.where(mine, query + 1, 0) + limit
            bias_s[...] = jnp.where(key < bound, 0.0, LOW)

        def scored(h):
            scores = dot_t(q_s[h], k_s[...])
            if masked:
                scores = scores + bias_s[...]
            return scores

        def weighed(h, scores):
            before = top_s[h]
            top = jnp.maximum(before, jnp.max(scores, axis=1, keepdims=True))
            top_s[h] = top
            weights = jnp.exp2((scores - top[:, :1]) * FACTOR).astype(BF)
            fade = jnp.exp2((before - top) * FACTOR)
            fade = jnp.concatenate([fade, fade], axis=1)
            sum_s[h] = sum_s[h] * fade + dot(weights, v_s[...])

        in_turn(range(heads), scored, weighed)

    @pl.when(limit >= WIDE)
    def _():
        run(False)

    @pl.when((limit < WIDE) & (ends > 0))
    def _():
        run(True)

    @pl.when(step == 2 * half - 1)
    def _():
        for h in range(heads):
            total = sum_s[h]
            out_ref[:, h * HD : (h + 1) * HD] = (total[:, :HD] / total[:, HD:]).astype(BF)


def attend(info, q2, mine, other, part=0, parts=1, filled=None):
    tokens = mine.shape[0]
    half = tokens // WIDE
    heads = GROUP // parts
    block = pl.BlockSpec((q2.shape[0], heads * HD), lambda i, info: (0, part))
    spec = pltpu.PrefetchScalarGridSpec(
        num_scalar_prefetch=1,
        grid=(2 * half,),
        in_specs=[
            block,
            pl.BlockSpec((WIDE, 2 * HD), lambda i, info: (jnp.minimum(i, info[0] * ROWS // WIDE), 0)),
            pl.BlockSpec(
                (WIDE, 2 * HD),
                lambda i, info: (jnp.clip(i - half, 0, info[0] * ROWS // WIDE), 0),
            ),
        ]
        + ([] if filled is None else [pl.BlockSpec(memory_space=pl.ANY)]),
        out_specs=block,
        scratch_shapes=[
            pltpu.VMEM((heads, ROWS, HD), BF),
            pltpu.VMEM((heads, ROWS, HD), F32),
            pltpu.VMEM((heads, ROWS, 2 * HD), F32),
            pltpu.VMEM((WIDE, HD), BF),
            pltpu.VMEM((WIDE, 2 * HD), BF),
            pltpu.VMEM((ROWS, WIDE), F32),
        ],
    )

    def kernel(*refs):
        attend_kernel(heads, *refs)

    return pl.pallas_call(
        kernel,
        out_shape=jax.ShapeDtypeStruct(q2.shape, BF),
        grid_spec=spec,
        input_output_aliases={} if filled is None else {4: 0},
        compiler_params=pltpu.CompilerParams(vmem_limit_bytes=40 << 20),
        cost_estimate=pl.CostEstimate(
            flops=12 * heads * ROWS * tokens * HD,
            transcendentals=2 * heads * ROWS * tokens,
            bytes_accessed=8 * tokens * HD,
        ),
        name="attend2",
    )(info, q2, mine, other, *(() if filled is None else (filled,)))


CHUNK = 8
SPAN = 1024


def text_kernel(info, text, q_ref, mine_ref, other_ref, high_ref, low_ref, out_ref, score_s):
    chip, core, low, count = (info[i] for i in range(4))
    first = (2 * chip + core) * ROWS
    half = mine_ref.shape[0]
    blocks = SPAN // ROWS
    parts = (
        (mine_ref, 0, core, chip // blocks + 1),
        (other_ref, half, 1 - core, (chip + core + blocks - 1) // blocks),
    )
    out_ref[...] = jnp.zeros_like(out_ref)
    rows = GROUP * CHUNK

    def chunk(c, carry):
        place = jnp.zeros((CHUNK, ROWS), jnp.int32)
        sub = lax.broadcasted_iota(jnp.int32, (CHUNK, ROWS), 0)
        for i in range(CHUNK):
            n = c * CHUNK + i
            at = text[jnp.minimum(low + n, text.shape[0] - 1)] - first
            place = jnp.where(sub == i, jnp.where(n < count, at, -1), place)
        lane = lax.broadcasted_iota(jnp.int32, (CHUNK, ROWS), 1)
        select = jnp.where(lane == place, 1.0, 0.0).astype(BF)
        picked = dot(select, q_ref[...]).astype(BF)
        queries = jnp.concatenate(
            [picked[:, h * HD : (h + 1) * HD] for h in range(GROUP)], axis=0
        )
        place = jnp.concatenate([place[:, :HD]] * GROUP, axis=0)[:, :1]
        limit = first + jnp.maximum(place, 0)
        lane = lax.broadcasted_iota(jnp.int32, (1, SPAN), 1)
        spread = lane + (lane // ROWS) * ROWS

        top = jnp.full((rows, 1), LOW, F32)
        for ref, offset, parity, steps in parts:

            def scored(b, top, ref=ref, offset=offset, parity=parity):
                keys = ref[pl.ds(pl.multiple_of(b * SPAN, SPAN), SPAN), :HD]
                position = spread + (2 * b * SPAN + parity * ROWS)
                scores = jnp.where(position <= limit, dot_t(queries, keys), LOW)
                score_s[:, pl.ds(pl.multiple_of(offset + b * SPAN, SPAN), SPAN)] = scores
                return jnp.maximum(top, jnp.max(scores, axis=1, keepdims=True))

            top = lax.fori_loop(0, steps, scored, top)
        total = jnp.zeros((rows, 1), F32)
        for _, offset, _, steps in parts:

            def weighed(b, total, offset=offset):
                at = pl.ds(pl.multiple_of(offset + b * SPAN, SPAN), SPAN)
                weights = jnp.exp2((score_s[:, at] - top) * FACTOR)
                score_s[:, at] = weights
                return total + jnp.sum(weights, axis=1, keepdims=True)

            total = lax.fori_loop(0, steps, weighed, total)
        share = jnp.where(place >= 0, 1.0 / total, 0.0)
        for _, offset, parity, steps in parts:

            def summed(b, carry, offset=offset, parity=parity):
                at = pl.ds(pl.multiple_of(offset + b * SPAN, SPAN), SPAN)
                sums = jnp.sum(score_s[:, at] * share, axis=0, keepdims=True)
                for i in range(blocks):
                    to = pl.ds(2 * (b * blocks + i) + parity, 1)
                    out_ref[to, :] += sums[:, i * ROWS : (i + 1) * ROWS]
                return carry

            lax.fori_loop(0, steps, summed, 0)
        return carry

    lax.fori_loop(0, (count + CHUNK - 1) // CHUNK, chunk, 0)
    high = out_ref[...].astype(BF)
    high_ref[...] = high
    low_ref[...] = (out_ref[...] - high.astype(F32)).astype(BF)


def text_sums(info, text_rows, q2, mine, other):
    tokens = 2 * mine.shape[0]
    vmem = pl.BlockSpec(memory_space=pltpu.VMEM)
    return pl.pallas_call(
        text_kernel,
        out_shape=(jax.ShapeDtypeStruct((tokens // ROWS, ROWS), BF),) * 2,
        in_specs=[smem(), smem(), vmem, vmem, vmem],
        out_specs=(vmem, vmem),
        scratch_shapes=[
            pltpu.VMEM((tokens // ROWS, ROWS), F32),
            pltpu.VMEM((GROUP * CHUNK, tokens), F32),
        ],
        compiler_params=pltpu.CompilerParams(vmem_limit_bytes=24 << 20),
        cost_estimate=pl.CostEstimate(
            flops=2 * GROUP * CHUNK * tokens * HD,
            transcendentals=GROUP * CHUNK * tokens,
            bytes_accessed=4 * tokens * HD,
        ),
        name="text_sums",
    )(info, text_rows, q2, mine, other)


def attend3_kernel(info, q_ref, mine_ref, other_ref, out_ref, v_s, bias_s):
    chip, core = info[0], info[1]
    half = mine_ref.shape[0]
    v_s[:half, :HD] = mine_ref[:, HD:]
    v_s[half:, :HD] = other_ref[:, HD:]
    v_s[:, HD:] = jnp.ones((2 * half, HD), BF)
    row = lax.broadcasted_iota(jnp.int32, (1, half), 1)
    rest = row % PAD
    live = rest < SHARE
    query = lax.broadcasted_iota(jnp.int32, (PAD, half), 0)
    start = chip * PAD
    own = (row - start <= query) & live
    bias_s[:, :half] = jnp.where(own, 0.0, LOW)
    earlier = (row < start + core * PAD) & live
    bias_s[:, half:] = jnp.where(earlier & (query >= 0), 0.0, LOW)

    def scored(h):
        q = q_ref[:, h * HD : (h + 1) * HD]
        left = dot_t(q, mine_ref[:, :HD]) + bias_s[:, :half]
        right = dot_t(q, other_ref[:, :HD]) + bias_s[:, half:]
        return left, right

    def weighed(h, scores):
        left, right = scores
        top = jnp.maximum(
            jnp.max(left, axis=1, keepdims=True), jnp.max(right, axis=1, keepdims=True)
        )
        left = jnp.exp2((left - top) * FACTOR).astype(BF)
        right = jnp.exp2((right - top) * FACTOR).astype(BF)
        total = dot(left, v_s[:half]) + dot(right, v_s[half:])
        out = (total[:, :HD] / total[:, HD:]).astype(BF)
        out_ref[:, h * HD : (h + 1) * HD] = out[:SHARE]

    in_turn(range(GROUP), scored, weighed)


def attend3(info, q3, mine, other):
    vmem = pl.BlockSpec(memory_space=pltpu.VMEM)
    keys = 2 * mine.shape[0]
    return pl.pallas_call(
        attend3_kernel,
        out_shape=jax.ShapeDtypeStruct((SHARE, q3.shape[1]), BF),
        in_specs=[smem(), vmem, vmem, vmem],
        out_specs=vmem,
        scratch_shapes=[
            pltpu.VMEM((keys, 2 * HD), BF),
            pltpu.VMEM((PAD, keys), F32),
        ],
        compiler_params=pltpu.CompilerParams(vmem_limit_bytes=40 << 20),
        cost_estimate=pl.CostEstimate(
            flops=6 * GROUP * PAD * keys * HD,
            transcendentals=GROUP * PAD * keys,
            bytes_accessed=4 * keys * HD,
        ),
        name="attend3",
    )(info, q3, mine, other)


def from_core(x):
    count = lax.axis_size("seq")
    return lax.ppermute(x, "seq", [(i ^ 1, i) for i in range(count)])


def from_head(x, distance):
    count = lax.axis_size("head")
    return lax.ppermute(x, "head", [((i + distance) % count, i) for i in range(count)])


def over_chips(many):
    count = lax.axis_size("seq")
    groups = [[i for i in range(count) if i % 2 == core] for core in range(2)]
    return lax.all_to_all(many, "seq", 0, 0, axis_index_groups=groups, tiled=True)


def over_heads(x):
    count = lax.axis_size("head")
    step = 1
    while step < count:
        x = x + lax.ppermute(x, "head", [(i ^ step, i) for i in range(count)])
        step *= 2
    return x


def body(
    q2,
    k2,
    v2,
    hidden,
    w_query,
    b_query,
    w_key,
    b_key,
    w_value,
    b_value,
    kept_index,
    block_count,
    text_rows,
):
    rank = lax.axis_index("seq")
    head = lax.axis_index("head")
    seq_count = lax.axis_size("seq")
    head_count = lax.axis_size("head")
    core = rank % 2
    chip = rank // 2
    first = rank * ROWS
    depth = hidden.shape[1]

    chips = seq_count // 2
    kv2 = jnp.concatenate([k2, v2], axis=1)
    mine2 = over_chips(jnp.broadcast_to(kv2[None], (chips, *kv2.shape)))
    mine2 = mine2.reshape(-1, 2 * HD)

    numbers = jnp.stack([core, first, 0, block_count[0], block_count[1]])
    own, sent = pick_rows(numbers, kept_index, hidden)
    x = own + from_core(sent)
    marks = x[:, depth : depth + 2].astype(jnp.int32)
    positions = marks[:, 0] * 128 + marks[:, 1]
    x = x[:, :depth]
    freqs = 1000000.0 ** (-(jnp.arange(HD // 2, dtype=F32) * 2.0) / HD)
    angles = positions.astype(F32)[:, None] * freqs[None, :]
    cosine, sine = (jnp.cos(angles), jnp.sin(angles))
    cosine = jnp.concatenate([cosine, cosine], axis=1)
    sine = jnp.concatenate([-sine, sine], axis=1)

    distances = (-1, 1, 2)
    pieces = [from_head(x, d) for d in distances]
    weights = (w_query, w_key, w_value)
    partial = project(head[None].astype(jnp.int32), [x], weights, ())
    mine2, pieces, partial = lax.optimization_barrier((mine2, pieces, partial))
    other2 = from_core(mine2)
    blocks = jnp.stack([(head + d) % head_count for d in distances]).astype(jnp.int32)
    biases = tuple(b[None, :] for b in (b_query, b_key, b_value))
    q3, kv3 = project(blocks, pieces, weights, (*partial, *biases, cosine, sine))
    kv3, other2 = lax.optimization_barrier((kv3, other2))
    low = jnp.sum((text_rows < first).astype(jnp.int32))
    count = jnp.sum((text_rows < first + ROWS).astype(jnp.int32)) - low
    place = jnp.stack([chip, core])
    sums = text_sums(jnp.stack([chip, core, low, count]), text_rows, q2, mine2, other2)

    sums = [part.reshape(chips, 2, ROWS) for part in sums]
    kept = jnp.broadcast_to(kv3[None, :SHARE], (chips, SHARE, 2 * HD))
    many = jnp.concatenate([kept, *sums], axis=1)
    mine = over_chips(many)
    q2, many = lax.optimization_barrier((q2, many))
    attn2 = attend(place, q2, mine2, other2)
    attn2, mine = lax.optimization_barrier((attn2, mine))
    other = from_core(mine)
    attn3 = attend3(place, q3, mine.reshape(-1, 2 * HD), other.reshape(-1, 2 * HD))

    got = sum(jnp.sum(x[:, SHARE:].astype(F32), axis=0) for x in (mine, other))
    got = got[:2] + got[2:]
    got = over_heads(jnp.where(core == 0, got[0], got[1]))
    tokens = seq_count * ROWS
    importance = got * (tokens / (GROUP * head_count * text_rows.shape[0]))
    return (attn2, importance, attn3)


def solution(mesh):
    placed = (
        P("seq", "head"),
        P("seq", "head"),
        P("seq", "head"),
        P("seq", "head"),
        P(None, "head"),
        P("head"),
        P(None, "head"),
        P("head"),
        P(None, "head"),
        P("head"),
        P("seq"),
        P("seq"),
        P(),
    )
    return jax.shard_map(
        body,
        mesh=mesh,
        in_specs=placed,
        out_specs=(P("seq", "head"), P("seq"), P("seq", "head")),
        check_vma=False,
    )
```

time: 169 us -> 121 us (0.72)
  the two profiles are of different devices: /device:TPU:23 before, /device:TPU:6 now
where the time goes in v2:
time: 121 us
  Pallas kernels  54.1 us (45%)
  starting transfers between devices  24.5 us (20%)
  waiting for transfers between devices  21.8 us (18%)
  local copies, waits for them, and re-layouts  12.5 us (10%)
  other arithmetic  5.73 us (5%)
  between operations  2.14 us (2%)
    pallas_call x1, Pallas kernels, attend(): pl.pallas_call(kernel, out_shape=jax.ShapeDtypeStruct(q2.shape, BF), grid...  26.6 us
    all_to_all x2, starting transfers between devices, over_chips(): lax.all_to_all(many, 'seq', 0, 0, axis_index_groups=groups, tiled=True)  15 us
    ppermute x3, waiting for transfers between devices, from_head(): lax.ppermute(x, 'head', [((i + distance) % count, i) for i in range(count)])  14.4 us
    unnamed x34, local copies, waits for them, and re-layouts  10.8 us
    pallas_call x2, Pallas kernels, project(): pl.pallas_call(kernel, out_shape=(jax.ShapeDtypeStruct((PAD, columns), ki...  10.3 us
    pallas_call x1, Pallas kernels, attend3(): pl.pallas_call(attend3_kernel, out_shape=jax.ShapeDtypeStruct((SHARE, q3....  9.88 us
    pallas_call x1, Pallas kernels, text_sums(): pl.pallas_call(text_kernel, out_shape=(jax.ShapeDtypeStruct((tokens // RO...  6.16 us
    ppermute x3, starting transfers between devices, from_head(): lax.ppermute(x, 'head', [((i + distance) % count, i) for i in range(count)])  5.98 us
  transfers between devices with their start and end apart: 10, of which 5 were waited for; matrix products, arithmetic and copies ran while one was open for 3% of the time, Pallas kernels for 40%

profile of v2, /device:TPU:6, one launch (start us, length us, event | category | flops | bytes accessed | tf_op | source)
XLA Modules:
  0.0 120.7 jit_solution(481949736623591190)
XLA Ops:
  0.6 0.9 pad_maximum_fusion.1
  1.5 1.5 %broadcast_in_dim.12 = bf16[16,256,256]{2,1,0:T(8,128)(2,1)} broadcast(bf16[256,256]{1,0:T(8,128)(2,1)S(1)} %pad_maximum_fusion.1), dimensions={1,2} | broadcast | bytes 2228224 | tf_op jit(solution)/shard_map/broadcast_in_dim | solution.py:479
  3.0 0.0 copy-start.16
  3.0 0.0 copy-start.14
  3.0 7.6 %all-to-all-start = ((bf16[16,256,256]{2,1,0:T(8,128)(2,1)}), bf16[16,256,256]{2,1,0:T(8,128)(2,1)}, u32[]{:S(2)}, u32[]{:S(2)}) async-start(bf16[16,256,256]{2,1,0:T(8,128)(2,1)} %broadcast_in_dim.12), calls=%async_computation | async-start | bytes 4194304 | tf_op jit(solution)/shard_map/all_to_all | solution.py:441
  10.6 0.0 copy-done.16
  10.6 0.1 pad_add_fusion.2.info
  10.7 0.0 copy-done.11
  10.7 0.0 copy-done.14
  10.7 1.1 pick_rows.1
  11.8 0.1 collective-permute-start
  11.9 2.0 %collective-permute-done = bf16[136,2176]{1,0:T(8,128)(2,1)S(1)} collective-permute-done((bf16[136,2176]{1,0:T(8,128)(2,1)S(1)}, bf16[136,2176]{1,0:T(8,128)(2,1)S(1)}, u32[]{:S(2)}, u32[]{:S(2)}) %collective-permute-start) | collective-permute-done | bytes 591904 | tf_op jit(solution)/shard_map/ppermute | solution.py:430
  13.9 0.1 add.52
  14.0 0.0 copy-start.15
  14.1 4.0 %collective-permute-start.3 = (bf16[136,2048]{1,0:T(8,128)(2,1)S(1)}, bf16[136,2048]{1,0:T(8,128)(2,1)S(1)}, u32[]{:S(2)}, u32[]{:S(2)}) collective-permute-start(bf16[136,2048]{1,0:T(8,128)(2,1)S(1)} %slice.47.refs_1_), channel_id=1, source_target_pairs={{2,0},{3,1},{0,2},{1,3},{6,4},{7,5},{4,6},{5,7},{10,8},{11,9},{8,1... | collective-permute-start | bytes 1671176 | tf_op jit(solution)/shard_map/ppermute | solution.py:435
  18.1 0.0 copy-done.15
  18.1 0.8 collective-permute-start.2
  18.9 1.2 collective-permute-start.1
  20.1 0.0 copy-done.1
  20.1 5.8 %copy-done = bf16[8192,1024]{1,0:T(8,128)(2,1)S(1)} copy-done((bf16[8192,1024]{1,0:T(8,128)(2,1)S(1)}, bf16[8192,1024]{1,0:T(8,128)(2,1)}, u32[]{:S(2)}) %copy-start) | copy-done | bytes 16777240
  25.9 1.6 %copy-done.2 = bf16[8192,128]{1,0:T(8,128)(2,1)S(1)} copy-done((bf16[8192,128]{1,0:T(8,128)(2,1)S(1)}, bf16[8192,128]{1,0:T(8,128)(2,1)}, u32[]{:S(2)}) %copy-start.2) | copy-done | bytes 2097176
  27.5 1.1 project_own.1
  28.6 0.0 copy-start.4
  28.6 0.8 copy-done.4
  29.4 2.1 %collective-permute-done.3.refs_3_ = bf16[136,2048]{1,0:T(8,128)(2,1)S(1)} collective-permute-done((bf16[136,2048]{1,0:T(8,128)(2,1)S(1)}, bf16[136,2048]{1,0:T(8,128)(2,1)S(1)}, u32[]{:S(2)}, u32[]{:S(2)}) %collective-permute-start.3) | collective-permute-done | bytes 557088 | tf_op jit(solution)/shard_map/ppermute | solution.py:435
  31.5 12.3 %collective-permute-done.2.refs_2_ = bf16[136,2048]{1,0:T(8,128)(2,1)} collective-permute-done((bf16[136,2048]{1,0:T(8,128)(2,1)S(1)}, bf16[136,2048]{1,0:T(8,128)(2,1)}, u32[]{:S(2)}, u32[]{:S(2)}) %collective-permute-start.2) | collective-permute-done | bytes 557088 | tf_op jit(solution)/shard_map/ppermute | solution.py:435
  43.8 0.0 collective-permute-done.1.refs_1_
  43.8 0.0 all-to-all-done
  43.8 0.0 collective-permute-start.4
  43.9 0.0 copy-done.8
  43.9 0.6 fusion.3
  45.7 0.1 pad_add_fusion.refs_0_.info
  45.8 0.6 pad_add_fusion.3.info
  46.4 0.1 pad_add_fusion.1.refs_0_
  46.5 0.8 slice_convert_fusion
  47.3 0.2 fusion.1
  47.5 0.3 fusion.2
  47.8 0.1 pad_maximum_fusion.2
  47.9 0.0 copy-done.7
  47.9 0.0 copy-done.9
  47.9 0.0 copy-done.10
  48.0 0.0 copy-start.3
  48.0 1.6 %copy-done.3 = bf16[8192,128]{1,0:T(8,128)(2,1)S(1)} copy-done((bf16[8192,128]{1,0:T(8,128)(2,1)S(1)}, bf16[8192,128]{1,0:T(8,128)(2,1)}, u32[]{:S(2)}) %copy-start.3) | copy-done | bytes 2097176
  49.6 1.1 copy-done.5
  50.6 9.2 %project_rest.1 = (bf16[136,1024]{1,0:T(8,128)(2,1)S(1)}, bf16[136,256]{1,0:T(8,128)(2,1)S(1)}) custom-call(s32[3]{0:T(128)S(1)} %pad_add_fusion.1.refs_0_, bf16[136,2048]{1,0:T(8,128)(2,1)} %collective-permute-done.1.refs_1_, bf16[136,2048]{1,0:T(8,128)(2,1)} %collective-permute-done.2.refs_2_, bf16[136,2048]{1,0:T(8,128)(2,1)S(1)} %collective-permute-done.3.refs_3_, ...), custom_call_target="tpu_custom_call" | custom-call | flops 2139095040 | bytes 15728640 | tf_op jit(solution)/shard_map/project_rest/pallas_call | solution.py:136
  59.8 0.0 copy-start.12
  59.9 0.0 collective-permute-done.4.other_ref.refs_3_
  59.9 0.0 copy-done.6
  59.9 6.2 %text_sums.1 = (bf16[32,256]{1,0:T(8,128)(2,1)S(1)}, bf16[32,256]{1,0:T(8,128)(2,1)S(1)}) custom-call(s32[4]{0:T(128)S(1)} %pad_add_fusion.3.info, s32[256]{0:T(256)S(1)} %copy-done.8, bf16[256,1024]{1,0:T(8,128)(2,1)S(1)} %copy-done.6, bf16[4096,256]{1,0:T(8,128)(2,1)} %bitcast.5.mine_ref.refs_2_, bf16[4096,256]{1,0:T(8,128)(2,1)} %collective-permute-done.4.other_ref.refs_3_), custom_call_target="tpu_custom_call" | custom-call | flops 134217728 | bytes 4194304 | tf_op jit(solution)/shard_map/text_sums/pallas_call | solution.py:351
  66.0 0.0 copy-done.12
  66.1 0.1 broadcast_in_dim.31
  66.2 1.1 pad_maximum_fusion
  67.3 7.5 %all-to-all-start.1 = ((bf16[16,136,256]{2,1,0:T(8,128)(2,1)}), bf16[16,136,256]{2,1,0:T(8,128)(2,1)S(1)}, u32[]{:S(2)}, u32[]{:S(2)}) async-start(bf16[16,136,256]{2,1,0:T(8,128)(2,1)} %pad_maximum_fusion), calls=%async_computation.1 | async-start | bytes 2228224 | tf_op jit(solution)/shard_map/all_to_all | solution.py:441
  74.8 26.6 %attend2.1 = bf16[256,1024]{1,0:T(8,128)(2,1)} custom-call(s32[2]{0:T(128)S(1)} %pad_add_fusion.refs_0_.info, bf16[256,1024]{1,0:T(8,128)(2,1)S(1)} %copy-done.6, bf16[4096,256]{1,0:T(8,128)(2,1)} %bitcast.5.mine_ref.refs_2_, bf16[4096,256]{1,0:T(8,128)(2,1)} %collective-permute-done.4.other_ref.refs_3_), custom_call_target="tpu_custom_call" | custom-call | flops 12884901888 | bytes 4194304 | tf_op jit(solution)/shard_map/attend2/pallas_call | solution.py:258
  101.4 0.0 all-to-all-done.1
  101.4 0.0 collective-permute-start.5
  101.5 2.7 %collective-permute-done.5 = bf16[16,136,256]{2,1,0:T(8,128)(2,1)S(1)} collective-permute-done((bf16[16,136,256]{2,1,0:T(8,128)(2,1)S(1)}, bf16[16,136,256]{2,1,0:T(8,128)(2,1)S(1)}, u32[]{:S(2)}, u32[]{:S(2)}) %collective-permute-start.5) | collective-permute-done | bytes 1114144 | tf_op jit(solution)/shard_map/ppermute | solution.py:430
  104.2 1.0 collective-permute-start.6
  105.3 2.6 %collective-permute-done.6 = f32[256]{0:T(256)S(1)} collective-permute-done((f32[256]{0:T(256)S(1)}, f32[256]{0:T(256)S(1)}, u32[]{:S(2)}, u32[]{:S(2)}) %collective-permute-start.6) | collective-permute-done | bytes 1056 | tf_op jit(solution)/shard_map/ppermute | solution.py:448
  107.9 2.4 %collective-permute-start.7 = (f32[256]{0:T(256)S(1)}, f32[256]{0:T(256)S(1)}, u32[]{:S(2)}, u32[]{:S(2)}) collective-permute-start(f32[256]{0:T(256)S(1)} %add.57), channel_id=1, source_target_pairs={{2,0},{3,1},{0,2},{1,3},{6,4},{7,5},{4,6},{5,7},{10,8},{11,9},{8,1... | collective-permute-start | bytes 3080 | tf_op jit(solution)/shard_map/ppermute | solution.py:448
  110.3 0.0 copy-done.13
  110.3 9.9 %attend3.1 = bf16[132,1024]{1,0:T(8,128)(2,1)} custom-call(s32[2]{0:T(128)S(1)} %pad_add_fusion.refs_0_.info, bf16[136,1024]{1,0:T(8,128)(2,1)S(1)} %copy-done.13, bf16[2176,256]{1,0:T(8,128)(2,1)S(1)} %bitcast.18, bf16[2176,256]{1,0:T(8,128)(2,1)S(1)} %bitcast.21), custom_call_target="tpu_custom_call" | custom-call | flops 3636461568 | bytes 2228224 | tf_op jit(solution)/shard_map/attend3/pallas_call | solution.py:409
  120.2 0.0 collective-permute-done.7
  120.2 0.6 add.58
  (21 shorter events, 0.2 us)
Async XLA Ops:
  3.0 7.6 %copy-start.16 = (s32[2]{0:T(128)S(1)}, s32[2]{0:T(128)}, u32[]{:S(2)}) copy-start(s32[2]{0:T(128)} %param.24) | copy-start | bytes 28
  3.0 7.7 %copy-start.11 = (bf16[256,2048]{1,0:T(8,128)(2,1)S(1)}, bf16[256,2048]{1,0:T(8,128)(2,1)}, u32[]{:S(2)}) copy-start(bf16[256,2048]{1,0:T(8,128)(2,1)} %hidden_ref.1) | copy-start | bytes 3145732
  3.0 7.7 %copy-start.14 = (s32[256]{0:T(256)S(1)}, s32[256]{0:T(256)}, u32[]{:S(2)}) copy-start(s32[256]{0:T(256)} %param.23) | copy-start | bytes 3076
  3.0 40.8 %all-to-all-start = ((bf16[16,256,256]{2,1,0:T(8,128)(2,1)}), bf16[16,256,256]{2,1,0:T(8,128)(2,1)}, u32[]{:S(2)}, u32[]{:S(2)}) async-start(bf16[16,256,256]{2,1,0:T(8,128)(2,1)} %broadcast_in_dim.12), calls=%async_computation | async-start | bytes 4194304 | tf_op jit(solution)/shard_map/all_to_all | solution.py:441
  10.6 9.5 %copy-start.1 = (bf16[8192,128]{1,0:T(8,128)(2,1)S(1)}, bf16[8192,128]{1,0:T(8,128)(2,1)}, u32[]{:S(2)}) copy-start(bf16[8192,128]{1,0:T(8,128)(2,1)} %refs_5_.1) | copy-start | bytes 6291460
  11.8 2.1 %collective-permute-start = (bf16[136,2176]{1,0:T(8,128)(2,1)S(1)}, bf16[136,2176]{1,0:T(8,128)(2,1)S(1)}, u32[]{:S(2)}, u32[]{:S(2)}) collective-permute-start(bf16[136,2176]{1,0:T(8,128)(2,1)S(1)} %get-tuple-element.23), channel_id=1, source_target_pairs={{4,0},{0,4},{12,8},{8,12},{20,16},{16,20},{28,24},{24,28},{36,32},... | collective-permute-start | bytes 1775624 | tf_op jit(solution)/shard_map/ppermute | solution.py:430
  14.0 4.0 %copy-start.15 = (bf16[136,2176]{1,0:T(8,128)(2,1)}, bf16[136,2176]{1,0:T(8,128)(2,1)S(1)}, u32[]{:S(2)}) copy-start(bf16[136,2176]{1,0:T(8,128)(2,1)S(1)} %add.52) | copy-start | bytes 1775620
  14.1 17.4 %collective-permute-start.3 = (bf16[136,2048]{1,0:T(8,128)(2,1)S(1)}, bf16[136,2048]{1,0:T(8,128)(2,1)S(1)}, u32[]{:S(2)}, u32[]{:S(2)}) collective-permute-start(bf16[136,2048]{1,0:T(8,128)(2,1)S(1)} %slice.47.refs_1_), channel_id=1, source_target_pairs={{2,0},{3,1},{0,2},{1,3},{6,4},{7,5},{4,6},{5,7},{10,8},{11,9},{8,1... | collective-permute-start | bytes 1671176 | tf_op jit(solution)/shard_map/ppermute | solution.py:435
  18.1 25.7 %collective-permute-start.2 = (bf16[136,2048]{1,0:T(8,128)(2,1)S(1)}, bf16[136,2048]{1,0:T(8,128)(2,1)}, u32[]{:S(2)}, u32[]{:S(2)}) collective-permute-start(bf16[136,2048]{1,0:T(8,128)(2,1)S(1)} %slice.47.refs_1_), channel_id=1, source_target_pairs={{1,0},{2,1},{3,2},{0,3},{5,4},{6,5},{7,6},{4,7},{9,8},{10,9},{11,1... | collective-permute-start | bytes 1671176 | tf_op jit(solution)/shard_map/ppermute | solution.py:435
  18.9 24.9 %collective-permute-start.1 = (bf16[136,2048]{1,0:T(8,128)(2,1)S(1)}, bf16[136,2048]{1,0:T(8,128)(2,1)}, u32[]{:S(2)}, u32[]{:S(2)}) collective-permute-start(bf16[136,2048]{1,0:T(8,128)(2,1)S(1)} %slice.47.refs_1_), channel_id=1, source_target_pairs={{3,0},{0,1},{1,2},{2,3},{7,4},{4,5},{5,6},{6,7},{11,8},{8,9},{9,10... | collective-permute-start | bytes 1671176 | tf_op jit(solution)/shard_map/ppermute | solution.py:435
  20.1 5.8 %copy-start = (bf16[8192,1024]{1,0:T(8,128)(2,1)S(1)}, bf16[8192,1024]{1,0:T(8,128)(2,1)}, u32[]{:S(2)}) copy-start(bf16[8192,1024]{1,0:T(8,128)(2,1)} %refs_4_.3) | copy-start | bytes 50331652
  25.9 1.6 %copy-start.2 = (bf16[8192,128]{1,0:T(8,128)(2,1)S(1)}, bf16[8192,128]{1,0:T(8,128)(2,1)}, u32[]{:S(2)}) copy-start(bf16[8192,128]{1,0:T(8,128)(2,1)} %refs_6_.1) | copy-start | bytes 6291460
  27.5 16.4 %copy-start.8 = (s32[256]{0:T(256)S(1)}, s32[256]{0:T(256)}, u32[]{:S(2)}) copy-start(s32[256]{0:T(256)} %text.1) | copy-start | bytes 3076
  27.5 20.5 %copy-start.7 = (f32[1024]{0:T(1024)S(1)}, f32[1024]{0:T(1024)}, u32[]{:S(2)}) copy-start(f32[1024]{0:T(1024)} %param.18) | copy-start | bytes 12292
  27.5 20.5 %copy-start.9 = (f32[128]{0:T(128)S(1)}, f32[128]{0:T(128)}, u32[]{:S(2)}) copy-start(f32[128]{0:T(128)} %param.20) | copy-start | bytes 1540
  27.5 20.5 %copy-start.10 = (f32[128]{0:T(128)S(1)}, f32[128]{0:T(128)}, u32[]{:S(2)}) copy-start(f32[128]{0:T(128)} %param.22) | copy-start | bytes 1540
  28.6 0.8 copy-start.4
  43.8 16.1 %collective-permute-start.4 = (bf16[4096,256]{1,0:T(8,128)(2,1)}, bf16[4096,256]{1,0:T(8,128)(2,1)}, u32[]{:S(2)}, u32[]{:S(2)}) collective-permute-start(bf16[4096,256]{1,0:T(8,128)(2,1)} %bitcast.5.mine_ref.refs_2_), channel_id=1, source_target_pairs={{4,0},{0,4},{12,8},{8,12},{20,16},{16,20},{28,24},{24,28},{36,32},... | collective-permute-start | bytes 6291464 | tf_op jit(solution)/shard_map/ppermute | solution.py:430
  48.0 1.6 %copy-start.3 = (bf16[8192,128]{1,0:T(8,128)(2,1)S(1)}, bf16[8192,128]{1,0:T(8,128)(2,1)}, u32[]{:S(2)}) copy-start(bf16[8192,128]{1,0:T(8,128)(2,1)} %refs_6_.1) | copy-start | bytes 6291460
  49.6 1.1 copy-start.5
  50.6 9.3 %copy-start.6 = (bf16[256,1024]{1,0:T(8,128)(2,1)S(1)}, bf16[256,1024]{1,0:T(8,128)(2,1)}, u32[]{:S(2)}) copy-start(bf16[256,1024]{1,0:T(8,128)(2,1)} %refs_1_) | copy-start | bytes 1572868
  59.8 6.2 %copy-start.12 = (bf16[136,1024]{1,0:T(8,128)(2,1)}, bf16[136,1024]{1,0:T(8,128)(2,1)S(1)}, u32[]{:S(2)}) copy-start(bf16[136,1024]{1,0:T(8,128)(2,1)S(1)} %get-tuple-element.40.q_ref) | copy-start | bytes 835588
  67.3 34.1 %all-to-all-start.1 = ((bf16[16,136,256]{2,1,0:T(8,128)(2,1)}), bf16[16,136,256]{2,1,0:T(8,128)(2,1)S(1)}, u32[]{:S(2)}, u32[]{:S(2)}) async-start(bf16[16,136,256]{2,1,0:T(8,128)(2,1)} %pad_maximum_fusion), calls=%async_computation.1 | async-start | bytes 2228224 | tf_op jit(solution)/shard_map/all_to_all | solution.py:441
  74.8 35.5 %copy-start.13 = (bf16[136,1024]{1,0:T(8,128)(2,1)S(1)}, bf16[136,1024]{1,0:T(8,128)(2,1)}, u32[]{:S(2)}) copy-start(bf16[136,1024]{1,0:T(8,128)(2,1)} %copy-done.12) | copy-start | bytes 835588
  101.4 2.8 %collective-permute-start.5 = (bf16[16,136,256]{2,1,0:T(8,128)(2,1)S(1)}, bf16[16,136,256]{2,1,0:T(8,128)(2,1)S(1)}, u32[]{:S(2)}, u32[]{:S(2)}) collective-permute-start(bf16[16,136,256]{2,1,0:T(8,128)(2,1)S(1)} %all-to-all-done.1), channel_id=1, source_target_pairs={{4,0},{0,4},{12,8},{8,12},{20,16},{16,20},{28,24},{24,28},{36,32},... | collective-permute-start | bytes 3342344 | tf_op jit(solution)/shard_map/ppermute | solution.py:430
  104.2 3.6 %collective-permute-start.6 = (f32[256]{0:T(256)S(1)}, f32[256]{0:T(256)S(1)}, u32[]{:S(2)}, u32[]{:S(2)}) collective-permute-start(f32[256]{0:T(256)S(1)} %bitcast.25), channel_id=1, source_target_pairs={{1,0},{0,1},{3,2},{2,3},{5,4},{4,5},{7,6},{6,7},{9,8},{8,9},{11,10... | collective-permute-start | bytes 3080 | tf_op jit(solution)/shard_map/ppermute | solution.py:448
  107.9 12.3 %collective-permute-start.7 = (f32[256]{0:T(256)S(1)}, f32[256]{0:T(256)S(1)}, u32[]{:S(2)}, u32[]{:S(2)}) collective-permute-start(f32[256]{0:T(256)S(1)} %add.57), channel_id=1, source_target_pairs={{2,0},{3,1},{0,2},{1,3},{6,4},{7,5},{4,6},{5,7},{10,8},{11,9},{8,1... | collective-permute-start | bytes 3080 | tf_op jit(solution)/shard_map/ppermute | solution.py:448

commit v3 on v2

v3 whole, which is shorter than its diff:
```python
import math

import jax
import jax.numpy as jnp
from jax import lax
from jax.experimental import pallas as pl
from jax.experimental.pallas import tpu as pltpu
from jax.sharding import PartitionSpec as P

HD = 128
GROUP = 8
BLOCK = 128
ROWS = 256
SHARE = 132
PAD = 136
PART = ROWS // 2
WIDE = 1024
FACTOR = math.log2(math.e) / math.sqrt(HD)
LOW = -1e30
BF = jnp.bfloat16
F32 = jnp.float32


def dot(a, b):
    return jnp.dot(a, b, preferred_element_type=F32)


def dot_t(a, b):
    return lax.dot_general(a, b, (((1,), (1,)), ((), ())), preferred_element_type=F32)


def whole(shape):
    return pl.BlockSpec(shape, lambda *_: (0,) * len(shape))


def smem():
    return pl.BlockSpec(memory_space=pltpu.SMEM)


def pick_kernel(info, index_ref, hidden_ref, own_ref, send_ref):
    core, first, before, live0, live1 = (info[i] for i in range(5))
    count = live0 + live1
    start = jnp.where(core == 0, 0, 2 * SHARE - count)
    lane = lax.broadcasted_iota(jnp.int32, (PAD, ROWS), 1)
    place = lax.broadcasted_iota(jnp.int32, (PAD, ROWS), 0)
    second = lane >= BLOCK
    within = jnp.where(second, lane - BLOCK, lane)
    rank = jnp.where(second, within + live0, within)
    live = within < jnp.where(second, live1, live0)
    row = index_ref[...] + jnp.where(second, BLOCK, 0)
    column = lax.broadcasted_iota(jnp.int32, (PAD, BLOCK), 1)
    for out_ref, base in ((own_ref, SHARE * core), (send_ref, SHARE * (1 - core))):
        wanted = place + (base - start)
        match = (rank == wanted) & live & (place < SHARE)
        source = jnp.sum(jnp.where(match, (row + 1).astype(F32), 0.0), axis=1, keepdims=True)
        source = source.astype(jnp.int32) - 1
        select = jnp.where(lane == source, 1.0, 0.0).astype(BF)
        out_ref[:, : hidden_ref.shape[1]] = dot(select, hidden_ref[...]).astype(BF)
        position = jnp.where(source >= 0, source + first, 0)
        high = jnp.where(column == 0, position >> 7, 0)
        marks = jnp.where(column == 1, position & 127, high)
        out_ref[:, hidden_ref.shape[1] :] = marks.astype(F32).astype(BF)


def pick_rows(info, kept_index, hidden):
    width = hidden.shape[1] + BLOCK
    shape = jax.ShapeDtypeStruct((PAD, width), BF)
    return pl.pallas_call(
        pick_kernel,
        out_shape=(shape, shape),
        in_specs=[smem(), pl.BlockSpec(memory_space=pltpu.VMEM), pl.BlockSpec(memory_space=pltpu.VMEM)],
        out_specs=(pl.BlockSpec(memory_space=pltpu.VMEM),) * 2,
        compiler_params=pltpu.CompilerParams(vmem_limit_bytes=24 << 20),
        cost_estimate=pl.CostEstimate(
            flops=4 * PAD * ROWS * width, transcendentals=0, bytes_accessed=4 * ROWS * width
        ),
        name="pick_rows",
    )(info, kept_index.reshape(1, ROWS), hidden)


def rotated(u, cosine, sine):
    return u * cosine + pltpu.roll(u, HD // 2, 1) * sine


STEP = 1024


def project_kernel(pieces, last, blocks, *refs):
    x_refs = refs[:pieces]
    wq, wk, wv = refs[pieces : pieces + 3]
    rest = refs[pieces + 3 :]
    if last:
        q_in, kv_in, bq, bk, bv, cosine, sine, q_out, kv_out, q_acc, kv_acc = rest
    else:
        q_acc, kv_acc = rest
    step = pl.program_id(0)
    splits = pl.num_programs(0) // pieces
    for p in range(pieces):
        for part in range(splits):

            @pl.when(step == p * splits + part)
            def _(p=p, part=part):
                x = x_refs[p][:, part * STEP : (part + 1) * STEP]
                got = (dot(x, wq[...]), dot(x, wk[...]), dot(x, wv[...]))
                if p + part > 0:
                    held = (q_acc[...], kv_acc[:, :HD], kv_acc[:, HD:])
                elif last:
                    held = (q_in[...], kv_in[:, :HD], kv_in[:, HD:])
                else:
                    held = (0.0, 0.0, 0.0)
                q, k, v = (new + old for new, old in zip(got, held))
                if last and p == pieces - 1 and part == splits - 1:
                    c, s = (cosine[...], sine[...])
                    for h in range(GROUP):
                        at = slice(h * HD, (h + 1) * HD)
                        q_out[:, at] = rotated(q[:, at] + bq[:, at], c, s).astype(BF)
                    kv_out[:, :HD] = rotated(k + bk[...], c, s).astype(BF)
                    kv_out[:, HD:] = (v + bv[...]).astype(BF)
                else:
                    q_acc[...] = q
                    kv_acc[:, :HD] = k
                    kv_acc[:, HD:] = v


def project(blocks, xs, weights, extra):
    pieces = len(xs)
    last = bool(extra)
    depth = xs[0].shape[1]
    splits = depth // STEP
    columns = weights[0].shape[1]
    kind = BF if last else F32

    def weight(width):
        return pl.BlockSpec((STEP, width), lambda i, b: (b[i // splits] * splits + i % splits, 0))

    def kernel(*refs):
        project_kernel(pieces, last, *refs)

    outs = ((PAD, columns), (PAD, 2 * HD))
    spec = pltpu.PrefetchScalarGridSpec(
        num_scalar_prefetch=1,
        grid=(pieces * splits,),
        in_specs=[whole(x.shape) for x in xs]
        + [weight(w.shape[1]) for w in weights]
        + [whole(e.shape) for e in extra],
        out_specs=tuple(whole(o) for o in outs),
        scratch_shapes=[pltpu.VMEM(o, F32) for o in outs] if last else [],
    )
    weights = [pltpu.with_memory_space_constraint(w, pltpu.HBM) for w in weights]
    return pl.pallas_call(
        kernel,
        out_shape=tuple(jax.ShapeDtypeStruct(o, kind) for o in outs),
        grid_spec=spec,
        compiler_params=pltpu.CompilerParams(vmem_limit_bytes=24 << 20),
        cost_estimate=pl.CostEstimate(
            flops=2 * pieces * PAD * depth * (columns + 2 * HD),
            transcendentals=0,
            bytes_accessed=2 * pieces * depth * (columns + 2 * HD),
        ),
        name="project_rest" if last else "project_own",
    )(blocks, *xs, *weights, *extra)


def in_turn(heads, scored, weighed):
    ahead = scored(heads[0])
    for at, h in enumerate(heads):
        scores = ahead
        if at + 1 < len(heads):
            ahead = scored(heads[at + 1])
        weighed(h, scores)


def attend_kernel(info, own_ref, far_ref, mine_ref, other_ref, *refs):
    own_out, far_out, q_s, top_s, sum_s, v_s, bias_s = refs
    core = info[2]
    half = mine_ref.shape[0]
    pairs = GROUP // 2
    for g, ref in enumerate((own_ref, far_ref)):
        for h in range(GROUP):
            to = (h % 2) * PART
            q_s[g, h // 2, to : to + PART] = ref[:, h * HD : (h + 1) * HD]
    top_s[...] = jnp.full_like(top_s, LOW)
    sum_s[...] = jnp.zeros_like(sum_s)
    for p, ref in enumerate((mine_ref, other_ref)):
        v_s[p, :, :HD] = ref[:, HD:]
    v_s[:, :, HD:] = jnp.ones((2, half, HD), BF)

    def step(g, p, ref, b, bound):
        at = pl.ds(pl.multiple_of(b * WIDE, WIDE), WIDE)
        keys = ref[at, :HD]
        values = v_s[p, at, :]
        if bound is not None:
            key = lax.broadcasted_iota(jnp.int32, (PART, WIDE), 1)
            query = lax.broadcasted_iota(jnp.int32, (PART, WIDE), 0)
            bias = jnp.where(key + b * WIDE < bound[0] + bound[1] * query, 0.0, LOW)
            bias_s[:PART] = bias
            bias_s[PART:] = bias

        def scored(h):
            scores = dot_t(q_s[g, h], keys)
            return scores if bound is None else scores + bias_s[...]

        def weighed(h, scores):
            before = top_s[g, h]
            top = jnp.maximum(before, jnp.max(scores, axis=1, keepdims=True))
            top_s[g, h] = top
            weights = jnp.exp2((scores - top[:, :1]) * FACTOR).astype(BF)
            fade = jnp.exp2((before - top) * FACTOR)
            fade = jnp.concatenate([fade, fade], axis=1)
            sum_s[g, h] = sum_s[g, h] * fade + dot(weights, values)

        in_turn(range(pairs), scored, weighed)

    def group(g, carry):
        chip, side = info[2 * g + 1], info[2 * g + 2]
        for p, ref in enumerate((mine_ref, other_ref)):
            parity = core if p == 0 else 1 - core
            same = jnp.where(parity == side, 1, 0)
            before = (chip + jnp.where(parity < side, 1, 0)) * ROWS
            whole_steps = before // WIDE

            def plain(b, carry, p=p, ref=ref):
                step(g, p, ref, b, None)
                return carry

            lax.fori_loop(0, whole_steps, plain, 0)

            @pl.when((before % WIDE > 0) | (same > 0))
            def _(p=p, ref=ref):
                step(g, p, ref, whole_steps, (before + same * (PART * g + 1), same))

        return carry

    lax.fori_loop(0, 2, group, 0)
    for g, ref in enumerate((own_out, far_out)):
        for h in range(GROUP):
            total = sum_s[g, h // 2, (h % 2) * PART : (h % 2) * PART + PART]
            ref[:, h * HD : (h + 1) * HD] = (total[:, :HD] / total[:, HD:]).astype(BF)


def attend(info, own, far, mine, other):
    tokens = 2 * mine.shape[0]
    vmem = pl.BlockSpec(memory_space=pltpu.VMEM)
    out = jax.ShapeDtypeStruct(own.shape, BF)
    return pl.pallas_call(
        attend_kernel,
        out_shape=(out, out),
        in_specs=[smem(), vmem, vmem, vmem, vmem],
        out_specs=(vmem, vmem),
        scratch_shapes=[
            pltpu.VMEM((2, GROUP // 2, 2 * PART, HD), BF),
            pltpu.VMEM((2, GROUP // 2, 2 * PART, HD), F32),
            pltpu.VMEM((2, GROUP // 2, 2 * PART, 2 * HD), F32),
            pltpu.VMEM((2, tokens // 2, 2 * HD), BF),
            pltpu.VMEM((2 * PART, WIDE), F32),
        ],
        compiler_params=pltpu.CompilerParams(vmem_limit_bytes=40 << 20),
        cost_estimate=pl.CostEstimate(
            flops=4 * GROUP * PART * tokens * HD,
            transcendentals=GROUP * PART * tokens,
            bytes_accessed=4 * tokens * HD,
        ),
        name="attend2",
    )(info, own, far, mine, other)


CHUNK = 8


def text_kernel(info, text, q_ref, mine_ref, other_ref, high_ref, low_ref, out_ref):
    chip, core, low, count = (info[i] for i in range(4))
    first = (2 * chip + core) * ROWS
    half = mine_ref.shape[0]
    out_ref[...] = jnp.zeros_like(out_ref)
    rows = GROUP * CHUNK

    def chunk(c, carry):
        place = jnp.zeros((CHUNK, ROWS), jnp.int32)
        sub = lax.broadcasted_iota(jnp.int32, (CHUNK, ROWS), 0)
        for i in range(CHUNK):
            n = c * CHUNK + i
            at = text[jnp.minimum(low + n, text.shape[0] - 1)] - first
            place = jnp.where(sub == i, jnp.where(n < count, at, -1), place)
        lane = lax.broadcasted_iota(jnp.int32, (CHUNK, ROWS), 1)
        select = jnp.where(lane == place, 1.0, 0.0).astype(BF)
        picked = dot(select, q_ref[...]).astype(BF)
        queries = jnp.concatenate(
            [picked[:, h * HD : (h + 1) * HD] for h in range(GROUP)], axis=0
        )
        place = jnp.concatenate([place[:, :HD]] * GROUP, axis=0)[:, :1]
        limit = first + jnp.maximum(place, 0)
        lane = lax.broadcasted_iota(jnp.int32, (1, half), 1)
        spread = lane + (lane // ROWS) * ROWS
        parts = []
        for ref, parity in ((mine_ref, core), (other_ref, 1 - core)):
            live = spread + parity * ROWS <= limit
            parts.append(jnp.where(live, dot_t(queries, ref[:, :HD]), LOW))
        top = jnp.maximum(*(jnp.max(x, axis=1, keepdims=True) for x in parts))
        parts = [jnp.exp2((x - top) * FACTOR) for x in parts]
        total = sum(jnp.sum(x, axis=1, keepdims=True) for x in parts)
        share = jnp.where(place >= 0, 1.0 / total, 0.0)
        for p, x in enumerate(parts):
            out_ref[p : p + 1, :] += jnp.sum(x * share, axis=0, keepdims=True)
        return carry

    lax.fori_loop(0, (count + CHUNK - 1) // CHUNK, chunk, 0)
    mine, other = (out_ref[0:1, :], out_ref[1:2, :])
    even, odd = (jnp.where(core == 0, mine, other), jnp.where(core == 0, other, mine))
    for p, x in enumerate((even, odd)):
        high = x.astype(BF)
        high_ref[p : p + 1, :] = high
        low_ref[p : p + 1, :] = (x - high.astype(F32)).astype(BF)


def text_sums(info, text_rows, q2, mine, other):
    tokens = 2 * mine.shape[0]
    vmem = pl.BlockSpec(memory_space=pltpu.VMEM)
    return pl.pallas_call(
        text_kernel,
        out_shape=(jax.ShapeDtypeStruct((2, tokens // 2), BF),) * 2,
        in_specs=[smem(), smem(), vmem, vmem, vmem],
        out_specs=(vmem, vmem),
        scratch_shapes=[pltpu.VMEM((2, tokens // 2), F32)],
        compiler_params=pltpu.CompilerParams(vmem_limit_bytes=24 << 20),
        cost_estimate=pl.CostEstimate(
            flops=2 * GROUP * CHUNK * tokens * HD,
            transcendentals=GROUP * CHUNK * tokens,
            bytes_accessed=4 * tokens * HD,
        ),
        name="text_sums",
    )(info, text_rows, q2, mine, other)


def attend3_kernel(info, q_ref, mine_ref, other_ref, out_ref, v_s, bias_s):
    chip, core = info[0], info[1]
    half = mine_ref.shape[0]
    v_s[:half, :HD] = mine_ref[:, HD:]
    v_s[half:, :HD] = other_ref[:, HD:]
    v_s[:, HD:] = jnp.ones((2 * half, HD), BF)
    row = lax.broadcasted_iota(jnp.int32, (1, half), 1)
    rest = row % PAD
    live = rest < SHARE
    query = lax.broadcasted_iota(jnp.int32, (PAD, half), 0)
    start = chip * PAD
    own = (row - start <= query) & live
    bias_s[:, :half] = jnp.where(own, 0.0, LOW)
    earlier = (row < start + core * PAD) & live
    bias_s[:, half:] = jnp.where(earlier & (query >= 0), 0.0, LOW)

    def scored(h):
        q = q_ref[:, h * HD : (h + 1) * HD]
        left = dot_t(q, mine_ref[:, :HD]) + bias_s[:, :half]
        right = dot_t(q, other_ref[:, :HD]) + bias_s[:, half:]
        return left, right

    def weighed(h, scores):
        left, right = scores
        top = jnp.maximum(
            jnp.max(left, axis=1, keepdims=True), jnp.max(right, axis=1, keepdims=True)
        )
        left = jnp.exp2((left - top) * FACTOR).astype(BF)
        right = jnp.exp2((right - top) * FACTOR).astype(BF)
        total = dot(left, v_s[:half]) + dot(right, v_s[half:])
        out = (total[:, :HD] / total[:, HD:]).astype(BF)
        out_ref[:, h * HD : (h + 1) * HD] = out[:SHARE]

    in_turn(range(GROUP), scored, weighed)


def attend3(info, q3, mine, other):
    vmem = pl.BlockSpec(memory_space=pltpu.VMEM)
    keys = 2 * mine.shape[0]
    return pl.pallas_call(
        attend3_kernel,
        out_shape=jax.ShapeDtypeStruct((SHARE, q3.shape[1]), BF),
        in_specs=[smem(), vmem, vmem, vmem],
        out_specs=vmem,
        scratch_shapes=[
            pltpu.VMEM((keys, 2 * HD), BF),
            pltpu.VMEM((PAD, keys), F32),
        ],
        compiler_params=pltpu.CompilerParams(vmem_limit_bytes=40 << 20),
        cost_estimate=pl.CostEstimate(
            flops=6 * GROUP * PAD * keys * HD,
            transcendentals=GROUP * PAD * keys,
            bytes_accessed=4 * keys * HD,
        ),
        name="attend3",
    )(info, q3, mine, other)


def from_core(x):
    count = lax.axis_size("seq")
    return lax.ppermute(x, "seq", [(i ^ 1, i) for i in range(count)])


def from_head(x, distance):
    count = lax.axis_size("head")
    return lax.ppermute(x, "head", [((i + distance) % count, i) for i in range(count)])


def over_chips(many):
    count = lax.axis_size("seq")
    groups = [[i for i in range(count) if i % 2 == core] for core in range(2)]
    return lax.all_to_all(many, "seq", 0, 0, axis_index_groups=groups, tiled=True)


def over_heads(x):
    count = lax.axis_size("head")
    return [x] + [
        lax.ppermute(x, "head", [(i ^ step, i) for i in range(count)]) for step in range(1, count)
    ]


def from_partner(x):
    count = lax.axis_size("seq")
    return lax.ppermute(x, "seq", [(count - 1 - i, i) for i in range(count)])


def body(
    q2,
    k2,
    v2,
    hidden,
    w_query,
    b_query,
    w_key,
    b_key,
    w_value,
    b_value,
    kept_index,
    block_count,
    text_rows,
):
    rank = lax.axis_index("seq")
    head = lax.axis_index("head")
    seq_count = lax.axis_size("seq")
    head_count = lax.axis_size("head")
    core = rank % 2
    chip = rank // 2
    first = rank * ROWS
    depth = hidden.shape[1]

    chips = seq_count // 2
    kv2 = jnp.concatenate([k2, v2], axis=1)
    mine2 = over_chips(jnp.broadcast_to(kv2[None], (chips, *kv2.shape)))
    mine2 = mine2.reshape(-1, 2 * HD)

    numbers = jnp.stack([core, first, 0, block_count[0], block_count[1]])
    own, sent = pick_rows(numbers, kept_index, hidden)
    x = own + from_core(sent)
    marks = x[:, depth : depth + 2].astype(jnp.int32)
    positions = marks[:, 0] * 128 + marks[:, 1]
    x = x[:, :depth]
    freqs = 1000000.0 ** (-(jnp.arange(HD // 2, dtype=F32) * 2.0) / HD)
    angles = positions.astype(F32)[:, None] * freqs[None, :]
    cosine, sine = (jnp.cos(angles), jnp.sin(angles))
    cosine = jnp.concatenate([cosine, cosine], axis=1)
    sine = jnp.concatenate([-sine, sine], axis=1)

    distances = (-1, 1, 2)
    pieces = [from_head(x, d) for d in distances]
    weights = (w_query, w_key, w_value)
    partial = project(head[None].astype(jnp.int32), [x], weights, ())
    low = jnp.sum((text_rows < first).astype(jnp.int32))
    count = jnp.sum((text_rows < first + ROWS).astype(jnp.int32)) - low
    partner = seq_count - 1 - rank
    place = jnp.stack([0, chip, core, partner // 2, partner % 2])
    text_info = jnp.stack([chip, core, low, count])
    far = from_partner(q2[PART:])
    blocks = jnp.stack([(head + d) % head_count for d in distances]).astype(jnp.int32)
    biases = tuple(b[None, :] for b in (b_query, b_key, b_value))
    mine2, pieces, far, *ready = lax.optimization_barrier(
        (mine2, pieces, far, *partial, *biases, cosine, sine, place, text_info, blocks)
    )
    *ready, place, text_info, blocks = ready
    other2 = from_core(mine2)
    q3, kv3 = project(blocks, pieces, weights, ready)
    kv3, other2 = lax.optimization_barrier((kv3, other2))
    sums = text_sums(text_info, text_rows, q2, mine2, other2)

    sums = [part.reshape(2, chips, ROWS).swapaxes(0, 1) for part in sums]
    kept = jnp.broadcast_to(kv3[None, :SHARE], (chips, SHARE, 2 * HD))
    many = jnp.concatenate([kept, *sums], axis=1)
    mine = over_chips(many)
    far, many = lax.optimization_barrier((far, many))
    near, far = attend(place, q2[:PART], far, mine2, other2)
    far, mine = lax.optimization_barrier((far, mine))
    other = from_core(mine)
    far = from_partner(far)

    got = sum(jnp.sum(x[:, SHARE:].astype(F32), axis=0) for x in (mine, other))
    got = got[:2] + got[2:]
    got = over_heads(jnp.where(core == 0, got[0], got[1]))
    attn3 = attend3(place[1:3], q3, mine.reshape(-1, 2 * HD), other.reshape(-1, 2 * HD))
    attn3, far, *got = lax.optimization_barrier((attn3, far, *got))
    attn2 = jnp.concatenate([near, far], axis=0)
    tokens = seq_count * ROWS
    importance = (got[0] + got[1]) + (got[2] + got[3])
    importance = importance * (tokens / (GROUP * head_count * text_rows.shape[0]))
    return (attn2, importance, attn3)


def solution(mesh):
    placed = (
        P("seq", "head"),
        P("seq", "head"),
        P("seq", "head"),
        P("seq", "head"),
        P(None, "head"),
        P("head"),
        P(None, "head"),
        P("head"),
        P(None, "head"),
        P("head"),
        P("seq"),
        P("seq"),
        P(),
    )
    return jax.shard_map(
        body,
        mesh=mesh,
        in_specs=placed,
        out_specs=(P("seq", "head"), P("seq"), P("seq", "head")),
        check_vma=False,
    )
```

time: 121 us -> 120 us (level)
  the two profiles are of different devices: /device:TPU:6 before, /device:TPU:1 now
where the time goes in v3:
time: 120 us; the launch traced here: 119 us
  Pallas kernels  45.7 us (38%)
  starting transfers between devices  31.9 us (27%)
  waiting for transfers between devices  18.8 us (16%)
  local copies, waits for them, and re-layouts  13.4 us (11%)
  other arithmetic  6.84 us (6%)
  between operations  2.17 us (2%)
    pallas_call x1, Pallas kernels, attend(): pl.pallas_call(attend_kernel, out_shape=(out, out), in_specs=[smem(), vme...  19.4 us
    pallas_call x2, Pallas kernels, project(): pl.pallas_call(kernel, out_shape=tuple((jax.ShapeDtypeStruct(o, kind) for...  12.1 us
    all_to_all x2, starting transfers between devices, over_chips(): lax.all_to_all(many, 'seq', 0, 0, axis_index_groups=groups, tiled=True)  11.6 us
    ppermute x2, waiting for transfers between devices, from_partner(): return lax.ppermute(x, 'seq', [(count - 1 - i, i) for i in range(count)])  11 us
    unnamed x44, local copies, waits for them, and re-layouts  10.8 us
    pallas_call x1, Pallas kernels, attend3(): pl.pallas_call(attend3_kernel, out_shape=jax.ShapeDtypeStruct((SHARE, q3....  9.88 us
    ppermute x2, starting transfers between devices, from_partner(): return lax.ppermute(x, 'seq', [(count - 1 - i, i) for i in range(count)])  9.52 us
    ppermute x3, waiting for transfers between devices, from_head(): lax.ppermute(x, 'head', [((i + distance) % count, i) for i in range(count)])  7.71 us
  transfers between devices with their start and end apart: 13, of which 2 were waited for; matrix products, arithmetic and copies ran while one was open for 4% of the time, Pallas kernels for 36%

profile of v3, /device:TPU:1, one launch (start us, length us, event | category | flops | bytes accessed | tf_op | source)
XLA Modules:
  0.0 118.8 jit_solution(3523099931637107985)
XLA Ops:
  0.6 0.9 pad_maximum_fusion.2
  1.5 1.6 %broadcast_in_dim.12 = bf16[16,256,256]{2,1,0:T(8,128)(2,1)} broadcast(bf16[256,256]{1,0:T(8,128)(2,1)S(1)} %pad_maximum_fusion.2), dimensions={1,2} | broadcast | bytes 2228224 | tf_op jit(solution)/shard_map/broadcast_in_dim | solution.py:446
  3.1 7.7 %all-to-all-start = ((bf16[16,256,256]{2,1,0:T(8,128)(2,1)}), bf16[16,256,256]{2,1,0:T(8,128)(2,1)S(1)}, u32[]{:S(2)}, u32[]{:S(2)}) async-start(bf16[16,256,256]{2,1,0:T(8,128)(2,1)} %broadcast_in_dim.12), calls=%async_computation | async-start | bytes 4194304 | tf_op jit(solution)/shard_map/all_to_all | solution.py:405
  10.8 0.0 copy-start.13
  10.8 0.1 pad_add_fusion.info
  10.9 1.2 %copy-done.16 = bf16[256,2048]{1,0:T(8,128)(2,1)S(1)} copy-done((bf16[256,2048]{1,0:T(8,128)(2,1)S(1)}, bf16[256,2048]{1,0:T(8,128)(2,1)}, u32[]{:S(2)}) %copy-start.16) | copy-done | bytes 1048600
  12.1 1.9 %pick_rows.1 = (bf16[136,2176]{1,0:T(8,128)(2,1)S(1)}, bf16[136,2176]{1,0:T(8,128)(2,1)}) custom-call(s32[5]{0:T(128)S(1)} %pad_add_fusion.info, s32[1,256]{1,0:T(1,128)S(1)} %bitcast.37, bf16[256,2048]{1,0:T(8,128)(2,1)S(1)} %copy-done.16), custom_call_target="tpu_custom_call" | custom-call | flops 303038464 | bytes 2228224 | tf_op jit(solution)/shard_map/pick_rows/pallas_call | solution.py:68
  14.1 1.0 collective-permute-start
  15.0 0.8 fusion.5
  15.9 4.9 %collective-permute-start.4 = (bf16[128,1024]{1,0:T(8,128)(2,1)}, bf16[128,1024]{1,0:T(8,128)(2,1)}, u32[]{:S(2)}, u32[]{:S(2)}) collective-permute-start(bf16[128,1024]{1,0:T(8,128)(2,1)} %get-tuple-element.78), channel_id=1, source_target_pairs={{124,0},{120,4},{116,8},{112,12},{108,16},{104,20},{100,24},{96,28... | collective-permute-start | bytes 786440 | tf_op jit(solution)/shard_map/ppermute | solution.py:417
  20.7 0.7 fusion.3
  22.6 0.1 stack.51.info
  22.7 0.7 pad_add_fusion.1.info
  23.4 0.1 pad_add_fusion.2.refs_0_
  23.5 0.0 collective-permute-done
  23.5 1.2 %add.53 = bf16[136,2176]{1,0:T(8,128)(2,1)S(1)} add(bf16[136,2176]{1,0:T(8,128)(2,1)S(1)} %get-tuple-element.39, bf16[136,2176]{1,0:T(8,128)(2,1)} %collective-permute-done) | non-fusion elementwise | flops 295936 | bytes 1775616 | tf_op jit(solution)/shard_map/add | solution.py:451
  24.8 3.7 %collective-permute-start.3 = (bf16[136,2048]{1,0:T(8,128)(2,1)S(1)}, bf16[136,2048]{1,0:T(8,128)(2,1)S(1)}, u32[]{:S(2)}, u32[]{:S(2)}) collective-permute-start(bf16[136,2048]{1,0:T(8,128)(2,1)S(1)} %slice.59.refs_1_), channel_id=1, source_target_pairs={{2,0},{3,1},{0,2},{1,3},{6,4},{7,5},{4,6},{5,7},{10,8},{11,9},{8,1... | collective-permute-start | bytes 1671176 | tf_op jit(solution)/shard_map/ppermute | solution.py:399
  28.4 0.4 collective-permute-start.2
  28.9 1.0 collective-permute-start.1
  29.9 0.2 fusion.1
  30.1 0.3 fusion.2
  30.4 0.0 copy-start.12
  30.4 0.0 copy-start.14
  30.5 0.0 copy-start.15
  30.5 3.2 %project_own.1 = (f32[136,1024]{1,0:T(8,128)S(1)}, f32[136,256]{1,0:T(8,128)S(1)}) custom-call(s32[1]{0:T(128)} %bitcast.4.refs_0_, bf16[136,2048]{1,0:T(8,128)(2,1)S(1)} %slice.59.refs_1_, bf16[8192,1024]{1,0:T(8,128)(2,1)} %refs_4_.3, bf16[8192,128]{1,0:T(8,128)(2,1)} %refs_5_.1, bf16[8192,128]{1,0:T(8,128)(2,1)} %refs_6_.1), custom_call_target="tpu_custom_call" | custom-call | flops 713031680 | bytes 5242880 | tf_op jit(solution)/shard_map/project_own/pallas_call | solution.py:150
  33.7 0.8 copy-done.7
  34.5 0.1 pad_maximum_fusion.3
  34.6 11.0 %collective-permute-done.4.far_ref = bf16[128,1024]{1,0:T(8,128)(2,1)} collective-permute-done((bf16[128,1024]{1,0:T(8,128)(2,1)}, bf16[128,1024]{1,0:T(8,128)(2,1)}, u32[]{:S(2)}, u32[]{:S(2)}) %collective-permute-start.4) | collective-permute-done | bytes 262176 | tf_op jit(solution)/shard_map/ppermute | solution.py:417
  45.7 0.0 collective-permute-done.3.refs_3_
  45.7 7.7 %collective-permute-done.2.refs_2_ = bf16[136,2048]{1,0:T(8,128)(2,1)S(1)} collective-permute-done((bf16[136,2048]{1,0:T(8,128)(2,1)S(1)}, bf16[136,2048]{1,0:T(8,128)(2,1)S(1)}, u32[]{:S(2)}, u32[]{:S(2)}) %collective-permute-start.2) | collective-permute-done | bytes 557088 | tf_op jit(solution)/shard_map/ppermute | solution.py:399
  53.4 0.8 copy-done.3
  54.2 0.0 collective-permute-done.1.refs_1_
  54.2 0.8 copy-done.5
  55.0 0.0 all-to-all-done
  55.0 1.4 %collective-permute-start.5 = (bf16[4096,256]{1,0:T(8,128)(2,1)S(1)}, bf16[4096,256]{1,0:T(8,128)(2,1)S(1)}, u32[]{:S(2)}, u32[]{:S(2)}) collective-permute-start(bf16[4096,256]{1,0:T(8,128)(2,1)S(1)} %bitcast.26), channel_id=1, source_target_pairs={{4,0},{0,4},{12,8},{8,12},{20,16},{16,20},{28,24},{24,28},{36,32},... | collective-permute-start | bytes 6291464 | tf_op jit(solution)/shard_map/ppermute | solution.py:394
  56.4 1.0 copy-done.4
  57.4 1.1 copy-done.6
  58.5 1.1 copy-done.8
  59.5 8.9 %project_rest.1 = (bf16[136,1024]{1,0:T(8,128)(2,1)S(1)}, bf16[136,256]{1,0:T(8,128)(2,1)S(1)}) custom-call(s32[3]{0:T(128)S(1)} %pad_add_fusion.2.refs_0_, bf16[136,2048]{1,0:T(8,128)(2,1)S(1)} %copy-done.6, bf16[136,2048]{1,0:T(8,128)(2,1)S(1)} %copy-done.4, bf16[136,2048]{1,0:T(8,128)(2,1)S(1)} %collective-permute-done.3.refs_3_, ...), custom_call_target="tpu_custom_call" | custom-call | flops 2139095040 | bytes 15728640 | tf_op jit(solution)/shard_map/project_rest/pallas_call | solution.py:150
  68.4 0.0 copy-start.17
  68.4 0.0 collective-permute-done.5.other_ref
  68.4 2.4 %text_sums.1 = (bf16[2,4096]{1,0:T(2,128)(2,1)S(1)}, bf16[2,4096]{1,0:T(2,128)(2,1)S(1)}) custom-call(s32[4]{0:T(128)S(1)} %pad_add_fusion.1.info, s32[256]{0:T(256)S(1)} %copy-done.13, bf16[256,1024]{1,0:T(8,128)(2,1)S(1)} %copy-done.2, bf16[4096,256]{1,0:T(8,128)(2,1)S(1)} %bitcast.27, bf16[4096,256]{1,0:T(8,128)(2,1)S(1)} %collective-permute-done.5.other_ref), custom_call_target="tpu_custom_call" | custom-call | flops 134217728 | bytes 4194304 | tf_op jit(solution)/shard_map/text_sums/pallas_call | solution.py:318
  70.9 0.1 broadcast_in_dim.31
  71.0 0.0 copy-start.9
  71.0 1.1 pad_maximum_fusion
  72.1 3.9 %all-to-all-start.1 = ((bf16[16,136,256]{2,1,0:T(8,128)(2,1)}), bf16[16,136,256]{2,1,0:T(8,128)(2,1)S(1)}, u32[]{:S(2)}, u32[]{:S(2)}) async-start(bf16[16,136,256]{2,1,0:T(8,128)(2,1)} %pad_maximum_fusion), calls=%async_computation.1 | async-start | bytes 2228224 | tf_op jit(solution)/shard_map/all_to_all | solution.py:405
  76.0 1.6 %copy-done.1 = bf16[4096,256]{1,0:T(8,128)(2,1)S(1)} copy-done((bf16[4096,256]{1,0:T(8,128)(2,1)S(1)}, bf16[4096,256]{1,0:T(8,128)(2,1)}, u32[]{:S(2)}) %copy-start.1) | copy-done | bytes 2097176
  77.6 19.4 %attend2.1 = (bf16[128,1024]{1,0:T(8,128)(2,1)S(1)}, bf16[128,1024]{1,0:T(8,128)(2,1)S(1)}) custom-call(s32[5]{0:T(128)S(1)} %stack.51.info, bf16[128,1024]{1,0:T(8,128)(2,1)S(1)} %copy-done.9, bf16[128,1024]{1,0:T(8,128)(2,1)} %collective-permute-done.4.far_ref, bf16[4096,256]{1,0:T(8,128)(2,1)S(1)} %bitcast.28, bf16[4096,256]{1,0:T(8,128)(2,1)S(1)} %copy-done.1), custom_call_target="tpu_custom_call" | custom-call | flops 4294967296 | bytes 4194304 | tf_op jit(solution)/shard_map/attend2/pallas_call | solution.py:245
  97.0 0.7 copy-done.10
  97.7 0.7 copy-done.19
  98.4 0.0 all-to-all-done.1
  98.4 0.0 collective-permute-start.6
  98.4 0.1 slice.52.info
  98.4 4.7 %collective-permute-start.7 = (bf16[128,1024]{1,0:T(8,128)(2,1)}, bf16[128,1024]{1,0:T(8,128)(2,1)S(1)}, u32[]{:S(2)}, u32[]{:S(2)}) collective-permute-start(bf16[128,1024]{1,0:T(8,128)(2,1)} %copy-done.19), channel_id=1, source_target_pairs={{124,0},{120,4},{116,8},{112,12},{108,16},{104,20},{100,24},{96,28... | collective-permute-start | bytes 786440 | tf_op jit(solution)/shard_map/ppermute | solution.py:417
  103.1 0.0 collective-permute-done.6
  103.2 2.4 %collective-permute-start.10 = (f32[256]{0:T(256)S(1)}, f32[256]{0:T(256)S(1)}, u32[]{:S(2)}, u32[]{:S(2)}) collective-permute-start(f32[256]{0:T(256)S(1)} %bitcast.38), channel_id=1, source_target_pairs={{3,0},{2,1},{1,2},{0,3},{7,4},{6,5},{5,6},{4,7},{11,8},{10,9},{9,1... | collective-permute-start | bytes 3080 | tf_op jit(solution)/shard_map/ppermute | solution.py:411
  105.6 0.9 collective-permute-start.8
  106.6 1.0 copy-done.18
  107.5 9.9 %attend3.1 = bf16[132,1024]{1,0:T(8,128)(2,1)} custom-call(s32[2]{0:T(128)S(1)} %slice.52.info, bf16[136,1024]{1,0:T(8,128)(2,1)S(1)} %copy-done.18, bf16[2176,256]{1,0:T(8,128)(2,1)S(1)} %bitcast.29, bf16[2176,256]{1,0:T(8,128)(2,1)S(1)} %bitcast.34), custom_call_target="tpu_custom_call" | custom-call | flops 3636461568 | bytes 2228224 | tf_op jit(solution)/shard_map/attend3/pallas_call | solution.py:373
  117.4 0.0 collective-permute-done.7
  117.4 0.0 collective-permute-done.10
  117.4 0.0 collective-permute-done.9
  117.4 0.8 pad_maximum_fusion.1
  118.3 0.6 add_add_fusion
  (37 shorter events, 0.2 us)
Async XLA Ops:
  3.1 7.8 %copy-start.21 = (s32[2]{0:T(128)S(1)}, s32[2]{0:T(128)}, u32[]{:S(2)}) copy-start(s32[2]{0:T(128)} %param.24) | copy-start | bytes 28
  3.1 7.8 %copy-start.20 = (s32[256]{0:T(256)S(1)}, s32[256]{0:T(256)}, u32[]{:S(2)}) copy-start(s32[256]{0:T(256)} %param.23) | copy-start | bytes 3076
  3.1 12.0 %copy-start.2 = (bf16[256,1024]{1,0:T(8,128)(2,1)S(1)}, bf16[256,1024]{1,0:T(8,128)(2,1)}, u32[]{:S(2)}) copy-start(bf16[256,1024]{1,0:T(8,128)(2,1)} %q_ref.1) | copy-start | bytes 1572868
  3.1 51.9 %all-to-all-start = ((bf16[16,256,256]{2,1,0:T(8,128)(2,1)}), bf16[16,256,256]{2,1,0:T(8,128)(2,1)S(1)}, u32[]{:S(2)}, u32[]{:S(2)}) async-start(bf16[16,256,256]{2,1,0:T(8,128)(2,1)} %broadcast_in_dim.12), calls=%async_computation | async-start | bytes 4194304 | tf_op jit(solution)/shard_map/all_to_all | solution.py:405
  10.8 9.9 %copy-start.13 = (s32[256]{0:T(256)S(1)}, s32[256]{0:T(256)}, u32[]{:S(2)}) copy-start(s32[256]{0:T(256)} %text.1) | copy-start | bytes 3076
  10.9 1.2 %copy-start.16 = (bf16[256,2048]{1,0:T(8,128)(2,1)S(1)}, bf16[256,2048]{1,0:T(8,128)(2,1)}, u32[]{:S(2)}) copy-start(bf16[256,2048]{1,0:T(8,128)(2,1)} %hidden_ref.1) | copy-start | bytes 3145732
  14.1 9.4 %collective-permute-start = (bf16[136,2176]{1,0:T(8,128)(2,1)}, bf16[136,2176]{1,0:T(8,128)(2,1)}, u32[]{:S(2)}, u32[]{:S(2)}) collective-permute-start(bf16[136,2176]{1,0:T(8,128)(2,1)} %get-tuple-element.40), channel_id=1, source_target_pairs={{4,0},{0,4},{12,8},{8,12},{20,16},{16,20},{28,24},{24,28},{36,32},... | collective-permute-start | bytes 1775624 | tf_op jit(solution)/shard_map/ppermute | solution.py:394
  15.9 29.8 %collective-permute-start.4 = (bf16[128,1024]{1,0:T(8,128)(2,1)}, bf16[128,1024]{1,0:T(8,128)(2,1)}, u32[]{:S(2)}, u32[]{:S(2)}) collective-permute-start(bf16[128,1024]{1,0:T(8,128)(2,1)} %get-tuple-element.78), channel_id=1, source_target_pairs={{124,0},{120,4},{116,8},{112,12},{108,16},{104,20},{100,24},{96,28... | collective-permute-start | bytes 786440 | tf_op jit(solution)/shard_map/ppermute | solution.py:417
  24.8 20.9 %collective-permute-start.3 = (bf16[136,2048]{1,0:T(8,128)(2,1)S(1)}, bf16[136,2048]{1,0:T(8,128)(2,1)S(1)}, u32[]{:S(2)}, u32[]{:S(2)}) collective-permute-start(bf16[136,2048]{1,0:T(8,128)(2,1)S(1)} %slice.59.refs_1_), channel_id=1, source_target_pairs={{2,0},{3,1},{0,2},{1,3},{6,4},{7,5},{4,6},{5,7},{10,8},{11,9},{8,1... | collective-permute-start | bytes 1671176 | tf_op jit(solution)/shard_map/ppermute | solution.py:399
  28.4 24.9 %collective-permute-start.2 = (bf16[136,2048]{1,0:T(8,128)(2,1)S(1)}, bf16[136,2048]{1,0:T(8,128)(2,1)S(1)}, u32[]{:S(2)}, u32[]{:S(2)}) collective-permute-start(bf16[136,2048]{1,0:T(8,128)(2,1)S(1)} %slice.59.refs_1_), channel_id=1, source_target_pairs={{1,0},{2,1},{3,2},{0,3},{5,4},{6,5},{7,6},{4,7},{9,8},{10,9},{11,1... | collective-permute-start | bytes 1671176 | tf_op jit(solution)/shard_map/ppermute | solution.py:399
  28.9 25.3 %collective-permute-start.1 = (bf16[136,2048]{1,0:T(8,128)(2,1)S(1)}, bf16[136,2048]{1,0:T(8,128)(2,1)S(1)}, u32[]{:S(2)}, u32[]{:S(2)}) collective-permute-start(bf16[136,2048]{1,0:T(8,128)(2,1)S(1)} %slice.59.refs_1_), channel_id=1, source_target_pairs={{3,0},{0,1},{1,2},{2,3},{7,4},{4,5},{5,6},{6,7},{11,8},{8,9},{9,10... | collective-permute-start | bytes 1671176 | tf_op jit(solution)/shard_map/ppermute | solution.py:399
  30.4 25.9 %copy-start.12 = (f32[1024]{0:T(1024)S(1)}, f32[1024]{0:T(1024)}, u32[]{:S(2)}) copy-start(f32[1024]{0:T(1024)} %param.18) | copy-start | bytes 12292
  30.4 25.9 %copy-start.14 = (f32[128]{0:T(128)S(1)}, f32[128]{0:T(128)}, u32[]{:S(2)}) copy-start(f32[128]{0:T(128)} %param.20) | copy-start | bytes 1540
  30.5 25.9 %copy-start.15 = (f32[128]{0:T(128)S(1)}, f32[128]{0:T(128)}, u32[]{:S(2)}) copy-start(f32[128]{0:T(128)} %param.22) | copy-start | bytes 1540
  33.7 0.8 copy-start.7
  53.4 0.8 copy-start.3
  54.2 0.8 copy-start.5
  55.0 13.4 %collective-permute-start.5 = (bf16[4096,256]{1,0:T(8,128)(2,1)S(1)}, bf16[4096,256]{1,0:T(8,128)(2,1)S(1)}, u32[]{:S(2)}, u32[]{:S(2)}) collective-permute-start(bf16[4096,256]{1,0:T(8,128)(2,1)S(1)} %bitcast.26), channel_id=1, source_target_pairs={{4,0},{0,4},{12,8},{8,12},{20,16},{16,20},{28,24},{24,28},{36,32},... | collective-permute-start | bytes 6291464 | tf_op jit(solution)/shard_map/ppermute | solution.py:394
  56.4 1.1 copy-start.4
  57.4 1.1 copy-start.6
  58.5 1.1 copy-start.8
  68.4 2.5 %copy-start.17 = (bf16[136,1024]{1,0:T(8,128)(2,1)}, bf16[136,1024]{1,0:T(8,128)(2,1)S(1)}, u32[]{:S(2)}) copy-start(bf16[136,1024]{1,0:T(8,128)(2,1)S(1)} %get-tuple-element.65.q_ref) | copy-start | bytes 835588
  68.4 2.5 %copy-start = (bf16[4096,256]{1,0:T(8,128)(2,1)}, bf16[4096,256]{1,0:T(8,128)(2,1)S(1)}, u32[]{:S(2)}) copy-start(bf16[4096,256]{1,0:T(8,128)(2,1)S(1)} %collective-permute-done.5.other_ref) | copy-start | bytes 6291460
  71.0 5.0 %copy-start.9 = (bf16[128,1024]{1,0:T(8,128)(2,1)S(1)}, bf16[128,1024]{1,0:T(8,128)(2,1)}, u32[]{:S(2)}) copy-start(bf16[128,1024]{1,0:T(8,128)(2,1)} %get-tuple-element.77.own_ref) | copy-start | bytes 786436
  72.1 26.3 %all-to-all-start.1 = ((bf16[16,136,256]{2,1,0:T(8,128)(2,1)}), bf16[16,136,256]{2,1,0:T(8,128)(2,1)S(1)}, u32[]{:S(2)}, u32[]{:S(2)}) async-start(bf16[16,136,256]{2,1,0:T(8,128)(2,1)} %pad_maximum_fusion), calls=%async_computation.1 | async-start | bytes 2228224 | tf_op jit(solution)/shard_map/all_to_all | solution.py:405
  76.0 1.6 %copy-start.1 = (bf16[4096,256]{1,0:T(8,128)(2,1)S(1)}, bf16[4096,256]{1,0:T(8,128)(2,1)}, u32[]{:S(2)}) copy-start(bf16[4096,256]{1,0:T(8,128)(2,1)} %copy-done) | copy-start | bytes 6291460
  97.0 0.7 copy-start.10
  97.7 0.7 copy-start.19
  98.4 4.8 %collective-permute-start.6 = (bf16[16,136,256]{2,1,0:T(8,128)(2,1)S(1)}, bf16[16,136,256]{2,1,0:T(8,128)(2,1)S(1)}, u32[]{:S(2)}, u32[]{:S(2)}) collective-permute-start(bf16[16,136,256]{2,1,0:T(8,128)(2,1)S(1)} %all-to-all-done.1), channel_id=1, source_target_pairs={{4,0},{0,4},{12,8},{8,12},{20,16},{16,20},{28,24},{24,28},{36,32},... | collective-permute-start | bytes 3342344 | tf_op jit(solution)/shard_map/ppermute | solution.py:394
  98.4 19.0 %collective-permute-start.7 = (bf16[128,1024]{1,0:T(8,128)(2,1)}, bf16[128,1024]{1,0:T(8,128)(2,1)S(1)}, u32[]{:S(2)}, u32[]{:S(2)}) collective-permute-start(bf16[128,1024]{1,0:T(8,128)(2,1)} %copy-done.19), channel_id=1, source_target_pairs={{124,0},{120,4},{116,8},{112,12},{108,16},{104,20},{100,24},{96,28... | collective-permute-start | bytes 786440 | tf_op jit(solution)/shard_map/ppermute | solution.py:417
  103.2 14.2 %collective-permute-start.10 = (f32[256]{0:T(256)S(1)}, f32[256]{0:T(256)S(1)}, u32[]{:S(2)}, u32[]{:S(2)}) collective-permute-start(f32[256]{0:T(256)S(1)} %bitcast.38), channel_id=1, source_target_pairs={{3,0},{2,1},{1,2},{0,3},{7,4},{6,5},{5,6},{4,7},{11,8},{10,9},{9,1... | collective-permute-start | bytes 3080 | tf_op jit(solution)/shard_map/ppermute | solution.py:411
  105.6 11.8 %collective-permute-start.9 = (f32[256]{0:T(256)S(1)}, f32[256]{0:T(256)S(1)}, u32[]{:S(2)}, u32[]{:S(2)}) collective-permute-start(f32[256]{0:T(256)S(1)} %bitcast.39), channel_id=1, source_target_pairs={{2,0},{3,1},{0,2},{1,3},{6,4},{7,5},{4,6},{5,7},{10,8},{11,9},{8,1... | collective-permute-start | bytes 3080 | tf_op jit(solution)/shard_map/ppermute | solution.py:411
  105.6 11.8 %collective-permute-start.8 = (f32[256]{0:T(256)S(1)}, f32[256]{0:T(256)S(1)}, u32[]{:S(2)}, u32[]{:S(2)}) collective-permute-start(f32[256]{0:T(256)S(1)} %bitcast.40), channel_id=1, source_target_pairs={{1,0},{0,1},{3,2},{2,3},{5,4},{4,5},{7,6},{6,7},{9,8},{8,9},{11,10... | collective-permute-start | bytes 3080 | tf_op jit(solution)/shard_map/ppermute | solution.py:411
  106.6 1.0 copy-start.18
  107.5 9.9 %copy-start.11 = (bf16[128,1024]{1,0:T(8,128)(2,1)S(1)}, bf16[128,1024]{1,0:T(8,128)(2,1)}, u32[]{:S(2)}) copy-start(bf16[128,1024]{1,0:T(8,128)(2,1)} %copy-done.10) | copy-start | bytes 786436

commit v4 on v3

--- a/solution.py
+++ b/solution.py
@@ -70,7 +70,7 @@
         out_shape=(shape, shape),
         in_specs=[smem(), pl.BlockSpec(memory_space=pltpu.VMEM), pl.BlockSpec(memory_space=pltpu.VMEM)],
         out_specs=(pl.BlockSpec(memory_space=pltpu.VMEM),) * 2,
-        compiler_params=pltpu.CompilerParams(vmem_limit_bytes=24 << 20),
+        compiler_params=pltpu.CompilerParams(vmem_limit_bytes=16 << 20),
         cost_estimate=pl.CostEstimate(
             flops=4 * PAD * ROWS * width, transcendentals=0, bytes_accessed=4 * ROWS * width
         ),
@@ -85,80 +85,117 @@
 STEP = 1024
 
 
-def project_kernel(pieces, last, blocks, *refs):
+def project_kernel(pieces, first, last, blocks, *refs):
     x_refs = refs[:pieces]
-    wq, wk, wv = refs[pieces : pieces + 3]
+    weights = refs[pieces : pieces + 3]
     rest = refs[pieces + 3 :]
+    if not first:
+        before = rest[:2]
+        rest = rest[2:]
     if last:
-        q_in, kv_in, bq, bk, bv, cosine, sine, q_out, kv_out, q_acc, kv_acc = rest
+        bq, bk, bv, cosine, sine = rest[:5]
+        rest = rest[5:]
+    q_to, kv_out, *held, kv_s, q_s, q_out, sems, part_sems = rest
+    sums = (q_s, kv_s)
+    loads = []
+    if not first:
+        loads = [
+            pltpu.make_async_copy(x, to, part_sems.at[i])
+            for i, (x, to) in enumerate(zip(before, sums))
+        ]
+    depth = x_refs[0].shape[1]
+    copies = []
+    for p in range(pieces):
+        for part in range(depth // STEP):
+            at = len(copies) * STEP
+            start = pl.multiple_of(blocks[p] * depth + part * STEP, STEP)
+            copies.append(
+                [
+                    pltpu.make_async_copy(
+                        w.at[pl.ds(start, STEP), :], to.at[at : at + STEP, :], sems.at[len(copies), i]
+                    )
+                    for i, (w, to) in enumerate(zip(weights, held))
+                ]
+            )
+    for group in [*copies, loads]:
+        for copy in group:
+            copy.start()
+    totals = [0.0, 0.0, 0.0]
+    for n, group in enumerate(copies):
+        p, part = divmod(n, depth // STEP)
+        x = x_refs[p][:, part * STEP : (part + 1) * STEP]
+        for copy in group:
+            copy.wait()
+        at = slice(n * STEP, (n + 1) * STEP)
+        totals = [old + dot(x, w[at, :]) for old, w in zip(totals, held)]
+    for copy in loads:
+        copy.wait()
+    q, k, v = totals
+    if not first:
+        q, k, v = (q + q_s[...], k + kv_s[:, :HD], v + kv_s[:, HD:])
+    if last:
+        c, s = (cosine[...], sine[...])
+        for h in range(GROUP):
+            at = slice(h * HD, (h + 1) * HD)
+            q_out[:, at] = rotated(q[:, at] + bq[:, at], c, s).astype(BF)
+        kv_out[:, :HD] = rotated(k + bk[...], c, s).astype(BF)
+        kv_out[:, HD:] = (v + bv[...]).astype(BF)
+        stores = [pltpu.make_async_copy(q_out, q_to, part_sems.at[2])]
     else:
-        q_acc, kv_acc = rest
-    step = pl.program_id(0)
-    splits = pl.num_programs(0) // pieces
-    for p in range(pieces):
-        for part in range(splits):
-
-            @pl.when(step == p * splits + part)
-            def _(p=p, part=part):
-                x = x_refs[p][:, part * STEP : (part + 1) * STEP]
-                got = (dot(x, wq[...]), dot(x, wk[...]), dot(x, wv[...]))
-                if p + part > 0:
-                    held = (q_acc[...], kv_acc[:, :HD], kv_acc[:, HD:])
-                elif last:
-                    held = (q_in[...], kv_in[:, :HD], kv_in[:, HD:])
-                else:
-                    held = (0.0, 0.0, 0.0)
-                q, k, v = (new + old for new, old in zip(got, held))
-                if last and p == pieces - 1 and part == splits - 1:
-                    c, s = (cosine[...], sine[...])
-                    for h in range(GROUP):
-                        at = slice(h * HD, (h + 1) * HD)
-                        q_out[:, at] = rotated(q[:, at] + bq[:, at], c, s).astype(BF)
-                    kv_out[:, :HD] = rotated(k + bk[...], c, s).astype(BF)
-                    kv_out[:, HD:] = (v + bv[...]).astype(BF)
-                else:
-                    q_acc[...] = q
-                    kv_acc[:, :HD] = k
-                    kv_acc[:, HD:] = v
-
-
-def project(blocks, xs, weights, extra):
+        q_out[...] = q
+        kv_s[:, :HD] = k
+        kv_s[:, HD:] = v
+        stores = [
+            pltpu.make_async_copy(q_out, q_to, part_sems.at[2]),
+            pltpu.make_async_copy(kv_s, kv_out, part_sems.at[3]),
+        ]
+    for copy in stores:
+        copy.start()
+    for copy in stores:
+        copy.wait()
+
+
+def project(blocks, xs, weights, partial=(), finish=()):
     pieces = len(xs)
-    last = bool(extra)
     depth = xs[0].shape[1]
-    splits = depth // STEP
-    columns = weights[0].shape[1]
-    kind = BF if last else F32
-
-    def weight(width):
-        return pl.BlockSpec((STEP, width), lambda i, b: (b[i // splits] * splits + i % splits, 0))
+    widths = [w.shape[1] for w in weights]
+    kind = BF if finish else F32
+    vmem = pl.BlockSpec(memory_space=pltpu.VMEM)
+    weights = [pltpu.with_memory_space_constraint(w, pltpu.HBM) for w in weights]
+    hbm = pl.BlockSpec(memory_space=pl.ANY)
+    partial = [pltpu.with_memory_space_constraint(part, pltpu.HBM) for part in partial]
 
     def kernel(*refs):
-        project_kernel(pieces, last, *refs)
-
-    outs = ((PAD, columns), (PAD, 2 * HD))
-    spec = pltpu.PrefetchScalarGridSpec(
-        num_scalar_prefetch=1,
-        grid=(pieces * splits,),
-        in_specs=[whole(x.shape) for x in xs]
-        + [weight(w.shape[1]) for w in weights]
-        + [whole(e.shape) for e in extra],
-        out_specs=tuple(whole(o) for o in outs),
-        scratch_shapes=[pltpu.VMEM(o, F32) for o in outs] if last else [],
-    )
-    weights = [pltpu.with_memory_space_constraint(w, pltpu.HBM) for w in weights]
+        project_kernel(pieces, not partial, bool(finish), *refs)
+
+    outs = ((PAD, widths[0]), (PAD, 2 * HD))
     return pl.pallas_call(
         kernel,
-        out_shape=tuple(jax.ShapeDtypeStruct(o, kind) for o in outs),
-        grid_spec=spec,
-        compiler_params=pltpu.CompilerParams(vmem_limit_bytes=24 << 20),
+        out_shape=(
+            pltpu.HBM(outs[0], kind),
+            jax.ShapeDtypeStruct(outs[1], kind) if finish else pltpu.HBM(outs[1], kind),
+        ),
+        in_specs=[smem()]
+        + [vmem] * pieces
+        + [hbm] * (3 + len(partial))
+        + [vmem] * len(finish),
+        out_specs=(hbm, vmem if finish else hbm),
+        scratch_shapes=[pltpu.VMEM((pieces * depth, width), BF) for width in widths]
+        + [
+            pltpu.VMEM(outs[1], F32),
+            pltpu.VMEM(outs[0], F32),
+            pltpu.VMEM(outs[0], kind),
+            pltpu.SemaphoreType.DMA((pieces * depth // STEP, 3)),
+            pltpu.SemaphoreType.DMA((4,)),
+        ],
+        compiler_params=pltpu.CompilerParams(vmem_limit_bytes=28 << 20),
         cost_estimate=pl.CostEstimate(
-            flops=2 * pieces * PAD * depth * (columns + 2 * HD),
+            flops=2 * pieces * PAD * depth * sum(widths),
             transcendentals=0,
-            bytes_accessed=2 * pieces * depth * (columns + 2 * HD),
+            bytes_accessed=2 * pieces * depth * sum(widths),
         ),
-        name="project_rest" if last else "project_own",
-    )(blocks, *xs, *weights, *extra)
+        name="project",
+    )(blocks, *xs, *weights, *partial, *finish)
 
 
 def in_turn(heads, scored, weighed):
@@ -171,7 +208,9 @@
 
 
 def attend_kernel(info, own_ref, far_ref, mine_ref, other_ref, *refs):
-    own_out, far_out, q_s, top_s, sum_s, v_s, bias_s = refs
+    own_to, far_to, q_s, top_s, sum_s, v_s, bias_s, other_s, own_out, far_out, sems = refs
+    fetch = pltpu.make_async_copy(other_ref, other_s, sems.at[0])
+    fetch.start()
     core = info[2]
     half = mine_ref.shape[0]
     pairs = GROUP // 2
@@ -181,9 +220,10 @@
             q_s[g, h // 2, to : to + PART] = ref[:, h * HD : (h + 1) * HD]
     top_s[...] = jnp.full_like(top_s, LOW)
     sum_s[...] = jnp.zeros_like(sum_s)
-    for p, ref in enumerate((mine_ref, other_ref)):
-        v_s[p, :, :HD] = ref[:, HD:]
+    v_s[0, :, :HD] = mine_ref[:, HD:]
     v_s[:, :, HD:] = jnp.ones((2, half, HD), BF)
+    fetch.wait()
+    v_s[1, :, :HD] = other_s[:, HD:]
 
     def step(g, p, ref, b, bound):
         at = pl.ds(pl.multiple_of(b * WIDE, WIDE), WIDE)
@@ -213,7 +253,7 @@
 
     def group(g, carry):
         chip, side = info[2 * g + 1], info[2 * g + 2]
-        for p, ref in enumerate((mine_ref, other_ref)):
+        for p, ref in enumerate((mine_ref, other_s)):
             parity = core if p == 0 else 1 - core
             same = jnp.where(parity == side, 1, 0)
             before = (chip + jnp.where(parity < side, 1, 0)) * ROWS
@@ -236,25 +276,39 @@
         for h in range(GROUP):
             total = sum_s[g, h // 2, (h % 2) * PART : (h % 2) * PART + PART]
             ref[:, h * HD : (h + 1) * HD] = (total[:, :HD] / total[:, HD:]).astype(BF)
+    stores = [
+        pltpu.make_async_copy(own_out, own_to, sems.at[1]),
+        pltpu.make_async_copy(far_out, far_to, sems.at[2]),
+    ]
+    for copy in stores:
+        copy.start()
+    for copy in stores:
+        copy.wait()
 
 
 def attend(info, own, far, mine, other):
     tokens = 2 * mine.shape[0]
     vmem = pl.BlockSpec(memory_space=pltpu.VMEM)
-    out = jax.ShapeDtypeStruct(own.shape, BF)
+    hbm = pl.BlockSpec(memory_space=pl.ANY)
+    other = pltpu.with_memory_space_constraint(other, pltpu.HBM)
+    out = pltpu.HBM(own.shape, BF)
     return pl.pallas_call(
         attend_kernel,
         out_shape=(out, out),
-        in_specs=[smem(), vmem, vmem, vmem, vmem],
-        out_specs=(vmem, vmem),
+        in_specs=[smem(), vmem, vmem, vmem, hbm],
+        out_specs=(hbm, hbm),
         scratch_shapes=[
             pltpu.VMEM((2, GROUP // 2, 2 * PART, HD), BF),
             pltpu.VMEM((2, GROUP // 2, 2 * PART, HD), F32),
             pltpu.VMEM((2, GROUP // 2, 2 * PART, 2 * HD), F32),
             pltpu.VMEM((2, tokens // 2, 2 * HD), BF),
             pltpu.VMEM((2 * PART, WIDE), F32),
+            pltpu.VMEM(other.shape, BF),
+            pltpu.VMEM(own.shape, BF),
+            pltpu.VMEM(own.shape, BF),
+            pltpu.SemaphoreType.DMA((3,)),
         ],
-        compiler_params=pltpu.CompilerParams(vmem_limit_bytes=40 << 20),
+        compiler_params=pltpu.CompilerParams(vmem_limit_bytes=28 << 20),
         cost_estimate=pl.CostEstimate(
             flops=4 * GROUP * PART * tokens * HD,
             transcendentals=GROUP * PART * tokens,
@@ -267,12 +321,15 @@
 CHUNK = 8
 
 
-def text_kernel(info, text, q_ref, mine_ref, other_ref, high_ref, low_ref, out_ref):
+def text_kernel(info, text, q_ref, mine_ref, other_hbm, high_ref, low_ref, out_ref, other_ref, sem):
     chip, core, low, count = (info[i] for i in range(4))
     first = (2 * chip + core) * ROWS
     half = mine_ref.shape[0]
+    fetch = pltpu.make_async_copy(other_hbm, other_ref, sem)
+    fetch.start()
     out_ref[...] = jnp.zeros_like(out_ref)
     rows = GROUP * CHUNK
+    fetch.wait()
 
     def chunk(c, carry):
         place = jnp.zeros((CHUNK, ROWS), jnp.int32)
@@ -318,9 +375,13 @@
     return pl.pallas_call(
         text_kernel,
         out_shape=(jax.ShapeDtypeStruct((2, tokens // 2), BF),) * 2,
-        in_specs=[smem(), smem(), vmem, vmem, vmem],
+        in_specs=[smem(), smem(), vmem, vmem, pl.BlockSpec(memory_space=pl.ANY)],
         out_specs=(vmem, vmem),
-        scratch_shapes=[pltpu.VMEM((2, tokens // 2), F32)],
+        scratch_shapes=[
+            pltpu.VMEM((2, tokens // 2), F32),
+            pltpu.VMEM(other.shape, BF),
+            pltpu.SemaphoreType.DMA(()),
+        ],
         compiler_params=pltpu.CompilerParams(vmem_limit_bytes=24 << 20),
         cost_estimate=pl.CostEstimate(
             flops=2 * GROUP * CHUNK * tokens * HD,
@@ -331,7 +392,9 @@
     )(info, text_rows, q2, mine, other)
 
 
-def attend3_kernel(info, q_ref, mine_ref, other_ref, out_ref, v_s, bias_s):
+def attend3_kernel(info, q_hbm, mine_ref, other_ref, out_ref, v_s, bias_s, q_ref, sem):
+    fetch = pltpu.make_async_copy(q_hbm, q_ref, sem)
+    fetch.start()
     chip, core = info[0], info[1]
     half = mine_ref.shape[0]
     v_s[:half, :HD] = mine_ref[:, HD:]
@@ -364,22 +427,26 @@
         out = (total[:, :HD] / total[:, HD:]).astype(BF)
         out_ref[:, h * HD : (h + 1) * HD] = out[:SHARE]
 
+    fetch.wait()
     in_turn(range(GROUP), scored, weighed)
 
 
 def attend3(info, q3, mine, other):
     vmem = pl.BlockSpec(memory_space=pltpu.VMEM)
     keys = 2 * mine.shape[0]
+    q3 = pltpu.with_memory_space_constraint(q3, pltpu.HBM)
     return pl.pallas_call(
         attend3_kernel,
         out_shape=jax.ShapeDtypeStruct((SHARE, q3.shape[1]), BF),
-        in_specs=[smem(), vmem, vmem, vmem],
+        in_specs=[smem(), pl.BlockSpec(memory_space=pl.ANY), vmem, vmem],
         out_specs=vmem,
         scratch_shapes=[
             pltpu.VMEM((keys, 2 * HD), BF),
             pltpu.VMEM((PAD, keys), F32),
+            pltpu.VMEM(q3.shape, BF),
+            pltpu.SemaphoreType.DMA(()),
         ],
-        compiler_params=pltpu.CompilerParams(vmem_limit_bytes=40 << 20),
+        compiler_params=pltpu.CompilerParams(vmem_limit_bytes=28 << 20),
         cost_estimate=pl.CostEstimate(
             flops=6 * GROUP * PAD * keys * HD,
             transcendentals=GROUP * PAD * keys,
@@ -458,24 +525,39 @@
     cosine = jnp.concatenate([cosine, cosine], axis=1)
     sine = jnp.concatenate([-sine, sine], axis=1)
 
-    distances = (-1, 1, 2)
-    pieces = [from_head(x, d) for d in distances]
     weights = (w_query, w_key, w_value)
-    partial = project(head[None].astype(jnp.int32), [x], weights, ())
+    here = head.astype(jnp.int32)
+
+    def block(distance):
+        return (here + distance) % head_count
+
+    pieces = {d: from_head(x, d) for d in (2, 1, -1)}
+    partial = project(here[None], [x], weights)
+    sums, text_rows, q2 = lax.optimization_barrier((partial[1], text_rows, q2))
+    partial = (partial[0], sums)
+    far = from_partner(q2[PART:])
     low = jnp.sum((text_rows < first).astype(jnp.int32))
     count = jnp.sum((text_rows < first + ROWS).astype(jnp.int32)) - low
     partner = seq_count - 1 - rank
     place = jnp.stack([0, chip, core, partner // 2, partner % 2])
     text_info = jnp.stack([chip, core, low, count])
-    far = from_partner(q2[PART:])
-    blocks = jnp.stack([(head + d) % head_count for d in distances]).astype(jnp.int32)
+    partial = project(block(2)[None], [pieces[2]], weights, partial)
     biases = tuple(b[None, :] for b in (b_query, b_key, b_value))
-    mine2, pieces, far, *ready = lax.optimization_barrier(
-        (mine2, pieces, far, *partial, *biases, cosine, sine, place, text_info, blocks)
+    blocks = jnp.stack([block(1), block(-1)])
+    mine2, far, partial, two, ready, place, text_info, blocks = lax.optimization_barrier(
+        (
+            mine2,
+            far,
+            partial,
+            [pieces[1], pieces[-1]],
+            (*biases, cosine, sine),
+            place,
+            text_info,
+            blocks,
+        )
     )
-    *ready, place, text_info, blocks = ready
     other2 = from_core(mine2)
-    q3, kv3 = project(blocks, pieces, weights, ready)
+    q3, kv3 = project(blocks, two, weights, partial, ready)
     kv3, other2 = lax.optimization_barrier((kv3, other2))
     sums = text_sums(text_info, text_rows, q2, mine2, other2)
 

time: 120 us -> 108 us (0.900)
  waiting for transfers between devices: 18.8 us -> 4.83 us
  local copies, waits for them, and re-layouts: 13.4 us -> 3.91 us
  Pallas kernels: 45.7 us -> 52.4 us
  starting transfers between devices: 31.9 us -> 37.3 us
    unnamed x44 -> x22, local copies, waits for them, and re-layouts: 10.8 us -> 1.27 us
    ppermute x2, waiting for transfers between devices: 11 us -> 2.72 us  [from_partner(): return lax.ppermute(x, 'seq', [(count - 1 - i, i) for i in range(count)])]
    ppermute x3, waiting for transfers between devices: 7.71 us -> 0.5 us  [from_head(): lax.ppermute(x, 'head', [((i + distance) % count, i) for i in range(count)])]
    pallas_call x2 -> x3, Pallas kernels: 12.1 us -> 17.4 us  [project(): pl.pallas_call(kernel, out_shape=(pltpu.HBM(outs[0], kind), jax.ShapeDtyp...]
    all_to_all x2, starting transfers between devices: 11.6 us -> 14.6 us  [over_chips(): lax.all_to_all(many, 'seq', 0, 0, axis_index_groups=groups, tiled=True)]
    ppermute x2, starting transfers between devices: 9.52 us -> 11.2 us  [from_partner(): return lax.ppermute(x, 'seq', [(count - 1 - i, i) for i in range(count)])]
    ppermute x3, waiting for transfers between devices: 0.01 us -> 1.6 us  [from_core(): return lax.ppermute(x, 'seq', [(i ^ 1, i) for i in range(count)])]
    pallas_call x1, Pallas kernels: 19.4 us -> 20.8 us  [attend(): pl.pallas_call(attend_kernel, out_shape=(out, out), in_specs=[smem(), vme...]
  transfers between devices with their start and end apart: 13 -> 13, of which waited for: 2 -> 3; matrix products, arithmetic and copies ran while one was open for 4% -> 4% of each run, Pallas kernels for 36% -> 46%
where the time goes in v4:
time: 108 us
  Pallas kernels  52.4 us (49%)
  starting transfers between devices  37.3 us (35%)
  other arithmetic  6.95 us (6%)
  waiting for transfers between devices  4.83 us (4%)
  local copies, waits for them, and re-layouts  3.91 us (4%)
  between operations  2.22 us (2%)
    pallas_call x1, Pallas kernels, attend(): pl.pallas_call(attend_kernel, out_shape=(out, out), in_specs=[smem(), vme...  20.8 us
    pallas_call x3, Pallas kernels, project(): pl.pallas_call(kernel, out_shape=(pltpu.HBM(outs[0], kind), jax.ShapeDtyp...  17.4 us
    all_to_all x2, starting transfers between devices, over_chips(): lax.all_to_all(many, 'seq', 0, 0, axis_index_groups=groups, tiled=True)  14.6 us
    ppermute x2, starting transfers between devices, from_partner(): return lax.ppermute(x, 'seq', [(count - 1 - i, i) for i in range(count)])  11.2 us
    pallas_call x1, Pallas kernels, attend3(): pl.pallas_call(attend3_kernel, out_shape=jax.ShapeDtypeStruct((SHARE, q3....  10.5 us
    ppermute x3, starting transfers between devices, from_head(): lax.ppermute(x, 'head', [((i + distance) % count, i) for i in range(count)])  5.14 us
    ppermute x3, starting transfers between devices, over_heads(): lax.ppermute(x, 'head', [(i ^ step, i) for i in range(count)])  3.94 us
    ppermute x2, waiting for transfers between devices, from_partner(): return lax.ppermute(x, 'seq', [(count - 1 - i, i) for i in range(count)])  2.72 us
  transfers between devices with their start and end apart: 13, of which 3 were waited for; matrix products, arithmetic and copies ran while one was open for 4% of the time, Pallas kernels for 46%

profile of v4, /device:TPU:1, one launch (start us, length us, event | category | flops | bytes accessed | tf_op | source)
XLA Modules:
  0.0 107.6 jit_solution(2816001499105615003)
XLA Ops:
  0.6 0.9 pad_maximum_fusion.2
  1.5 1.5 %broadcast_in_dim.14 = bf16[16,256,256]{2,1,0:T(8,128)(2,1)} broadcast(bf16[256,256]{1,0:T(8,128)(2,1)S(1)} %pad_maximum_fusion.2), dimensions={1,2} | broadcast | bytes 2228224 | tf_op jit(solution)/shard_map/broadcast_in_dim | solution.py:513
  3.1 7.7 %all-to-all-start = ((bf16[16,256,256]{2,1,0:T(8,128)(2,1)}), bf16[16,256,256]{2,1,0:T(8,128)(2,1)S(1)}, u32[]{:S(2)}, u32[]{:S(2)}) async-start(bf16[16,256,256]{2,1,0:T(8,128)(2,1)} %broadcast_in_dim.14), calls=%async_computation | async-start | bytes 4194304 | tf_op jit(solution)/shard_map/all_to_all | solution.py:472
  10.8 0.0 copy-done.10
  10.8 0.1 pad_add_fusion.info
  10.9 0.0 copy-done.8
  10.9 1.2 %copy-done.7 = bf16[256,2048]{1,0:T(8,128)(2,1)S(1)} copy-done((bf16[256,2048]{1,0:T(8,128)(2,1)S(1)}, bf16[256,2048]{1,0:T(8,128)(2,1)}, u32[]{:S(2)}) %copy-start.7) | copy-done | bytes 1048600
  12.1 1.1 %pick_rows.1 = (bf16[136,2176]{1,0:T(8,128)(2,1)S(1)}, bf16[136,2176]{1,0:T(8,128)(2,1)S(1)}) custom-call(s32[5]{0:T(128)S(1)} %pad_add_fusion.info, s32[1,256]{1,0:T(1,128)S(1)} %bitcast.37, bf16[256,2048]{1,0:T(8,128)(2,1)S(1)} %copy-done.7), custom_call_target="tpu_custom_call" | custom-call | flops 303038464 | bytes 2228224 | tf_op jit(solution)/shard_map/pick_rows/pallas_call | solution.py:68
  13.2 1.0 collective-permute-start
  14.3 0.1 stack.48.info
  14.3 0.1 pad_add_fusion.2.refs_0_
  14.4 1.6 %collective-permute-done = bf16[136,2176]{1,0:T(8,128)(2,1)} collective-permute-done((bf16[136,2176]{1,0:T(8,128)(2,1)S(1)}, bf16[136,2176]{1,0:T(8,128)(2,1)}, u32[]{:S(2)}, u32[]{:S(2)}) %collective-permute-start) | collective-permute-done | bytes 591904 | tf_op jit(solution)/shard_map/ppermute | solution.py:461
  16.0 1.2 %add.53 = bf16[136,2176]{1,0:T(8,128)(2,1)S(1)} add(bf16[136,2176]{1,0:T(8,128)(2,1)S(1)} %get-tuple-element.43, bf16[136,2176]{1,0:T(8,128)(2,1)} %collective-permute-done) | non-fusion elementwise | flops 295936 | bytes 1775616 | tf_op jit(solution)/shard_map/add | solution.py:518
  17.3 3.7 %collective-permute-start.2 = (bf16[136,2048]{1,0:T(8,128)(2,1)S(1)}, bf16[136,2048]{1,0:T(8,128)(2,1)}, u32[]{:S(2)}, u32[]{:S(2)}) collective-permute-start(bf16[136,2048]{1,0:T(8,128)(2,1)S(1)} %slice.59.refs_1_), channel_id=1, source_target_pairs={{2,0},{3,1},{0,2},{1,3},{6,4},{7,5},{4,6},{5,7},{10,8},{11,9},{8,1... | collective-permute-start | bytes 1671176 | tf_op jit(solution)/shard_map/ppermute | solution.py:466
  21.0 0.4 collective-permute-start.3
  21.4 1.0 collective-permute-start.4
  22.4 4.4 %project.3 = (f32[136,1024]{1,0:T(8,128)}, f32[136,256]{1,0:T(8,128)}) custom-call(s32[1]{0:T(128)} %bitcast.1.refs_0_, bf16[136,2048]{1,0:T(8,128)(2,1)S(1)} %slice.59.refs_1_, bf16[8192,1024]{1,0:T(8,128)(2,1)} %refs_3_.5, bf16[8192,128]{1,0:T(8,128)(2,1)} %refs_4_.5, bf16[8192,128]{1,0:T(8,128)(2,1)} %refs_5_.1), custom_call_target="tpu_custom_call" | custom-call | flops 713031680 | bytes 5242880 | tf_op jit(solution)/shard_map/project/pallas_call | solution.py:172
  26.8 0.0 copy-done.1
  26.8 0.8 fusion.5
  27.6 6.1 %collective-permute-start.1 = (bf16[128,1024]{1,0:T(8,128)(2,1)}, bf16[128,1024]{1,0:T(8,128)(2,1)}, u32[]{:S(2)}, u32[]{:S(2)}) collective-permute-start(bf16[128,1024]{1,0:T(8,128)(2,1)} %get-tuple-element.86), channel_id=1, source_target_pairs={{124,0},{120,4},{116,8},{112,12},{108,16},{104,20},{100,24},{96,28... | collective-permute-start | bytes 786440 | tf_op jit(solution)/shard_map/ppermute | solution.py:484
  33.7 0.2 fusion.1
  33.9 0.0 copy-done.4
  33.9 0.7 fusion.3
  35.9 0.3 fusion.2
  36.2 0.8 pad_add_fusion.1.info
  37.0 0.1 pad_maximum_fusion.3
  37.1 0.0 collective-permute-done.2.refs_1_
  37.1 0.0 copy-start.3
  37.1 0.0 copy-start.5
  37.1 0.0 copy-start.6
  37.1 5.8 %project.4 = (f32[136,1024]{1,0:T(8,128)}, f32[136,256]{1,0:T(8,128)}) custom-call(s32[1]{0:T(128)} %bitcast.5.refs_0_, bf16[136,2048]{1,0:T(8,128)(2,1)} %collective-permute-done.2.refs_1_, bf16[8192,1024]{1,0:T(8,128)(2,1)} %refs_3_.5, bf16[8192,128]{1,0:T(8,128)(2,1)} %refs_4_.5, bf16[8192,128]{1,0:T(8,128)(2,1)} %refs_5_.1, ...), custom_call_target="tpu_custom_call" | custom-call | flops 713031680 | bytes 5242880 | tf_op jit(solution)/shard_map/project/pallas_call | solution.py:172
  42.9 2.7 %collective-permute-done.1.far_ref = bf16[128,1024]{1,0:T(8,128)(2,1)} collective-permute-done((bf16[128,1024]{1,0:T(8,128)(2,1)}, bf16[128,1024]{1,0:T(8,128)(2,1)}, u32[]{:S(2)}, u32[]{:S(2)}) %collective-permute-start.1) | collective-permute-done | bytes 262176 | tf_op jit(solution)/shard_map/ppermute | solution.py:484
  45.7 0.5 collective-permute-done.3.refs_1_
  46.2 0.0 collective-permute-done.4.refs_2_
  46.2 0.0 all-to-all-done
  46.2 1.2 %collective-permute-start.5 = (bf16[4096,256]{1,0:T(8,128)(2,1)S(1)}, bf16[4096,256]{1,0:T(8,128)(2,1)S(1)}, u32[]{:S(2)}, u32[]{:S(2)}) collective-permute-start(bf16[4096,256]{1,0:T(8,128)(2,1)S(1)} %bitcast.26), channel_id=1, source_target_pairs={{4,0},{0,4},{12,8},{8,12},{20,16},{16,20},{28,24},{24,28},{36,32},... | collective-permute-start | bytes 6291464 | tf_op jit(solution)/shard_map/ppermute | solution.py:461
  47.4 0.0 copy-done.3
  47.4 0.0 copy-done.5
  47.4 0.0 copy-done.6
  47.4 7.2 %project.5 = (bf16[136,1024]{1,0:T(8,128)(2,1)}, bf16[136,256]{1,0:T(8,128)(2,1)S(1)}) custom-call(s32[2]{0:T(128)S(1)} %pad_add_fusion.2.refs_0_, bf16[136,2048]{1,0:T(8,128)(2,1)} %collective-permute-done.3.refs_1_, bf16[136,2048]{1,0:T(8,128)(2,1)} %collective-permute-done.4.refs_2_, bf16[8192,1024]{1,0:T(8,128)(2,1)} %refs_3_.5, ...), custom_call_target="tpu_custom_call" | custom-call | flops 1426063360 | bytes 10485760 | tf_op jit(solution)/shard_map/project/pallas_call | solution.py:172
  54.6 0.0 collective-permute-done.5.other_hbm.other_ref
  54.6 0.0 copy-start
  54.6 2.6 %text_sums.1 = (bf16[2,4096]{1,0:T(2,128)(2,1)S(1)}, bf16[2,4096]{1,0:T(2,128)(2,1)S(1)}) custom-call(s32[4]{0:T(128)S(1)} %pad_add_fusion.1.info, s32[256]{0:T(256)S(1)} %copy-done.4, bf16[256,1024]{1,0:T(8,128)(2,1)S(1)} %copy-done.1, bf16[4096,256]{1,0:T(8,128)(2,1)S(1)} %bitcast.27, bf16[4096,256]{1,0:T(8,128)(2,1)S(1)} %collective-permute-done.5.other_hbm.other_ref), custom_call_target="tpu_custom_call" | custom-call | flops 134217728 | bytes 4194304 | tf_op jit(solution)/shard_map/text_sums/pallas_call | solution.py:375
  57.2 0.0 copy-done
  57.2 0.1 broadcast_in_dim.35
  57.3 0.0 copy-start.2
  57.3 1.1 %pad_maximum_fusion = bf16[16,136,256]{2,1,0:T(8,128)(2,1)} fusion(bf16[16,2,256]{2,1,0:T(2,128)(2,1)S(1)} %bitcast.32, bf16[16,2,256]{2,1,0:T(2,128)(2,1)S(1)} %bitcast.31, bf16[16,132,256]{2,1,0:T(8,128)(2,1)S(1)} %broadcast_in_dim.35), kind=kLoop, calls=%fused_computation | loop fusion | flops 3342336 | bytes 2228224 | tf_op jit(solution)/shard_map/concatenate | solution.py:566
  58.4 6.9 %all-to-all-start.1 = ((bf16[16,136,256]{2,1,0:T(8,128)(2,1)}), bf16[16,136,256]{2,1,0:T(8,128)(2,1)S(1)}, u32[]{:S(2)}, u32[]{:S(2)}) async-start(bf16[16,136,256]{2,1,0:T(8,128)(2,1)} %pad_maximum_fusion), calls=%async_computation.1 | async-start | bytes 2228224 | tf_op jit(solution)/shard_map/all_to_all | solution.py:472
  65.4 20.8 %attend2.1 = (bf16[128,1024]{1,0:T(8,128)(2,1)}, bf16[128,1024]{1,0:T(8,128)(2,1)}) custom-call(s32[5]{0:T(128)S(1)} %stack.48.info, bf16[128,1024]{1,0:T(8,128)(2,1)S(1)} %copy-done.2, bf16[128,1024]{1,0:T(8,128)(2,1)} %collective-permute-done.1.far_ref, bf16[4096,256]{1,0:T(8,128)(2,1)S(1)} %bitcast.28, bf16[4096,256]{1,0:T(8,128)(2,1)} %copy-done), custom_call_target="tpu_custom_call" | custom-call | flops 4294967296 | bytes 4194304 | tf_op jit(solution)/shard_map/attend2/pallas_call | solution.py:295
  86.2 0.0 all-to-all-done.1
  86.2 0.1 collective-permute-start.6
  86.3 0.1 slice.52.info
  86.3 5.2 %collective-permute-start.7 = (bf16[128,1024]{1,0:T(8,128)(2,1)}, bf16[128,1024]{1,0:T(8,128)(2,1)S(1)}, u32[]{:S(2)}, u32[]{:S(2)}) collective-permute-start(bf16[128,1024]{1,0:T(8,128)(2,1)} %get-tuple-element.76), channel_id=1, source_target_pairs={{124,0},{120,4},{116,8},{112,12},{108,16},{104,20},{100,24},{96,28... | collective-permute-start | bytes 786440 | tf_op jit(solution)/shard_map/ppermute | solution.py:484
  91.6 0.0 collective-permute-done.6
  91.6 2.4 %collective-permute-start.10 = (f32[256]{0:T(256)S(1)}, f32[256]{0:T(256)S(1)}, u32[]{:S(2)}, u32[]{:S(2)}) collective-permute-start(f32[256]{0:T(256)S(1)} %bitcast.38), channel_id=1, source_target_pairs={{3,0},{2,1},{1,2},{0,3},{7,4},{6,5},{5,6},{4,7},{11,8},{10,9},{9,1... | collective-permute-start | bytes 3080 | tf_op jit(solution)/shard_map/ppermute | solution.py:478
  94.0 0.0 collective-permute-start.8
  94.0 1.5 %collective-permute-start.9 = (f32[256]{0:T(256)S(1)}, f32[256]{0:T(256)S(1)}, u32[]{:S(2)}, u32[]{:S(2)}) collective-permute-start(f32[256]{0:T(256)S(1)} %bitcast.40), channel_id=1, source_target_pairs={{2,0},{3,1},{0,2},{1,3},{6,4},{7,5},{4,6},{5,7},{10,8},{11,9},{8,1... | collective-permute-start | bytes 3080 | tf_op jit(solution)/shard_map/ppermute | solution.py:478
  95.6 10.5 %attend3.1 = bf16[132,1024]{1,0:T(8,128)(2,1)} custom-call(s32[2]{0:T(128)S(1)} %slice.52.info, bf16[136,1024]{1,0:T(8,128)(2,1)} %get-tuple-element.73.q_hbm, bf16[2176,256]{1,0:T(8,128)(2,1)S(1)} %bitcast.29, bf16[2176,256]{1,0:T(8,128)(2,1)S(1)} %bitcast.34), custom_call_target="tpu_custom_call" | custom-call | flops 3636461568 | bytes 2228224 | tf_op jit(solution)/shard_map/attend3/pallas_call | solution.py:438
  106.1 0.0 collective-permute-done.7
  106.1 0.0 collective-permute-done.10
  106.1 0.0 collective-permute-done.8
  106.2 0.0 collective-permute-done.9
  106.2 0.8 pad_maximum_fusion.1
  107.0 0.6 add_add_fusion
  (16 shorter events, 0.2 us)
Async XLA Ops:
  3.1 7.7 %copy-start.10 = (s32[2]{0:T(128)S(1)}, s32[2]{0:T(128)}, u32[]{:S(2)}) copy-start(s32[2]{0:T(128)} %param.24) | copy-start | bytes 28
  3.1 7.8 %copy-start.8 = (s32[256]{0:T(256)S(1)}, s32[256]{0:T(256)}, u32[]{:S(2)}) copy-start(s32[256]{0:T(256)} %param.23) | copy-start | bytes 3076
  3.1 43.1 %all-to-all-start = ((bf16[16,256,256]{2,1,0:T(8,128)(2,1)}), bf16[16,256,256]{2,1,0:T(8,128)(2,1)S(1)}, u32[]{:S(2)}, u32[]{:S(2)}) async-start(bf16[16,256,256]{2,1,0:T(8,128)(2,1)} %broadcast_in_dim.14), calls=%async_computation | async-start | bytes 4194304 | tf_op jit(solution)/shard_map/all_to_all | solution.py:472
  10.9 1.2 %copy-start.7 = (bf16[256,2048]{1,0:T(8,128)(2,1)S(1)}, bf16[256,2048]{1,0:T(8,128)(2,1)}, u32[]{:S(2)}) copy-start(bf16[256,2048]{1,0:T(8,128)(2,1)} %hidden_ref.1) | copy-start | bytes 3145732
  13.2 2.8 %collective-permute-start = (bf16[136,2176]{1,0:T(8,128)(2,1)S(1)}, bf16[136,2176]{1,0:T(8,128)(2,1)}, u32[]{:S(2)}, u32[]{:S(2)}) collective-permute-start(bf16[136,2176]{1,0:T(8,128)(2,1)S(1)} %get-tuple-element.44), channel_id=1, source_target_pairs={{4,0},{0,4},{12,8},{8,12},{20,16},{16,20},{28,24},{24,28},{36,32},... | collective-permute-start | bytes 1775624 | tf_op jit(solution)/shard_map/ppermute | solution.py:461
  17.3 19.8 %collective-permute-start.2 = (bf16[136,2048]{1,0:T(8,128)(2,1)S(1)}, bf16[136,2048]{1,0:T(8,128)(2,1)}, u32[]{:S(2)}, u32[]{:S(2)}) collective-permute-start(bf16[136,2048]{1,0:T(8,128)(2,1)S(1)} %slice.59.refs_1_), channel_id=1, source_target_pairs={{2,0},{3,1},{0,2},{1,3},{6,4},{7,5},{4,6},{5,7},{10,8},{11,9},{8,1... | collective-permute-start | bytes 1671176 | tf_op jit(solution)/shard_map/ppermute | solution.py:466
  21.0 25.2 %collective-permute-start.3 = (bf16[136,2048]{1,0:T(8,128)(2,1)S(1)}, bf16[136,2048]{1,0:T(8,128)(2,1)}, u32[]{:S(2)}, u32[]{:S(2)}) collective-permute-start(bf16[136,2048]{1,0:T(8,128)(2,1)S(1)} %slice.59.refs_1_), channel_id=1, source_target_pairs={{1,0},{2,1},{3,2},{0,3},{5,4},{6,5},{7,6},{4,7},{9,8},{10,9},{11,1... | collective-permute-start | bytes 1671176 | tf_op jit(solution)/shard_map/ppermute | solution.py:466
  21.4 24.8 %collective-permute-start.4 = (bf16[136,2048]{1,0:T(8,128)(2,1)S(1)}, bf16[136,2048]{1,0:T(8,128)(2,1)}, u32[]{:S(2)}, u32[]{:S(2)}) collective-permute-start(bf16[136,2048]{1,0:T(8,128)(2,1)S(1)} %slice.59.refs_1_), channel_id=1, source_target_pairs={{3,0},{0,1},{1,2},{2,3},{7,4},{4,5},{5,6},{6,7},{11,8},{8,9},{9,10... | collective-permute-start | bytes 1671176 | tf_op jit(solution)/shard_map/ppermute | solution.py:466
  22.4 4.4 %copy-start.1 = (bf16[256,1024]{1,0:T(8,128)(2,1)S(1)}, bf16[256,1024]{1,0:T(8,128)(2,1)}, u32[]{:S(2)}) copy-start(bf16[256,1024]{1,0:T(8,128)(2,1)} %q_ref) | copy-start | bytes 1572868
  22.4 11.5 %copy-start.4 = (s32[256]{0:T(256)S(1)}, s32[256]{0:T(256)}, u32[]{:S(2)}) copy-start(s32[256]{0:T(256)} %text) | copy-start | bytes 3076
  27.6 18.0 %collective-permute-start.1 = (bf16[128,1024]{1,0:T(8,128)(2,1)}, bf16[128,1024]{1,0:T(8,128)(2,1)}, u32[]{:S(2)}, u32[]{:S(2)}) collective-permute-start(bf16[128,1024]{1,0:T(8,128)(2,1)} %get-tuple-element.86), channel_id=1, source_target_pairs={{124,0},{120,4},{116,8},{112,12},{108,16},{104,20},{100,24},{96,28... | collective-permute-start | bytes 786440 | tf_op jit(solution)/shard_map/ppermute | solution.py:484
  37.1 10.3 %copy-start.3 = (f32[1024]{0:T(1024)S(1)}, f32[1024]{0:T(1024)}, u32[]{:S(2)}) copy-start(f32[1024]{0:T(1024)} %param.18) | copy-start | bytes 12292
  37.1 10.3 %copy-start.5 = (f32[128]{0:T(128)S(1)}, f32[128]{0:T(128)}, u32[]{:S(2)}) copy-start(f32[128]{0:T(128)} %param.20) | copy-start | bytes 1540
  37.1 10.3 %copy-start.6 = (f32[128]{0:T(128)S(1)}, f32[128]{0:T(128)}, u32[]{:S(2)}) copy-start(f32[128]{0:T(128)} %param.22) | copy-start | bytes 1540
  46.2 8.4 %collective-permute-start.5 = (bf16[4096,256]{1,0:T(8,128)(2,1)S(1)}, bf16[4096,256]{1,0:T(8,128)(2,1)S(1)}, u32[]{:S(2)}, u32[]{:S(2)}) collective-permute-start(bf16[4096,256]{1,0:T(8,128)(2,1)S(1)} %bitcast.26), channel_id=1, source_target_pairs={{4,0},{0,4},{12,8},{8,12},{20,16},{16,20},{28,24},{24,28},{36,32},... | collective-permute-start | bytes 6291464 | tf_op jit(solution)/shard_map/ppermute | solution.py:461
  54.6 2.6 %copy-start = (bf16[4096,256]{1,0:T(8,128)(2,1)}, bf16[4096,256]{1,0:T(8,128)(2,1)S(1)}, u32[]{:S(2)}) copy-start(bf16[4096,256]{1,0:T(8,128)(2,1)S(1)} %collective-permute-done.5.other_hbm.other_ref) | copy-start | bytes 6291460
  57.3 8.1 %copy-start.2 = (bf16[128,1024]{1,0:T(8,128)(2,1)S(1)}, bf16[128,1024]{1,0:T(8,128)(2,1)}, u32[]{:S(2)}) copy-start(bf16[128,1024]{1,0:T(8,128)(2,1)} %get-tuple-element.85.own_ref) | copy-start | bytes 786436
  58.4 27.7 %all-to-all-start.1 = ((bf16[16,136,256]{2,1,0:T(8,128)(2,1)}), bf16[16,136,256]{2,1,0:T(8,128)(2,1)S(1)}, u32[]{:S(2)}, u32[]{:S(2)}) async-start(bf16[16,136,256]{2,1,0:T(8,128)(2,1)} %pad_maximum_fusion), calls=%async_computation.1 | async-start | bytes 2228224 | tf_op jit(solution)/shard_map/all_to_all | solution.py:472
  86.2 5.4 %collective-permute-start.6 = (bf16[16,136,256]{2,1,0:T(8,128)(2,1)S(1)}, bf16[16,136,256]{2,1,0:T(8,128)(2,1)S(1)}, u32[]{:S(2)}, u32[]{:S(2)}) collective-permute-start(bf16[16,136,256]{2,1,0:T(8,128)(2,1)S(1)} %all-to-all-done.1), channel_id=1, source_target_pairs={{4,0},{0,4},{12,8},{8,12},{20,16},{16,20},{28,24},{24,28},{36,32},... | collective-permute-start | bytes 3342344 | tf_op jit(solution)/shard_map/ppermute | solution.py:461
  86.3 19.8 %collective-permute-start.7 = (bf16[128,1024]{1,0:T(8,128)(2,1)}, bf16[128,1024]{1,0:T(8,128)(2,1)S(1)}, u32[]{:S(2)}, u32[]{:S(2)}) collective-permute-start(bf16[128,1024]{1,0:T(8,128)(2,1)} %get-tuple-element.76), channel_id=1, source_target_pairs={{124,0},{120,4},{116,8},{112,12},{108,16},{104,20},{100,24},{96,28... | collective-permute-start | bytes 786440 | tf_op jit(solution)/shard_map/ppermute | solution.py:484
  91.6 14.5 %collective-permute-start.10 = (f32[256]{0:T(256)S(1)}, f32[256]{0:T(256)S(1)}, u32[]{:S(2)}, u32[]{:S(2)}) collective-permute-start(f32[256]{0:T(256)S(1)} %bitcast.38), channel_id=1, source_target_pairs={{3,0},{2,1},{1,2},{0,3},{7,4},{6,5},{5,6},{4,7},{11,8},{10,9},{9,1... | collective-permute-start | bytes 3080 | tf_op jit(solution)/shard_map/ppermute | solution.py:478
  94.0 12.1 %collective-permute-start.8 = (f32[256]{0:T(256)S(1)}, f32[256]{0:T(256)S(1)}, u32[]{:S(2)}, u32[]{:S(2)}) collective-permute-start(f32[256]{0:T(256)S(1)} %bitcast.39), channel_id=1, source_target_pairs={{1,0},{0,1},{3,2},{2,3},{5,4},{4,5},{7,6},{6,7},{9,8},{8,9},{11,10... | collective-permute-start | bytes 3080 | tf_op jit(solution)/shard_map/ppermute | solution.py:478
  94.0 12.1 %collective-permute-start.9 = (f32[256]{0:T(256)S(1)}, f32[256]{0:T(256)S(1)}, u32[]{:S(2)}, u32[]{:S(2)}) collective-permute-start(f32[256]{0:T(256)S(1)} %bitcast.40), channel_id=1, source_target_pairs={{2,0},{3,1},{0,2},{1,3},{6,4},{7,5},{4,6},{5,7},{10,8},{11,9},{8,1... | collective-permute-start | bytes 3080 | tf_op jit(solution)/shard_map/ppermute | solution.py:478
  95.6 10.6 %copy-start.9 = (bf16[128,1024]{1,0:T(8,128)(2,1)S(1)}, bf16[128,1024]{1,0:T(8,128)(2,1)}, u32[]{:S(2)}) copy-start(bf16[128,1024]{1,0:T(8,128)(2,1)} %get-tuple-element.72) | copy-start | bytes 786436

commit v5 on v4

--- a/solution.py
+++ b/solution.py
@@ -96,6 +96,8 @@
         bq, bk, bv, cosine, sine = rest[:5]
         rest = rest[5:]
     q_to, kv_out, *held, kv_s, q_s, q_out, sems, part_sems = rest
+    if last:
+        q_out = q_to
     sums = (q_s, kv_s)
     loads = []
     if not first:
@@ -140,7 +142,7 @@
             q_out[:, at] = rotated(q[:, at] + bq[:, at], c, s).astype(BF)
         kv_out[:, :HD] = rotated(k + bk[...], c, s).astype(BF)
         kv_out[:, HD:] = (v + bv[...]).astype(BF)
-        stores = [pltpu.make_async_copy(q_out, q_to, part_sems.at[2])]
+        stores = []
     else:
         q_out[...] = q
         kv_s[:, :HD] = k
@@ -172,14 +174,13 @@
     return pl.pallas_call(
         kernel,
         out_shape=(
-            pltpu.HBM(outs[0], kind),
-            jax.ShapeDtypeStruct(outs[1], kind) if finish else pltpu.HBM(outs[1], kind),
+            *(jax.ShapeDtypeStruct(o, kind) if finish else pltpu.HBM(o, kind) for o in outs),
         ),
         in_specs=[smem()]
         + [vmem] * pieces
         + [hbm] * (3 + len(partial))
         + [vmem] * len(finish),
-        out_specs=(hbm, vmem if finish else hbm),
+        out_specs=(vmem, vmem) if finish else (hbm, hbm),
         scratch_shapes=[pltpu.VMEM((pieces * depth, width), BF) for width in widths]
         + [
             pltpu.VMEM(outs[1], F32),
@@ -517,47 +518,50 @@
     own, sent = pick_rows(numbers, kept_index, hidden)
     x = own + from_core(sent)
     marks = x[:, depth : depth + 2].astype(jnp.int32)
+    half = depth // 2
+    low, high = (x[:, :half], x[:, half:depth])
+
+    weights = (w_query, w_key, w_value)
+    here = head.astype(jnp.int32)
+
+    def half_blocks(*pieces):
+        return jnp.stack([2 * ((here + d) % head_count) + side for d, side in pieces])
+
+    low_before, high_next = (from_head(low, -1), from_head(high, 1))
+    high_before, low_next = (from_head(high, -1), from_head(low, 1))
+    partial = project(half_blocks((0, 0), (0, 1)), [low, high], weights)
+    low_far, high_far = (from_head(low_before, -1), from_head(high_next, 1))
+
+    sums, marks, text_rows, q2 = lax.optimization_barrier((partial[1], marks, text_rows, q2))
+    partial = (partial[0], sums)
+    far = from_partner(q2[PART:])
     positions = marks[:, 0] * 128 + marks[:, 1]
-    x = x[:, :depth]
     freqs = 1000000.0 ** (-(jnp.arange(HD // 2, dtype=F32) * 2.0) / HD)
     angles = positions.astype(F32)[:, None] * freqs[None, :]
     cosine, sine = (jnp.cos(angles), jnp.sin(angles))
     cosine = jnp.concatenate([cosine, cosine], axis=1)
     sine = jnp.concatenate([-sine, sine], axis=1)
-
-    weights = (w_query, w_key, w_value)
-    here = head.astype(jnp.int32)
-
-    def block(distance):
-        return (here + distance) % head_count
-
-    pieces = {d: from_head(x, d) for d in (2, 1, -1)}
-    partial = project(here[None], [x], weights)
-    sums, text_rows, q2 = lax.optimization_barrier((partial[1], text_rows, q2))
-    partial = (partial[0], sums)
-    far = from_partner(q2[PART:])
-    low = jnp.sum((text_rows < first).astype(jnp.int32))
-    count = jnp.sum((text_rows < first + ROWS).astype(jnp.int32)) - low
+    before = jnp.sum((text_rows < first).astype(jnp.int32))
+    count = jnp.sum((text_rows < first + ROWS).astype(jnp.int32)) - before
     partner = seq_count - 1 - rank
     place = jnp.stack([0, chip, core, partner // 2, partner % 2])
-    text_info = jnp.stack([chip, core, low, count])
-    partial = project(block(2)[None], [pieces[2]], weights, partial)
+    text_info = jnp.stack([chip, core, before, count])
     biases = tuple(b[None, :] for b in (b_query, b_key, b_value))
-    blocks = jnp.stack([block(1), block(-1)])
-    mine2, far, partial, two, ready, place, text_info, blocks = lax.optimization_barrier(
-        (
-            mine2,
-            far,
-            partial,
-            [pieces[1], pieces[-1]],
-            (*biases, cosine, sine),
-            place,
-            text_info,
-            blocks,
-        )
+    partial = project(
+        half_blocks((-1, 0), (1, 1), (-1, 1), (1, 0)),
+        [low_before, high_next, high_before, low_next],
+        weights,
+        partial,
     )
+    last = [pltpu.with_memory_space_constraint(x, pltpu.HBM) for x in (low_far, high_far)]
+    sums, far, text_info, cosine, sine, mine2, last = lax.optimization_barrier(
+        (partial[1], far, text_info, cosine, sine, mine2, last)
+    )
+    partial = (partial[0], sums)
     other2 = from_core(mine2)
-    q3, kv3 = project(blocks, two, weights, partial, ready)
+    q3, kv3 = project(
+        half_blocks((-2, 0), (2, 1)), last, weights, partial, (*biases, cosine, sine)
+    )
     kv3, other2 = lax.optimization_barrier((kv3, other2))
     sums = text_sums(text_info, text_rows, q2, mine2, other2)
 

time: 108 us -> 112 us (1.037)
  waiting for transfers between devices: 4.83 us -> 0.5 us
  other arithmetic: 6.95 us -> 10.2 us
  local copies, waits for them, and re-layouts: 3.91 us -> 5.93 us
  starting transfers between devices: 37.3 us -> 39 us
  Pallas kernels: 52.4 us -> 53.7 us
    ppermute x3 -> x6, starting transfers between devices: 5.14 us -> 8.31 us  [from_head(): lax.ppermute(x, 'head', [((i + distance) % count, i) for i in range(count)])]
    ppermute x2, waiting for transfers between devices: 2.72 us -> 0.46 us  [from_partner(): return lax.ppermute(x, 'seq', [(count - 1 - i, i) for i in range(count)])]
    unnamed x22 -> x24, local copies, waits for them, and re-layouts: 1.27 us -> 3.35 us
    all_to_all x2, starting transfers between devices: 14.6 us -> 13 us  [over_chips(): lax.all_to_all(many, 'seq', 0, 0, axis_index_groups=groups, tiled=True)]
    pallas_call x1, Pallas kernels: 2.58 us -> 4.18 us  [text_sums(): pl.pallas_call(text_kernel, out_shape=(jax.ShapeDtypeStruct((2, tokens //...]
    concatenate x1, other arithmetic: 0.1 us -> 1.71 us  [body(): cosine = jnp.concatenate([cosine, cosine], axis=1)]
    ppermute x3, waiting for transfers between devices: 1.6 us -> 0.01 us  [from_core(): return lax.ppermute(x, 'seq', [(i ^ 1, i) for i in range(count)])]
  transfers between devices with their start and end apart: 13 -> 16, of which waited for: 3 -> 1; matrix products, arithmetic and copies ran while one was open for 4% -> 8% of each run, Pallas kernels for 46% -> 43%
where the time goes in v5:
time: 112 us
  Pallas kernels  53.7 us (48%)
  starting transfers between devices  39 us (35%)
  other arithmetic  10.2 us (9%)
  local copies, waits for them, and re-layouts  5.93 us (5%)
  between operations  2.31 us (2%)
    pallas_call x1, Pallas kernels, attend(): pl.pallas_call(attend_kernel, out_shape=(out, out), in_specs=[smem(), vme...  20.8 us
    pallas_call x3, Pallas kernels, project(): pl.pallas_call(kernel, out_shape=(*(jax.ShapeDtypeStruct(o, kind) if fini...  17.1 us
    all_to_all x2, starting transfers between devices, over_chips(): lax.all_to_all(many, 'seq', 0, 0, axis_index_groups=groups, tiled=True)  13 us
    ppermute x2, starting transfers between devices, from_partner(): return lax.ppermute(x, 'seq', [(count - 1 - i, i) for i in range(count)])  11.5 us
    pallas_call x1, Pallas kernels, attend3(): pl.pallas_call(attend3_kernel, out_shape=jax.ShapeDtypeStruct((SHARE, q3....  10.5 us
    ppermute x6, starting transfers between devices, from_head(): lax.ppermute(x, 'head', [((i + distance) % count, i) for i in range(count)])  8.31 us
    ppermute x3, starting transfers between devices, over_heads(): lax.ppermute(x, 'head', [(i ^ step, i) for i in range(count)])  4.5 us
    pallas_call x1, Pallas kernels, text_sums(): pl.pallas_call(text_kernel, out_shape=(jax.ShapeDtypeStruct((2, tokens //...  4.18 us
  transfers between devices with their start and end apart: 16, of which 1 were waited for; matrix products, arithmetic and copies ran while one was open for 8% of the time, Pallas kernels for 43%

profile of v5, /device:TPU:1, one launch (start us, length us, event | category | flops | bytes accessed | tf_op | source)
XLA Modules:
  0.0 111.6 jit_solution(1056274965253917860)
XLA Ops:
  0.6 0.7 pad_add_fusion.1.info
  1.4 1.2 %copy-done.7 = bf16[256,2048]{1,0:T(8,128)(2,1)S(1)} copy-done((bf16[256,2048]{1,0:T(8,128)(2,1)S(1)}, bf16[256,2048]{1,0:T(8,128)(2,1)}, u32[]{:S(2)}) %copy-start.7) | copy-done | bytes 1048600
  2.6 0.7 copy-done.9
  3.3 1.1 pick_rows.1
  4.4 1.5 %collective-permute-start = (bf16[136,2176]{1,0:T(8,128)(2,1)S(1)}, bf16[136,2176]{1,0:T(8,128)(2,1)}, u32[]{:S(2)}, u32[]{:S(2)}) collective-permute-start(bf16[136,2176]{1,0:T(8,128)(2,1)S(1)} %get-tuple-element.39), channel_id=1, source_target_pairs={{4,0},{0,4},{12,8},{8,12},{20,16},{16,20},{28,24},{24,28},{36,32},... | collective-permute-start | bytes 1775624 | tf_op jit(solution)/shard_map/ppermute | solution.py:462
  5.9 0.9 pad_maximum_fusion.2
  6.8 1.5 %broadcast_in_dim.10 = bf16[16,256,256]{2,1,0:T(8,128)(2,1)} broadcast(bf16[256,256]{1,0:T(8,128)(2,1)S(1)} %pad_maximum_fusion.2), dimensions={1,2} | broadcast | bytes 2228224 | tf_op jit(solution)/shard_map/broadcast_in_dim | solution.py:514
  8.3 6.8 %all-to-all-start = ((bf16[16,256,256]{2,1,0:T(8,128)(2,1)}), bf16[16,256,256]{2,1,0:T(8,128)(2,1)S(1)}, u32[]{:S(2)}, u32[]{:S(2)}) async-start(bf16[16,256,256]{2,1,0:T(8,128)(2,1)} %broadcast_in_dim.10), calls=%async_computation | async-start | bytes 4194304 | tf_op jit(solution)/shard_map/all_to_all | solution.py:473
  15.2 0.1 pad_add_fusion.refs_0_
  15.3 0.1 pad_add_fusion.2.refs_0_
  15.4 0.0 collective-permute-done
  15.4 1.2 %add.82 = bf16[136,2176]{1,0:T(8,128)(2,1)S(1)} add(bf16[136,2176]{1,0:T(8,128)(2,1)S(1)} %get-tuple-element.38, bf16[136,2176]{1,0:T(8,128)(2,1)} %collective-permute-done) | non-fusion elementwise | flops 295936 | bytes 1775616 | tf_op jit(solution)/shard_map/add | solution.py:519
  16.6 0.1 fusion.3
  16.7 1.7 %collective-permute-start.3 = (bf16[136,1024]{1,0:T(8,128)(2,1)S(1)}, bf16[136,1024]{1,0:T(8,128)(2,1)}, u32[]{:S(2)}, u32[]{:S(2)}) collective-permute-start(bf16[136,1024]{1,0:T(8,128)(2,1)S(1)} %get-tuple-element.75.refs_2_), channel_id=1, source_target_pairs={{3,0},{0,1},{1,2},{2,3},{7,4},{4,5},{5,6},{6,7},{11,8},{8,9},{9,10... | collective-permute-start | bytes 835592 | tf_op jit(solution)/shard_map/ppermute | solution.py:467
  18.4 2.2 %collective-permute-start.2 = (bf16[136,1024]{1,0:T(8,128)(2,1)S(1)}, bf16[136,1024]{1,0:T(8,128)(2,1)S(1)}, u32[]{:S(2)}, u32[]{:S(2)}) collective-permute-start(bf16[136,1024]{1,0:T(8,128)(2,1)S(1)} %get-tuple-element.75.refs_2_), channel_id=1, source_target_pairs={{1,0},{2,1},{3,2},{0,3},{5,4},{6,5},{7,6},{4,7},{9,8},{10,9},{11,1... | collective-permute-start | bytes 835592 | tf_op jit(solution)/shard_map/ppermute | solution.py:467
  20.6 1.4 %collective-permute-start.4 = (bf16[136,1024]{1,0:T(8,128)(2,1)S(1)}, bf16[136,1024]{1,0:T(8,128)(2,1)}, u32[]{:S(2)}, u32[]{:S(2)}) collective-permute-start(bf16[136,1024]{1,0:T(8,128)(2,1)S(1)} %get-tuple-element.76.refs_1_), channel_id=1, source_target_pairs={{1,0},{2,1},{3,2},{0,3},{5,4},{6,5},{7,6},{4,7},{9,8},{10,9},{11,1... | collective-permute-start | bytes 835592 | tf_op jit(solution)/shard_map/ppermute | solution.py:467
  22.0 0.1 collective-permute-start.1
  22.0 4.8 %project.3 = (f32[136,1024]{1,0:T(8,128)}, f32[136,256]{1,0:T(8,128)}) custom-call(s32[2]{0:T(128)S(1)} %pad_add_fusion.refs_0_, bf16[136,1024]{1,0:T(8,128)(2,1)S(1)} %get-tuple-element.76.refs_1_, bf16[136,1024]{1,0:T(8,128)(2,1)S(1)} %get-tuple-element.75.refs_2_, bf16[8192,1024]{1,0:T(8,128)(2,1)} %refs_3_.3, bf16[8192,128]{1,0:T(8,128)(2,1)} %refs_4_.3, ...), custom_call_target="tpu_custom_call" | custom-call | flops 713031680 | bytes 5242880 | tf_op jit(solution)/shard_map/project/pallas_call | solution.py:174
  26.9 0.8 fusion.4
  27.7 5.9 %collective-permute-start.5 = (bf16[128,1024]{1,0:T(8,128)(2,1)}, bf16[128,1024]{1,0:T(8,128)(2,1)}, u32[]{:S(2)}, u32[]{:S(2)}) collective-permute-start(bf16[128,1024]{1,0:T(8,128)(2,1)} %get-tuple-element.78), channel_id=1, source_target_pairs={{124,0},{120,4},{116,8},{112,12},{108,16},{104,20},{100,24},{96,28... | collective-permute-start | bytes 786440 | tf_op jit(solution)/shard_map/ppermute | solution.py:485
  33.7 0.2 convert_reduce_fusion
  33.8 1.0 fusion
  34.9 0.7 fusion.1
  36.9 0.0 collective-permute-done.2.refs_2_
  36.9 2.9 %collective-permute-start.7 = (bf16[136,1024]{1,0:T(8,128)(2,1)S(1)}, bf16[136,1024]{1,0:T(8,128)(2,1)S(1)}, u32[]{:S(2)}, u32[]{:S(2)}) collective-permute-start(bf16[136,1024]{1,0:T(8,128)(2,1)S(1)} %collective-permute-done.2.refs_2_), channel_id=1, source_target_pairs={{1,0},{2,1},{3,2},{0,3},{5,4},{6,5},{7,6},{4,7},{9,8},{10,9},{11,1... | collective-permute-start | bytes 835592 | tf_op jit(solution)/shard_map/ppermute | solution.py:467
  39.8 0.0 collective-permute-done.1.refs_1_
  39.8 0.0 collective-permute-start.6
  39.8 0.8 pad_add_fusion.3.info
  40.6 1.7 %pad_maximum_fusion.3 = (f32[136,128]{1,0:T(8,128)S(1)}, f32[136,128]{1,0:T(8,128)}) fusion(f32[136,64]{1,0:T(8,128)} %get-tuple-element.81, f32[136,64]{1,0:T(8,128)} %get-tuple-element.80, f32[136,64]{1,0:T(8,128)} %get-tuple-element.79), kind=kLoop, calls=%fused_computation.5 | loop fusion | flops 34816 | bytes 243712 | tf_op jit(solution)/shard_map/concatenate | solution.py:542
  42.3 0.0 collective-permute-done.4.refs_4_
  42.3 0.0 copy-start.3
  42.3 0.0 copy-start.5
  42.3 0.0 copy-start.6
  42.4 7.2 %project.4 = (f32[136,1024]{1,0:T(8,128)}, f32[136,256]{1,0:T(8,128)}) custom-call(s32[4]{0:T(128)S(1)} %pad_add_fusion.2.refs_0_, bf16[136,1024]{1,0:T(8,128)(2,1)} %collective-permute-done.1.refs_1_, bf16[136,1024]{1,0:T(8,128)(2,1)S(1)} %collective-permute-done.2.refs_2_, bf16[136,1024]{1,0:T(8,128)(2,1)} %collective-permute-done.3.refs_3_, ...), custom_call_target="tpu_custom_call" | custom-call | flops 1426063360 | bytes 10485760 | tf_op jit(solution)/shard_map/project/pallas_call | solution.py:174
  49.5 0.5 collective-permute-done.5.far_ref
  50.0 0.0 collective-permute-done.7.refs_2_
  50.0 0.7 copy-done.10
  50.7 0.0 collective-permute-done.6.refs_1_
  50.7 0.0 all-to-all-done
  50.7 0.0 collective-permute-start.8
  50.7 0.1 pad_add_fusion.4.refs_0_
  50.8 5.1 %project.5 = (bf16[136,1024]{1,0:T(8,128)(2,1)S(1)}, bf16[136,256]{1,0:T(8,128)(2,1)S(1)}) custom-call(s32[2]{0:T(128)S(1)} %pad_add_fusion.4.refs_0_, bf16[136,1024]{1,0:T(8,128)(2,1)} %collective-permute-done.6.refs_1_, bf16[136,1024]{1,0:T(8,128)(2,1)} %copy-done.10, bf16[8192,1024]{1,0:T(8,128)(2,1)} %refs_3_.3, bf16[8192,128]{1,0:T(8,128)(2,1)} %refs_4_.3, ...), custom_call_target="tpu_custom_call" | custom-call | flops 713031680 | bytes 5242880 | tf_op jit(solution)/shard_map/project/pallas_call | solution.py:174
  55.9 0.0 copy-start.8
  55.9 0.7 copy-done.8
  56.6 0.0 collective-permute-done.8.other_hbm.other_ref
  56.6 4.2 %text_sums.1 = (bf16[2,4096]{1,0:T(2,128)(2,1)S(1)}, bf16[2,4096]{1,0:T(2,128)(2,1)S(1)}) custom-call(s32[4]{0:T(128)S(1)} %pad_add_fusion.3.info, s32[256]{0:T(256)S(1)} %copy-done.4, bf16[256,1024]{1,0:T(8,128)(2,1)S(1)} %copy-done, bf16[4096,256]{1,0:T(8,128)(2,1)S(1)} %bitcast.31, bf16[4096,256]{1,0:T(8,128)(2,1)} %collective-permute-done.8.other_hbm.other_ref), custom_call_target="tpu_custom_call" | custom-call | flops 134217728 | bytes 4194304 | tf_op jit(solution)/shard_map/text_sums/pallas_call | solution.py:376
  60.8 0.1 broadcast_in_dim.27
  60.9 1.1 pad_maximum_fusion
  62.0 6.2 %all-to-all-start.1 = ((bf16[16,136,256]{2,1,0:T(8,128)(2,1)}), bf16[16,136,256]{2,1,0:T(8,128)(2,1)S(1)}, u32[]{:S(2)}, u32[]{:S(2)}) async-start(bf16[16,136,256]{2,1,0:T(8,128)(2,1)} %pad_maximum_fusion), calls=%async_computation.1 | async-start | bytes 2228224 | tf_op jit(solution)/shard_map/all_to_all | solution.py:473
  68.2 0.1 stack.72.info
  68.3 20.8 %attend2.1 = (bf16[128,1024]{1,0:T(8,128)(2,1)}, bf16[128,1024]{1,0:T(8,128)(2,1)}) custom-call(s32[5]{0:T(128)S(1)} %stack.72.info, bf16[128,1024]{1,0:T(8,128)(2,1)S(1)} %copy-done.2, bf16[128,1024]{1,0:T(8,128)(2,1)} %collective-permute-done.5.far_ref, bf16[4096,256]{1,0:T(8,128)(2,1)S(1)} %bitcast.32, ...), custom_call_target="tpu_custom_call" | custom-call | flops 4294967296 | bytes 4194304 | tf_op jit(solution)/shard_map/attend2/pallas_call | solution.py:296
  89.2 0.0 all-to-all-done.1
  89.2 0.1 collective-permute-start.9
  89.3 0.1 pad_add_fusion.5.info
  89.3 5.6 %collective-permute-start.10 = (bf16[128,1024]{1,0:T(8,128)(2,1)}, bf16[128,1024]{1,0:T(8,128)(2,1)S(1)}, u32[]{:S(2)}, u32[]{:S(2)}) collective-permute-start(bf16[128,1024]{1,0:T(8,128)(2,1)} %get-tuple-element.66), channel_id=1, source_target_pairs={{124,0},{120,4},{116,8},{112,12},{108,16},{104,20},{100,24},{96,28... | collective-permute-start | bytes 786440 | tf_op jit(solution)/shard_map/ppermute | solution.py:485
  95.0 0.0 collective-permute-done.9
  95.1 3.8 %collective-permute-start.13 = (f32[256]{0:T(256)S(1)}, f32[256]{0:T(256)S(1)}, u32[]{:S(2)}, u32[]{:S(2)}) collective-permute-start(f32[256]{0:T(256)S(1)} %bitcast.42), channel_id=1, source_target_pairs={{3,0},{2,1},{1,2},{0,3},{7,4},{6,5},{5,6},{4,7},{11,8},{10,9},{9,1... | collective-permute-start | bytes 3080 | tf_op jit(solution)/shard_map/ppermute | solution.py:479
  98.9 0.0 collective-permute-start.12
  98.9 0.7 collective-permute-start.11
  99.6 10.5 %attend3.1 = bf16[132,1024]{1,0:T(8,128)(2,1)} custom-call(s32[2]{0:T(128)S(1)} %pad_add_fusion.5.info, bf16[136,1024]{1,0:T(8,128)(2,1)} %copy-done.8, bf16[2176,256]{1,0:T(8,128)(2,1)S(1)} %bitcast.33, bf16[2176,256]{1,0:T(8,128)(2,1)S(1)} %bitcast.38), custom_call_target="tpu_custom_call" | custom-call | flops 3636461568 | bytes 2228224 | tf_op jit(solution)/shard_map/attend3/pallas_call | solution.py:439
  110.1 0.0 collective-permute-done.10
  110.1 0.0 collective-permute-done.11
  110.2 0.8 pad_maximum_fusion.1
  111.0 0.6 add_add_fusion
  (26 shorter events, 0.2 us)
Async XLA Ops:
  1.4 1.2 %copy-start.7 = (bf16[256,2048]{1,0:T(8,128)(2,1)S(1)}, bf16[256,2048]{1,0:T(8,128)(2,1)}, u32[]{:S(2)}) copy-start(bf16[256,2048]{1,0:T(8,128)(2,1)} %hidden_ref.1) | copy-start | bytes 3145732
  2.6 0.7 copy-start.9
  4.4 11.0 %collective-permute-start = (bf16[136,2176]{1,0:T(8,128)(2,1)S(1)}, bf16[136,2176]{1,0:T(8,128)(2,1)}, u32[]{:S(2)}, u32[]{:S(2)}) collective-permute-start(bf16[136,2176]{1,0:T(8,128)(2,1)S(1)} %get-tuple-element.39), channel_id=1, source_target_pairs={{4,0},{0,4},{12,8},{8,12},{20,16},{16,20},{28,24},{24,28},{36,32},... | collective-permute-start | bytes 1775624 | tf_op jit(solution)/shard_map/ppermute | solution.py:462
  8.3 42.4 %all-to-all-start = ((bf16[16,256,256]{2,1,0:T(8,128)(2,1)}), bf16[16,256,256]{2,1,0:T(8,128)(2,1)S(1)}, u32[]{:S(2)}, u32[]{:S(2)}) async-start(bf16[16,256,256]{2,1,0:T(8,128)(2,1)} %broadcast_in_dim.10), calls=%async_computation | async-start | bytes 4194304 | tf_op jit(solution)/shard_map/all_to_all | solution.py:473
  16.7 25.6 %collective-permute-start.3 = (bf16[136,1024]{1,0:T(8,128)(2,1)S(1)}, bf16[136,1024]{1,0:T(8,128)(2,1)}, u32[]{:S(2)}, u32[]{:S(2)}) collective-permute-start(bf16[136,1024]{1,0:T(8,128)(2,1)S(1)} %get-tuple-element.75.refs_2_), channel_id=1, source_target_pairs={{3,0},{0,1},{1,2},{2,3},{7,4},{4,5},{5,6},{6,7},{11,8},{8,9},{9,10... | collective-permute-start | bytes 835592 | tf_op jit(solution)/shard_map/ppermute | solution.py:467
  18.4 18.5 %collective-permute-start.2 = (bf16[136,1024]{1,0:T(8,128)(2,1)S(1)}, bf16[136,1024]{1,0:T(8,128)(2,1)S(1)}, u32[]{:S(2)}, u32[]{:S(2)}) collective-permute-start(bf16[136,1024]{1,0:T(8,128)(2,1)S(1)} %get-tuple-element.75.refs_2_), channel_id=1, source_target_pairs={{1,0},{2,1},{3,2},{0,3},{5,4},{6,5},{7,6},{4,7},{9,8},{10,9},{11,1... | collective-permute-start | bytes 835592 | tf_op jit(solution)/shard_map/ppermute | solution.py:467
  20.6 6.3 %copy-start = (bf16[256,1024]{1,0:T(8,128)(2,1)S(1)}, bf16[256,1024]{1,0:T(8,128)(2,1)}, u32[]{:S(2)}) copy-start(bf16[256,1024]{1,0:T(8,128)(2,1)} %q_ref) | copy-start | bytes 1572868
  20.6 14.3 %copy-start.4 = (s32[256]{0:T(256)S(1)}, s32[256]{0:T(256)}, u32[]{:S(2)}) copy-start(s32[256]{0:T(256)} %text) | copy-start | bytes 3076
  20.6 21.7 %collective-permute-start.4 = (bf16[136,1024]{1,0:T(8,128)(2,1)S(1)}, bf16[136,1024]{1,0:T(8,128)(2,1)}, u32[]{:S(2)}, u32[]{:S(2)}) collective-permute-start(bf16[136,1024]{1,0:T(8,128)(2,1)S(1)} %get-tuple-element.76.refs_1_), channel_id=1, source_target_pairs={{1,0},{2,1},{3,2},{0,3},{5,4},{6,5},{7,6},{4,7},{9,8},{10,9},{11,1... | collective-permute-start | bytes 835592 | tf_op jit(solution)/shard_map/ppermute | solution.py:467
  22.0 17.9 %collective-permute-start.1 = (bf16[136,1024]{1,0:T(8,128)(2,1)S(1)}, bf16[136,1024]{1,0:T(8,128)(2,1)}, u32[]{:S(2)}, u32[]{:S(2)}) collective-permute-start(bf16[136,1024]{1,0:T(8,128)(2,1)S(1)} %get-tuple-element.76.refs_1_), channel_id=1, source_target_pairs={{3,0},{0,1},{1,2},{2,3},{7,4},{4,5},{5,6},{6,7},{11,8},{8,9},{9,10... | collective-permute-start | bytes 835592 | tf_op jit(solution)/shard_map/ppermute | solution.py:467
  27.7 22.2 %collective-permute-start.5 = (bf16[128,1024]{1,0:T(8,128)(2,1)}, bf16[128,1024]{1,0:T(8,128)(2,1)}, u32[]{:S(2)}, u32[]{:S(2)}) collective-permute-start(bf16[128,1024]{1,0:T(8,128)(2,1)} %get-tuple-element.78), channel_id=1, source_target_pairs={{124,0},{120,4},{116,8},{112,12},{108,16},{104,20},{100,24},{96,28... | collective-permute-start | bytes 786440 | tf_op jit(solution)/shard_map/ppermute | solution.py:485
  36.9 13.1 %collective-permute-start.7 = (bf16[136,1024]{1,0:T(8,128)(2,1)S(1)}, bf16[136,1024]{1,0:T(8,128)(2,1)S(1)}, u32[]{:S(2)}, u32[]{:S(2)}) collective-permute-start(bf16[136,1024]{1,0:T(8,128)(2,1)S(1)} %collective-permute-done.2.refs_2_), channel_id=1, source_target_pairs={{1,0},{2,1},{3,2},{0,3},{5,4},{6,5},{7,6},{4,7},{9,8},{10,9},{11,1... | collective-permute-start | bytes 835592 | tf_op jit(solution)/shard_map/ppermute | solution.py:467
  39.8 10.9 %collective-permute-start.6 = (bf16[136,1024]{1,0:T(8,128)(2,1)}, bf16[136,1024]{1,0:T(8,128)(2,1)}, u32[]{:S(2)}, u32[]{:S(2)}) collective-permute-start(bf16[136,1024]{1,0:T(8,128)(2,1)} %collective-permute-done.1.refs_1_), channel_id=1, source_target_pairs={{3,0},{0,1},{1,2},{2,3},{7,4},{4,5},{5,6},{6,7},{11,8},{8,9},{9,10... | collective-permute-start | bytes 835592 | tf_op jit(solution)/shard_map/ppermute | solution.py:467
  42.3 8.5 %copy-start.1 = (f32[136,128]{1,0:T(8,128)S(1)}, f32[136,128]{1,0:T(8,128)}, u32[]{:S(2)}) copy-start(f32[136,128]{1,0:T(8,128)} %get-tuple-element.53.refs_12_) | copy-start | bytes 208900
  42.3 8.5 %copy-start.3 = (f32[1024]{0:T(1024)S(1)}, f32[1024]{0:T(1024)}, u32[]{:S(2)}) copy-start(f32[1024]{0:T(1024)} %param.18) | copy-start | bytes 12292
  42.3 8.5 %copy-start.5 = (f32[128]{0:T(128)S(1)}, f32[128]{0:T(128)}, u32[]{:S(2)}) copy-start(f32[128]{0:T(128)} %param.20) | copy-start | bytes 1540
  42.3 8.5 %copy-start.6 = (f32[128]{0:T(128)S(1)}, f32[128]{0:T(128)}, u32[]{:S(2)}) copy-start(f32[128]{0:T(128)} %param.22) | copy-start | bytes 1540
  50.0 0.7 copy-start.10
  50.7 6.0 %collective-permute-start.8 = (bf16[4096,256]{1,0:T(8,128)(2,1)S(1)}, bf16[4096,256]{1,0:T(8,128)(2,1)}, u32[]{:S(2)}, u32[]{:S(2)}) collective-permute-start(bf16[4096,256]{1,0:T(8,128)(2,1)S(1)} %bitcast.30), channel_id=1, source_target_pairs={{4,0},{0,4},{12,8},{8,12},{20,16},{16,20},{28,24},{24,28},{36,32},... | collective-permute-start | bytes 6291464 | tf_op jit(solution)/shard_map/ppermute | solution.py:462
  55.9 0.7 copy-start.8
  60.9 7.4 %copy-start.2 = (bf16[128,1024]{1,0:T(8,128)(2,1)S(1)}, bf16[128,1024]{1,0:T(8,128)(2,1)}, u32[]{:S(2)}) copy-start(bf16[128,1024]{1,0:T(8,128)(2,1)} %get-tuple-element.77.own_ref) | copy-start | bytes 786436
  62.0 27.1 %all-to-all-start.1 = ((bf16[16,136,256]{2,1,0:T(8,128)(2,1)}), bf16[16,136,256]{2,1,0:T(8,128)(2,1)S(1)}, u32[]{:S(2)}, u32[]{:S(2)}) async-start(bf16[16,136,256]{2,1,0:T(8,128)(2,1)} %pad_maximum_fusion), calls=%async_computation.1 | async-start | bytes 2228224 | tf_op jit(solution)/shard_map/all_to_all | solution.py:473
  89.2 5.8 %collective-permute-start.9 = (bf16[16,136,256]{2,1,0:T(8,128)(2,1)S(1)}, bf16[16,136,256]{2,1,0:T(8,128)(2,1)S(1)}, u32[]{:S(2)}, u32[]{:S(2)}) collective-permute-start(bf16[16,136,256]{2,1,0:T(8,128)(2,1)S(1)} %all-to-all-done.1), channel_id=1, source_target_pairs={{4,0},{0,4},{12,8},{8,12},{20,16},{16,20},{28,24},{24,28},{36,32},... | collective-permute-start | bytes 3342344 | tf_op jit(solution)/shard_map/ppermute | solution.py:462
  89.3 20.8 %collective-permute-start.10 = (bf16[128,1024]{1,0:T(8,128)(2,1)}, bf16[128,1024]{1,0:T(8,128)(2,1)S(1)}, u32[]{:S(2)}, u32[]{:S(2)}) collective-permute-start(bf16[128,1024]{1,0:T(8,128)(2,1)} %get-tuple-element.66), channel_id=1, source_target_pairs={{124,0},{120,4},{116,8},{112,12},{108,16},{104,20},{100,24},{96,28... | collective-permute-start | bytes 786440 | tf_op jit(solution)/shard_map/ppermute | solution.py:485
  95.1 15.1 %collective-permute-start.13 = (f32[256]{0:T(256)S(1)}, f32[256]{0:T(256)S(1)}, u32[]{:S(2)}, u32[]{:S(2)}) collective-permute-start(f32[256]{0:T(256)S(1)} %bitcast.42), channel_id=1, source_target_pairs={{3,0},{2,1},{1,2},{0,3},{7,4},{6,5},{5,6},{4,7},{11,8},{10,9},{9,1... | collective-permute-start | bytes 3080 | tf_op jit(solution)/shard_map/ppermute | solution.py:479
  98.9 11.2 %collective-permute-start.12 = (f32[256]{0:T(256)S(1)}, f32[256]{0:T(256)S(1)}, u32[]{:S(2)}, u32[]{:S(2)}) collective-permute-start(f32[256]{0:T(256)S(1)} %bitcast.43), channel_id=1, source_target_pairs={{2,0},{3,1},{0,2},{1,3},{6,4},{7,5},{4,6},{5,7},{10,8},{11,9},{8,1... | collective-permute-start | bytes 3080 | tf_op jit(solution)/shard_map/ppermute | solution.py:479
  98.9 11.2 %collective-permute-start.11 = (f32[256]{0:T(256)S(1)}, f32[256]{0:T(256)S(1)}, u32[]{:S(2)}, u32[]{:S(2)}) collective-permute-start(f32[256]{0:T(256)S(1)} %bitcast.44), channel_id=1, source_target_pairs={{1,0},{0,1},{3,2},{2,3},{5,4},{4,5},{7,6},{6,7},{9,8},{8,9},{11,10... | collective-permute-start | bytes 3080 | tf_op jit(solution)/shard_map/ppermute | solution.py:479
  99.6 10.6 %copy-start.11 = (bf16[128,1024]{1,0:T(8,128)(2,1)S(1)}, bf16[128,1024]{1,0:T(8,128)(2,1)}, u32[]{:S(2)}) copy-start(bf16[128,1024]{1,0:T(8,128)(2,1)} %get-tuple-element.62) | copy-start | bytes 786436

commit v6 on v5

--- a/solution.py
+++ b/solution.py
@@ -37,8 +37,10 @@
     return pl.BlockSpec(memory_space=pltpu.SMEM)
 
 
-def pick_kernel(info, index_ref, hidden_ref, own_ref, send_ref):
-    core, first, before, live0, live1 = (info[i] for i in range(5))
+def pick_kernel(counts, index_ref, hidden_ref, own_ref, send_ref):
+    rank = lax.axis_index("seq")
+    core, first = (rank % 2, rank * ROWS)
+    live0, live1 = (counts[0], counts[1])
     count = live0 + live1
     start = jnp.where(core == 0, 0, 2 * SHARE - count)
     lane = lax.broadcasted_iota(jnp.int32, (PAD, ROWS), 1)
@@ -62,7 +64,7 @@
         out_ref[:, hidden_ref.shape[1] :] = marks.astype(F32).astype(BF)
 
 
-def pick_rows(info, kept_index, hidden):
+def pick_rows(block_count, kept_index, hidden):
     width = hidden.shape[1] + BLOCK
     shape = jax.ShapeDtypeStruct((PAD, width), BF)
     return pl.pallas_call(
@@ -75,7 +77,7 @@
             flops=4 * PAD * ROWS * width, transcendentals=0, bytes_accessed=4 * ROWS * width
         ),
         name="pick_rows",
-    )(info, kept_index.reshape(1, ROWS), hidden)
+    )(block_count, kept_index.reshape(1, ROWS), hidden)
 
 
 def rotated(u, cosine, sine):
@@ -85,7 +87,9 @@
 STEP = 1024
 
 
-def project_kernel(pieces, first, last, blocks, *refs):
+def project_kernel(places, first, last, *refs):
+    pieces = len(places)
+    here, heads = (lax.axis_index("head"), lax.axis_size("head"))
     x_refs = refs[:pieces]
     weights = refs[pieces : pieces + 3]
     rest = refs[pieces + 3 :]
@@ -110,7 +114,9 @@
     for p in range(pieces):
         for part in range(depth // STEP):
             at = len(copies) * STEP
-            start = pl.multiple_of(blocks[p] * depth + part * STEP, STEP)
+            distance, side = places[p]
+            block = 2 * ((here + heads + distance) % heads) + side
+            start = pl.multiple_of(block * depth + part * STEP, STEP)
             copies.append(
                 [
                     pltpu.make_async_copy(
@@ -157,7 +163,7 @@
         copy.wait()
 
 
-def project(blocks, xs, weights, partial=(), finish=()):
+def project(places, xs, weights, partial=(), finish=()):
     pieces = len(xs)
     depth = xs[0].shape[1]
     widths = [w.shape[1] for w in weights]
@@ -168,7 +174,7 @@
     partial = [pltpu.with_memory_space_constraint(part, pltpu.HBM) for part in partial]
 
     def kernel(*refs):
-        project_kernel(pieces, not partial, bool(finish), *refs)
+        project_kernel(places, not partial, bool(finish), *refs)
 
     outs = ((PAD, widths[0]), (PAD, 2 * HD))
     return pl.pallas_call(
@@ -176,8 +182,7 @@
         out_shape=(
             *(jax.ShapeDtypeStruct(o, kind) if finish else pltpu.HBM(o, kind) for o in outs),
         ),
-        in_specs=[smem()]
-        + [vmem] * pieces
+        in_specs=[vmem] * pieces
         + [hbm] * (3 + len(partial))
         + [vmem] * len(finish),
         out_specs=(vmem, vmem) if finish else (hbm, hbm),
@@ -196,7 +201,7 @@
             bytes_accessed=2 * pieces * depth * sum(widths),
         ),
         name="project",
-    )(blocks, *xs, *weights, *partial, *finish)
+    )(*xs, *weights, *partial, *finish)
 
 
 def in_turn(heads, scored, weighed):
@@ -208,11 +213,13 @@
         weighed(h, scores)
 
 
-def attend_kernel(info, own_ref, far_ref, mine_ref, other_ref, *refs):
+def attend_kernel(own_ref, far_ref, mine_ref, other_ref, *refs):
+    rank = lax.axis_index("seq")
+    partner = lax.axis_size("seq") - 1 - rank
     own_to, far_to, q_s, top_s, sum_s, v_s, bias_s, other_s, own_out, far_out, sems = refs
     fetch = pltpu.make_async_copy(other_ref, other_s, sems.at[0])
     fetch.start()
-    core = info[2]
+    core = rank % 2
     half = mine_ref.shape[0]
     pairs = GROUP // 2
     for g, ref in enumerate((own_ref, far_ref)):
@@ -253,7 +260,8 @@
         in_turn(range(pairs), scored, weighed)
 
     def group(g, carry):
-        chip, side = info[2 * g + 1], info[2 * g + 2]
+        place = jnp.where(g == 0, rank, partner)
+        chip, side = (place // 2, place % 2)
         for p, ref in enumerate((mine_ref, other_s)):
             parity = core if p == 0 else 1 - core
             same = jnp.where(parity == side, 1, 0)
@@ -287,7 +295,7 @@
         copy.wait()
 
 
-def attend(info, own, far, mine, other):
+def attend(own, far, mine, other):
     tokens = 2 * mine.shape[0]
     vmem = pl.BlockSpec(memory_space=pltpu.VMEM)
     hbm = pl.BlockSpec(memory_space=pl.ANY)
@@ -296,7 +304,7 @@
     return pl.pallas_call(
         attend_kernel,
         out_shape=(out, out),
-        in_specs=[smem(), vmem, vmem, vmem, hbm],
+        in_specs=[vmem, vmem, vmem, hbm],
         out_specs=(hbm, hbm),
         scratch_shapes=[
             pltpu.VMEM((2, GROUP // 2, 2 * PART, HD), BF),
@@ -316,15 +324,18 @@
             bytes_accessed=4 * tokens * HD,
         ),
         name="attend2",
-    )(info, own, far, mine, other)
+    )(own, far, mine, other)
 
 
 CHUNK = 8
 
 
-def text_kernel(info, text, q_ref, mine_ref, other_hbm, high_ref, low_ref, out_ref, other_ref, sem):
-    chip, core, low, count = (info[i] for i in range(4))
-    first = (2 * chip + core) * ROWS
+def text_kernel(text, rows_ref, q_ref, mine_ref, other_hbm, high_ref, low_ref, out_ref, other_ref, sem):
+    rank = lax.axis_index("seq")
+    core, first = (rank % 2, rank * ROWS)
+    before = jnp.where(rows_ref[...] < first, 1.0, 0.0)
+    within = jnp.where(rows_ref[...] < first + ROWS, 1.0, 0.0) - before
+    low, count = (jnp.sum(x).astype(jnp.int32) for x in (before, within))
     half = mine_ref.shape[0]
     fetch = pltpu.make_async_copy(other_hbm, other_ref, sem)
     fetch.start()
@@ -370,13 +381,13 @@
         low_ref[p : p + 1, :] = (x - high.astype(F32)).astype(BF)
 
 
-def text_sums(info, text_rows, q2, mine, other):
+def text_sums(text_rows, q2, mine, other):
     tokens = 2 * mine.shape[0]
     vmem = pl.BlockSpec(memory_space=pltpu.VMEM)
     return pl.pallas_call(
         text_kernel,
         out_shape=(jax.ShapeDtypeStruct((2, tokens // 2), BF),) * 2,
-        in_specs=[smem(), smem(), vmem, vmem, pl.BlockSpec(memory_space=pl.ANY)],
+        in_specs=[smem(), vmem, vmem, vmem, pl.BlockSpec(memory_space=pl.ANY)],
         out_specs=(vmem, vmem),
         scratch_shapes=[
             pltpu.VMEM((2, tokens // 2), F32),
@@ -390,13 +401,14 @@
             bytes_accessed=4 * tokens * HD,
         ),
         name="text_sums",
-    )(info, text_rows, q2, mine, other)
-
-
-def attend3_kernel(info, q_hbm, mine_ref, other_ref, out_ref, v_s, bias_s, q_ref, sem):
+    )(text_rows, text_rows.reshape(1, -1), q2, mine, other)
+
+
+def attend3_kernel(q_hbm, mine_ref, other_ref, out_ref, v_s, bias_s, q_ref, sem):
     fetch = pltpu.make_async_copy(q_hbm, q_ref, sem)
     fetch.start()
-    chip, core = info[0], info[1]
+    rank = lax.axis_index("seq")
+    chip, core = (rank // 2, rank % 2)
     half = mine_ref.shape[0]
     v_s[:half, :HD] = mine_ref[:, HD:]
     v_s[half:, :HD] = other_ref[:, HD:]
@@ -432,14 +444,14 @@
     in_turn(range(GROUP), scored, weighed)
 
 
-def attend3(info, q3, mine, other):
+def attend3(q3, mine, other):
     vmem = pl.BlockSpec(memory_space=pltpu.VMEM)
     keys = 2 * mine.shape[0]
     q3 = pltpu.with_memory_space_constraint(q3, pltpu.HBM)
     return pl.pallas_call(
         attend3_kernel,
         out_shape=jax.ShapeDtypeStruct((SHARE, q3.shape[1]), BF),
-        in_specs=[smem(), pl.BlockSpec(memory_space=pl.ANY), vmem, vmem],
+        in_specs=[pl.BlockSpec(memory_space=pl.ANY), vmem, vmem],
         out_specs=vmem,
         scratch_shapes=[
             pltpu.VMEM((keys, 2 * HD), BF),
@@ -454,7 +466,7 @@
             bytes_accessed=4 * keys * HD,
         ),
         name="attend3",
-    )(info, q3, mine, other)
+    )(q3, mine, other)
 
 
 def from_core(x):
@@ -500,13 +512,8 @@
     block_count,
     text_rows,
 ):
-    rank = lax.axis_index("seq")
-    head = lax.axis_index("head")
     seq_count = lax.axis_size("seq")
     head_count = lax.axis_size("head")
-    core = rank % 2
-    chip = rank // 2
-    first = rank * ROWS
     depth = hidden.shape[1]
 
     chips = seq_count // 2
@@ -514,71 +521,58 @@
     mine2 = over_chips(jnp.broadcast_to(kv2[None], (chips, *kv2.shape)))
     mine2 = mine2.reshape(-1, 2 * HD)
 
-    numbers = jnp.stack([core, first, 0, block_count[0], block_count[1]])
-    own, sent = pick_rows(numbers, kept_index, hidden)
+    own, sent = pick_rows(block_count, kept_index, hidden)
     x = own + from_core(sent)
     marks = x[:, depth : depth + 2].astype(jnp.int32)
     half = depth // 2
     low, high = (x[:, :half], x[:, half:depth])
-
     weights = (w_query, w_key, w_value)
-    here = head.astype(jnp.int32)
-
-    def half_blocks(*pieces):
-        return jnp.stack([2 * ((here + d) % head_count) + side for d, side in pieces])
 
     low_before, high_next = (from_head(low, -1), from_head(high, 1))
     high_before, low_next = (from_head(high, -1), from_head(low, 1))
-    partial = project(half_blocks((0, 0), (0, 1)), [low, high], weights)
+    partial = project([(0, 0), (0, 1)], [low, high], weights)
     low_far, high_far = (from_head(low_before, -1), from_head(high_next, 1))
 
-    sums, marks, text_rows, q2 = lax.optimization_barrier((partial[1], marks, text_rows, q2))
+    sums, marks, far = lax.optimization_barrier((partial[1], marks, q2[PART:]))
     partial = (partial[0], sums)
-    far = from_partner(q2[PART:])
     positions = marks[:, 0] * 128 + marks[:, 1]
-    freqs = 1000000.0 ** (-(jnp.arange(HD // 2, dtype=F32) * 2.0) / HD)
+    lane = jnp.arange(HD, dtype=jnp.int32)
+    freqs = 1000000.0 ** (-((lane % (HD // 2)).astype(F32) * 2.0) / HD)
     angles = positions.astype(F32)[:, None] * freqs[None, :]
-    cosine, sine = (jnp.cos(angles), jnp.sin(angles))
-    cosine = jnp.concatenate([cosine, cosine], axis=1)
-    sine = jnp.concatenate([-sine, sine], axis=1)
-    before = jnp.sum((text_rows < first).astype(jnp.int32))
-    count = jnp.sum((text_rows < first + ROWS).astype(jnp.int32)) - before
-    partner = seq_count - 1 - rank
-    place = jnp.stack([0, chip, core, partner // 2, partner % 2])
-    text_info = jnp.stack([chip, core, before, count])
+    cosine = jnp.cos(angles)
+    sine = jnp.sin(angles) * jnp.where(lane < HD // 2, -1.0, 1.0)[None, :]
     biases = tuple(b[None, :] for b in (b_query, b_key, b_value))
     partial = project(
-        half_blocks((-1, 0), (1, 1), (-1, 1), (1, 0)),
+        [(-1, 0), (1, 1), (-1, 1), (1, 0)],
         [low_before, high_next, high_before, low_next],
         weights,
         partial,
     )
     last = [pltpu.with_memory_space_constraint(x, pltpu.HBM) for x in (low_far, high_far)]
-    sums, far, text_info, cosine, sine, mine2, last = lax.optimization_barrier(
-        (partial[1], far, text_info, cosine, sine, mine2, last)
+    sums, far, cosine, sine, mine2, last = lax.optimization_barrier(
+        (partial[1], far, cosine, sine, mine2, last)
     )
     partial = (partial[0], sums)
     other2 = from_core(mine2)
-    q3, kv3 = project(
-        half_blocks((-2, 0), (2, 1)), last, weights, partial, (*biases, cosine, sine)
-    )
-    kv3, other2 = lax.optimization_barrier((kv3, other2))
-    sums = text_sums(text_info, text_rows, q2, mine2, other2)
+    far = from_partner(far)
+    q3, kv3 = project([(-2, 0), (2, 1)], last, weights, partial, (*biases, cosine, sine))
+    kv3, other2, far = lax.optimization_barrier((kv3, other2, far))
+    sums = text_sums(text_rows, q2, mine2, other2)
 
     sums = [part.reshape(2, chips, ROWS).swapaxes(0, 1) for part in sums]
     kept = jnp.broadcast_to(kv3[None, :SHARE], (chips, SHARE, 2 * HD))
     many = jnp.concatenate([kept, *sums], axis=1)
     mine = over_chips(many)
     far, many = lax.optimization_barrier((far, many))
-    near, far = attend(place, q2[:PART], far, mine2, other2)
+    near, far = attend(q2[:PART], far, mine2, other2)
     far, mine = lax.optimization_barrier((far, mine))
     other = from_core(mine)
     far = from_partner(far)
 
     got = sum(jnp.sum(x[:, SHARE:].astype(F32), axis=0) for x in (mine, other))
     got = got[:2] + got[2:]
-    got = over_heads(jnp.where(core == 0, got[0], got[1]))
-    attn3 = attend3(place[1:3], q3, mine.reshape(-1, 2 * HD), other.reshape(-1, 2 * HD))
+    got = over_heads(jnp.where(lax.axis_index("seq") % 2 == 0, got[0], got[1]))
+    attn3 = attend3(q3, mine.reshape(-1, 2 * HD), other.reshape(-1, 2 * HD))
     attn3, far, *got = lax.optimization_barrier((attn3, far, *got))
     attn2 = jnp.concatenate([near, far], axis=0)
     tokens = seq_count * ROWS

time: 112 us -> 110 us (0.982)
  waiting for transfers between devices: 0.5 us -> 10.1 us
  other arithmetic: 10.2 us -> 4.18 us
  Pallas kernels: 53.7 us -> 49 us
  starting transfers between devices: 39 us -> 40.6 us
  between operations: 2.31 us -> 1 us
  local copies, waits for them, and re-layouts: 5.93 us -> 4.65 us
    ppermute x6, waiting for transfers between devices: 0.02 us -> 7.53 us  [from_head(): lax.ppermute(x, 'head', [((i + distance) % count, i) for i in range(count)])]
    another operation x6 -> x0, other arithmetic: 1.81 us -> none  [the longest x1 0.77 us: body(): text_info = jnp.stack([chip, core, before, count])]
    pallas_call x3, Pallas kernels: 17.1 us -> 15.3 us  [project(): pl.pallas_call(kernel, out_shape=(*(jax.ShapeDtypeStruct(o, kind) if fini...]
    ppermute x3, starting transfers between devices: 1.59 us -> 3.3 us  [from_core(): return lax.ppermute(x, 'seq', [(i ^ 1, i) for i in range(count)])]
    concatenate x1 -> x0, other arithmetic: 1.71 us -> none  [body(): cosine = jnp.concatenate([cosine, cosine], axis=1)]
    pallas_call x1, Pallas kernels: 4.18 us -> 2.69 us  [text_sums(): pl.pallas_call(text_kernel, out_shape=(jax.ShapeDtypeStruct((2, tokens //...]
    ppermute x2, starting transfers between devices: 11.5 us -> 10.3 us  [from_partner(): return lax.ppermute(x, 'seq', [(count - 1 - i, i) for i in range(count)])]
    ppermute x2, waiting for transfers between devices: 0.46 us -> 1.66 us  [from_partner(): return lax.ppermute(x, 'seq', [(count - 1 - i, i) for i in range(count)])]
  transfers between devices with their start and end apart: 16 -> 16, of which waited for: 1 -> 3; matrix products, arithmetic and copies ran while one was open for 8% -> 1% of each run, Pallas kernels for 43% -> 42%
where the time goes in v6:
time: 110 us
  Pallas kernels  49 us (45%)
  starting transfers between devices  40.6 us (37%)
  waiting for transfers between devices  10.1 us (9%)
  local copies, waits for them, and re-layouts  4.65 us (4%)
  other arithmetic  4.18 us (4%)
    pallas_call x1, Pallas kernels, attend(): pl.pallas_call(attend_kernel, out_shape=(out, out), in_specs=[vmem, vmem,...  19.9 us
    pallas_call x3, Pallas kernels, project(): pl.pallas_call(kernel, out_shape=(*(jax.ShapeDtypeStruct(o, kind) if fini...  15.3 us
    all_to_all x2, starting transfers between devices, over_chips(): lax.all_to_all(many, 'seq', 0, 0, axis_index_groups=groups, tiled=True)  13.9 us
    ppermute x2, starting transfers between devices, from_partner(): return lax.ppermute(x, 'seq', [(count - 1 - i, i) for i in range(count)])  10.3 us
    pallas_call x1, Pallas kernels, attend3(): pl.pallas_call(attend3_kernel, out_shape=jax.ShapeDtypeStruct((SHARE, q3....  10 us
    ppermute x6, starting transfers between devices, from_head(): lax.ppermute(x, 'head', [((i + distance) % count, i) for i in range(count)])  9.21 us
    ppermute x6, waiting for transfers between devices, from_head(): lax.ppermute(x, 'head', [((i + distance) % count, i) for i in range(count)])  7.53 us
    ppermute x3, starting transfers between devices, over_heads(): lax.ppermute(x, 'head', [(i ^ step, i) for i in range(count)])  3.93 us
  transfers between devices with their start and end apart: 16, of which 3 were waited for; matrix products, arithmetic and copies ran while one was open for 1% of the time, Pallas kernels for 42%

profile of v6, /device:TPU:1, one launch (start us, length us, event | category | flops | bytes accessed | tf_op | source)
XLA Modules:
  0.0 109.5 jit_solution(18189825867587885598)
XLA Ops:
  0.6 0.9 pad_maximum_fusion.2
  1.5 1.6 %broadcast_in_dim.34 = bf16[16,256,256]{2,1,0:T(8,128)(2,1)} broadcast(bf16[256,256]{1,0:T(8,128)(2,1)S(1)} %pad_maximum_fusion.2), dimensions={1,2} | broadcast | bytes 2228224 | tf_op jit(solution)/shard_map/broadcast_in_dim | solution.py:521
  3.1 7.7 %all-to-all-start = ((bf16[16,256,256]{2,1,0:T(8,128)(2,1)}), bf16[16,256,256]{2,1,0:T(8,128)(2,1)S(1)}, u32[]{:S(2)}, u32[]{:S(2)}) async-start(bf16[16,256,256]{2,1,0:T(8,128)(2,1)} %broadcast_in_dim.34), calls=%async_computation | async-start | bytes 4194304 | tf_op jit(solution)/shard_map/all_to_all | solution.py:485
  10.8 0.0 copy-done.10
  10.8 0.0 copy-done.11
  10.8 0.0 copy-start.6
  10.8 1.2 %copy-done.6 = bf16[256,2048]{1,0:T(8,128)(2,1)S(1)} copy-done((bf16[256,2048]{1,0:T(8,128)(2,1)S(1)}, bf16[256,2048]{1,0:T(8,128)(2,1)}, u32[]{:S(2)}) %copy-start.6) | copy-done | bytes 1048600
  12.1 1.1 pick_rows.1
  13.2 1.0 collective-permute-start
  14.2 0.7 fusion.7
  14.9 0.9 collective-permute-done
  15.8 0.2 add.36
  16.0 0.1 fusion.6
  16.1 3.8 %collective-permute-start.2 = (bf16[136,1024]{1,0:T(8,128)(2,1)S(1)}, bf16[136,1024]{1,0:T(8,128)(2,1)S(1)}, u32[]{:S(2)}, u32[]{:S(2)}) collective-permute-start(bf16[136,1024]{1,0:T(8,128)(2,1)S(1)} %get-tuple-element.71.refs_1_), channel_id=1, source_target_pairs={{1,0},{2,1},{3,2},{0,3},{5,4},{6,5},{7,6},{4,7},{9,8},{10,9},{11,1... | collective-permute-start | bytes 835592 | tf_op jit(solution)/shard_map/ppermute | solution.py:479
  19.9 0.0 collective-permute-start.3
  19.9 0.0 collective-permute-start.1
  19.9 2.7 %collective-permute-start.4 = (bf16[136,1024]{1,0:T(8,128)(2,1)S(1)}, bf16[136,1024]{1,0:T(8,128)(2,1)S(1)}, u32[]{:S(2)}, u32[]{:S(2)}) collective-permute-start(bf16[136,1024]{1,0:T(8,128)(2,1)S(1)} %get-tuple-element.72.refs_0_), channel_id=1, source_target_pairs={{1,0},{2,1},{3,2},{0,3},{5,4},{6,5},{7,6},{4,7},{9,8},{10,9},{11,1... | collective-permute-start | bytes 835592 | tf_op jit(solution)/shard_map/ppermute | solution.py:479
  22.6 4.3 %project.3 = (f32[136,1024]{1,0:T(8,128)}, f32[136,256]{1,0:T(8,128)}) custom-call(bf16[136,1024]{1,0:T(8,128)(2,1)S(1)} %get-tuple-element.72.refs_0_, bf16[136,1024]{1,0:T(8,128)(2,1)S(1)} %get-tuple-element.71.refs_1_, bf16[8192,1024]{1,0:T(8,128)(2,1)} %refs_2_.3, bf16[8192,128]{1,0:T(8,128)(2,1)} %refs_3_.3, bf16[8192,128]{1,0:T(8,128)(2,1)} %refs_4_.5), custom_call_target="tpu_custom_call" | custom-call | flops 713031680 | bytes 5242880 | tf_op jit(solution)/shard_map/project/pallas_call | solution.py:180
  26.9 0.2 convert_reduce_fusion
  27.1 7.5 %collective-permute-done.1.refs_0_ = bf16[136,1024]{1,0:T(8,128)(2,1)S(1)} collective-permute-done((bf16[136,1024]{1,0:T(8,128)(2,1)S(1)}, bf16[136,1024]{1,0:T(8,128)(2,1)S(1)}, u32[]{:S(2)}, u32[]{:S(2)}) %collective-permute-start.1) | collective-permute-done | bytes 278560 | tf_op jit(solution)/shard_map/ppermute | solution.py:479
  34.6 0.0 collective-permute-start.5
  34.6 0.0 collective-permute-done.2.refs_1_
  34.6 2.7 %collective-permute-start.6 = (bf16[136,1024]{1,0:T(8,128)(2,1)S(1)}, bf16[136,1024]{1,0:T(8,128)(2,1)}, u32[]{:S(2)}, u32[]{:S(2)}) collective-permute-start(bf16[136,1024]{1,0:T(8,128)(2,1)S(1)} %collective-permute-done.2.refs_1_), channel_id=1, source_target_pairs={{1,0},{2,1},{3,2},{0,3},{5,4},{6,5},{7,6},{4,7},{9,8},{10,9},{11,1... | collective-permute-start | bytes 835592 | tf_op jit(solution)/shard_map/ppermute | solution.py:479
  37.3 0.3 fusion
  37.6 0.0 collective-permute-done.3.refs_2_
  37.7 0.0 collective-permute-done.4.refs_3_
  37.7 0.0 copy-start.2
  37.7 0.0 copy-start.4
  37.7 0.0 copy-start.5
  37.7 5.9 %project.4 = (f32[136,1024]{1,0:T(8,128)}, f32[136,256]{1,0:T(8,128)}) custom-call(bf16[136,1024]{1,0:T(8,128)(2,1)S(1)} %collective-permute-done.1.refs_0_, bf16[136,1024]{1,0:T(8,128)(2,1)S(1)} %collective-permute-done.2.refs_1_, bf16[136,1024]{1,0:T(8,128)(2,1)S(1)} %collective-permute-done.3.refs_2_, ...), custom_call_target="tpu_custom_call" | custom-call | flops 1426063360 | bytes 10485760 | tf_op jit(solution)/shard_map/project/pallas_call | solution.py:180
  43.6 0.0 collective-permute-done.5.refs_0_
  43.7 0.0 copy-start.12
  43.7 0.0 collective-permute-done.6.refs_1_
  43.7 0.0 all-to-all-done
  43.7 2.2 %collective-permute-start.7 = (bf16[4096,256]{1,0:T(8,128)(2,1)S(1)}, bf16[4096,256]{1,0:T(8,128)(2,1)S(1)}, u32[]{:S(2)}, u32[]{:S(2)}) collective-permute-start(bf16[4096,256]{1,0:T(8,128)(2,1)S(1)} %bitcast.16), channel_id=1, source_target_pairs={{4,0},{0,4},{12,8},{8,12},{20,16},{16,20},{28,24},{24,28},{36,32},... | collective-permute-start | bytes 6291464 | tf_op jit(solution)/shard_map/ppermute | solution.py:474
  45.9 4.9 %collective-permute-start.8 = (bf16[128,1024]{1,0:T(8,128)(2,1)}, bf16[128,1024]{1,0:T(8,128)(2,1)S(1)}, u32[]{:S(2)}, u32[]{:S(2)}) collective-permute-start(bf16[128,1024]{1,0:T(8,128)(2,1)} %get-tuple-element.53), channel_id=1, source_target_pairs={{124,0},{120,4},{116,8},{112,12},{108,16},{104,20},{100,24},{96,28... | collective-permute-start | bytes 786440 | tf_op jit(solution)/shard_map/ppermute | solution.py:497
  50.8 0.0 copy-done.5
  50.8 0.0 copy-start.3
  50.8 5.1 %project.5 = (bf16[136,1024]{1,0:T(8,128)(2,1)S(1)}, bf16[136,256]{1,0:T(8,128)(2,1)S(1)}) custom-call(bf16[136,1024]{1,0:T(8,128)(2,1)} %copy-done.12, bf16[136,1024]{1,0:T(8,128)(2,1)} %collective-permute-done.6.refs_1_, bf16[8192,1024]{1,0:T(8,128)(2,1)} %refs_2_.3, bf16[8192,128]{1,0:T(8,128)(2,1)} %refs_3_.3, bf16[8192,128]{1,0:T(8,128)(2,1)} %refs_4_.5, ...), custom_call_target="tpu_custom_call" | custom-call | flops 713031680 | bytes 5242880 | tf_op jit(solution)/shard_map/project/pallas_call | solution.py:180
  55.9 0.0 copy-start.7
  55.9 1.7 %collective-permute-done.8.far_ref = bf16[128,1024]{1,0:T(8,128)(2,1)S(1)} collective-permute-done((bf16[128,1024]{1,0:T(8,128)(2,1)}, bf16[128,1024]{1,0:T(8,128)(2,1)S(1)}, u32[]{:S(2)}, u32[]{:S(2)}) %collective-permute-start.8) | collective-permute-done | bytes 262176 | tf_op jit(solution)/shard_map/ppermute | solution.py:497
  57.6 0.0 collective-permute-done.7.other_hbm.other_ref
  57.6 2.7 %text_sums.1 = (bf16[2,4096]{1,0:T(2,128)(2,1)S(1)}, bf16[2,4096]{1,0:T(2,128)(2,1)S(1)}) custom-call(s32[256]{0:T(256)S(1)} %copy-done.3, s32[1,256]{1,0:T(1,128)S(1)} %bitcast.24, bf16[256,1024]{1,0:T(8,128)(2,1)S(1)} %copy-done, bf16[4096,256]{1,0:T(8,128)(2,1)S(1)} %bitcast.17, bf16[4096,256]{1,0:T(8,128)(2,1)S(1)} %collective-permute-done.7.other_hbm.other_ref), custom_call_target="tpu_custom_call" | custom-call | flops 134217728 | bytes 4194304 | tf_op jit(solution)/shard_map/text_sums/pallas_call | solution.py:387
  60.3 0.1 broadcast_in_dim.38
  60.4 1.1 %pad_maximum_fusion = bf16[16,136,256]{2,1,0:T(8,128)(2,1)} fusion(bf16[16,2,256]{2,1,0:T(2,128)(2,1)S(1)} %bitcast.22, bf16[16,2,256]{2,1,0:T(2,128)(2,1)S(1)} %bitcast.21, bf16[16,132,256]{2,1,0:T(8,128)(2,1)S(1)} %broadcast_in_dim.38), kind=kLoop, calls=%fused_computation | loop fusion | flops 3342336 | bytes 2228224 | tf_op jit(solution)/shard_map/concatenate | solution.py:564
  61.5 6.1 %all-to-all-start.1 = ((bf16[16,136,256]{2,1,0:T(8,128)(2,1)}), bf16[16,136,256]{2,1,0:T(8,128)(2,1)S(1)}, u32[]{:S(2)}, u32[]{:S(2)}) async-start(bf16[16,136,256]{2,1,0:T(8,128)(2,1)} %pad_maximum_fusion), calls=%async_computation.1 | async-start | bytes 2228224 | tf_op jit(solution)/shard_map/all_to_all | solution.py:485
  67.7 0.0 copy-start.9
  67.7 0.9 copy-done.9
  68.6 19.9 %attend2.1 = (bf16[128,1024]{1,0:T(8,128)(2,1)}, bf16[128,1024]{1,0:T(8,128)(2,1)}) custom-call(bf16[128,1024]{1,0:T(8,128)(2,1)S(1)} %get-tuple-element.73.own_ref, bf16[128,1024]{1,0:T(8,128)(2,1)S(1)} %copy-done.9, bf16[4096,256]{1,0:T(8,128)(2,1)S(1)} %bitcast.18, bf16[4096,256]{1,0:T(8,128)(2,1)} %copy-done.1), custom_call_target="tpu_custom_call" | custom-call | flops 4294967296 | bytes 4194304 | tf_op jit(solution)/shard_map/attend2/pallas_call | solution.py:304
  88.5 0.0 all-to-all-done.1
  88.5 0.1 collective-permute-start.9
  88.6 5.4 %collective-permute-start.10 = (bf16[128,1024]{1,0:T(8,128)(2,1)}, bf16[128,1024]{1,0:T(8,128)(2,1)S(1)}, u32[]{:S(2)}, u32[]{:S(2)}) collective-permute-start(bf16[128,1024]{1,0:T(8,128)(2,1)} %get-tuple-element.64), channel_id=1, source_target_pairs={{124,0},{120,4},{116,8},{112,12},{108,16},{104,20},{100,24},{96,28... | collective-permute-start | bytes 786440 | tf_op jit(solution)/shard_map/ppermute | solution.py:497
  94.0 0.0 collective-permute-done.9
  94.1 0.1 collective-permute-start.11
  94.2 2.8 %collective-permute-start.12 = (f32[256]{0:T(256)S(1)}, f32[256]{0:T(256)S(1)}, u32[]{:S(2)}, u32[]{:S(2)}) collective-permute-start(f32[256]{0:T(256)S(1)} %bitcast.30), channel_id=1, source_target_pairs={{2,0},{3,1},{0,2},{1,3},{6,4},{7,5},{4,6},{5,7},{10,8},{11,9},{8,1... | collective-permute-start | bytes 3080 | tf_op jit(solution)/shard_map/ppermute | solution.py:491
  97.0 1.0 collective-permute-start.13
  98.0 10.0 %attend3.1 = bf16[132,1024]{1,0:T(8,128)(2,1)} custom-call(bf16[136,1024]{1,0:T(8,128)(2,1)} %copy-done.7, bf16[2176,256]{1,0:T(8,128)(2,1)S(1)} %bitcast.19, bf16[2176,256]{1,0:T(8,128)(2,1)S(1)} %bitcast.25), custom_call_target="tpu_custom_call" | custom-call | flops 3636461568 | bytes 2228224 | tf_op jit(solution)/shard_map/attend3/pallas_call | solution.py:451
  108.1 0.0 collective-permute-done.10
  108.1 0.0 collective-permute-done.11
  108.1 0.0 collective-permute-done.12
  108.1 0.0 collective-permute-done.13
  108.1 0.0 copy-done.13
  108.1 0.8 pad_maximum_fusion.1
  109.0 0.6 add_add_fusion
  (21 shorter events, 0.1 us)
Async XLA Ops:
  3.1 7.7 %copy-start.10 = (s32[256]{0:T(256)S(1)}, s32[256]{0:T(256)}, u32[]{:S(2)}) copy-start(s32[256]{0:T(256)} %param.23) | copy-start | bytes 3076
  3.1 7.7 %copy-start.11 = (s32[2]{0:T(128)S(1)}, s32[2]{0:T(128)}, u32[]{:S(2)}) copy-start(s32[2]{0:T(128)} %counts.1) | copy-start | bytes 28
  3.1 11.1 %copy-start = (bf16[256,1024]{1,0:T(8,128)(2,1)S(1)}, bf16[256,1024]{1,0:T(8,128)(2,1)}, u32[]{:S(2)}) copy-start(bf16[256,1024]{1,0:T(8,128)(2,1)} %q_ref.1) | copy-start | bytes 1572868
  3.1 40.6 %all-to-all-start = ((bf16[16,256,256]{2,1,0:T(8,128)(2,1)}), bf16[16,256,256]{2,1,0:T(8,128)(2,1)S(1)}, u32[]{:S(2)}, u32[]{:S(2)}) async-start(bf16[16,256,256]{2,1,0:T(8,128)(2,1)} %broadcast_in_dim.34), calls=%async_computation | async-start | bytes 4194304 | tf_op jit(solution)/shard_map/all_to_all | solution.py:485
  10.8 1.2 %copy-start.6 = (bf16[256,2048]{1,0:T(8,128)(2,1)S(1)}, bf16[256,2048]{1,0:T(8,128)(2,1)}, u32[]{:S(2)}) copy-start(bf16[256,2048]{1,0:T(8,128)(2,1)} %hidden_ref.1) | copy-start | bytes 3145732
  13.2 2.7 %collective-permute-start = (bf16[136,2176]{1,0:T(8,128)(2,1)S(1)}, bf16[136,2176]{1,0:T(8,128)(2,1)S(1)}, u32[]{:S(2)}, u32[]{:S(2)}) collective-permute-start(bf16[136,2176]{1,0:T(8,128)(2,1)S(1)} %get-tuple-element.38), channel_id=1, source_target_pairs={{4,0},{0,4},{12,8},{8,12},{20,16},{16,20},{28,24},{24,28},{36,32},... | collective-permute-start | bytes 1775624 | tf_op jit(solution)/shard_map/ppermute | solution.py:474
  16.1 18.6 %collective-permute-start.2 = (bf16[136,1024]{1,0:T(8,128)(2,1)S(1)}, bf16[136,1024]{1,0:T(8,128)(2,1)S(1)}, u32[]{:S(2)}, u32[]{:S(2)}) collective-permute-start(bf16[136,1024]{1,0:T(8,128)(2,1)S(1)} %get-tuple-element.71.refs_1_), channel_id=1, source_target_pairs={{1,0},{2,1},{3,2},{0,3},{5,4},{6,5},{7,6},{4,7},{9,8},{10,9},{11,1... | collective-permute-start | bytes 835592 | tf_op jit(solution)/shard_map/ppermute | solution.py:479
  19.9 17.7 %collective-permute-start.3 = (bf16[136,1024]{1,0:T(8,128)(2,1)S(1)}, bf16[136,1024]{1,0:T(8,128)(2,1)S(1)}, u32[]{:S(2)}, u32[]{:S(2)}) collective-permute-start(bf16[136,1024]{1,0:T(8,128)(2,1)S(1)} %get-tuple-element.71.refs_1_), channel_id=1, source_target_pairs={{3,0},{0,1},{1,2},{2,3},{7,4},{4,5},{5,6},{6,7},{11,8},{8,9},{9,10... | collective-permute-start | bytes 835592 | tf_op jit(solution)/shard_map/ppermute | solution.py:479
  19.9 14.7 %collective-permute-start.1 = (bf16[136,1024]{1,0:T(8,128)(2,1)S(1)}, bf16[136,1024]{1,0:T(8,128)(2,1)S(1)}, u32[]{:S(2)}, u32[]{:S(2)}) collective-permute-start(bf16[136,1024]{1,0:T(8,128)(2,1)S(1)} %get-tuple-element.72.refs_0_), channel_id=1, source_target_pairs={{3,0},{0,1},{1,2},{2,3},{7,4},{4,5},{5,6},{6,7},{11,8},{8,9},{9,10... | collective-permute-start | bytes 835592 | tf_op jit(solution)/shard_map/ppermute | solution.py:479
  19.9 17.7 %collective-permute-start.4 = (bf16[136,1024]{1,0:T(8,128)(2,1)S(1)}, bf16[136,1024]{1,0:T(8,128)(2,1)S(1)}, u32[]{:S(2)}, u32[]{:S(2)}) collective-permute-start(bf16[136,1024]{1,0:T(8,128)(2,1)S(1)} %get-tuple-element.72.refs_0_), channel_id=1, source_target_pairs={{1,0},{2,1},{3,2},{0,3},{5,4},{6,5},{7,6},{4,7},{9,8},{10,9},{11,1... | collective-permute-start | bytes 835592 | tf_op jit(solution)/shard_map/ppermute | solution.py:479
  34.6 9.0 %collective-permute-start.5 = (bf16[136,1024]{1,0:T(8,128)(2,1)S(1)}, bf16[136,1024]{1,0:T(8,128)(2,1)S(1)}, u32[]{:S(2)}, u32[]{:S(2)}) collective-permute-start(bf16[136,1024]{1,0:T(8,128)(2,1)S(1)} %collective-permute-done.1.refs_0_), channel_id=1, source_target_pairs={{3,0},{0,1},{1,2},{2,3},{7,4},{4,5},{5,6},{6,7},{11,8},{8,9},{9,10... | collective-permute-start | bytes 835592 | tf_op jit(solution)/shard_map/ppermute | solution.py:479
  34.6 9.0 %collective-permute-start.6 = (bf16[136,1024]{1,0:T(8,128)(2,1)S(1)}, bf16[136,1024]{1,0:T(8,128)(2,1)}, u32[]{:S(2)}, u32[]{:S(2)}) collective-permute-start(bf16[136,1024]{1,0:T(8,128)(2,1)S(1)} %collective-permute-done.2.refs_1_), channel_id=1, source_target_pairs={{1,0},{2,1},{3,2},{0,3},{5,4},{6,5},{7,6},{4,7},{9,8},{10,9},{11,1... | collective-permute-start | bytes 835592 | tf_op jit(solution)/shard_map/ppermute | solution.py:479
  37.7 13.1 %copy-start.2 = (f32[1024]{0:T(1024)S(1)}, f32[1024]{0:T(1024)}, u32[]{:S(2)}) copy-start(f32[1024]{0:T(1024)} %param.18) | copy-start | bytes 12292
  37.7 13.1 %copy-start.4 = (f32[128]{0:T(128)S(1)}, f32[128]{0:T(128)}, u32[]{:S(2)}) copy-start(f32[128]{0:T(128)} %param.20) | copy-start | bytes 1540
  37.7 13.1 %copy-start.5 = (f32[128]{0:T(128)S(1)}, f32[128]{0:T(128)}, u32[]{:S(2)}) copy-start(f32[128]{0:T(128)} %param.22) | copy-start | bytes 1540
  43.7 7.1 %copy-start.12 = (bf16[136,1024]{1,0:T(8,128)(2,1)}, bf16[136,1024]{1,0:T(8,128)(2,1)S(1)}, u32[]{:S(2)}) copy-start(bf16[136,1024]{1,0:T(8,128)(2,1)S(1)} %collective-permute-done.5.refs_0_) | copy-start | bytes 835588
  43.7 13.9 %collective-permute-start.7 = (bf16[4096,256]{1,0:T(8,128)(2,1)S(1)}, bf16[4096,256]{1,0:T(8,128)(2,1)S(1)}, u32[]{:S(2)}, u32[]{:S(2)}) collective-permute-start(bf16[4096,256]{1,0:T(8,128)(2,1)S(1)} %bitcast.16), channel_id=1, source_target_pairs={{4,0},{0,4},{12,8},{8,12},{20,16},{16,20},{28,24},{24,28},{36,32},... | collective-permute-start | bytes 6291464 | tf_op jit(solution)/shard_map/ppermute | solution.py:474
  45.9 11.7 %collective-permute-start.8 = (bf16[128,1024]{1,0:T(8,128)(2,1)}, bf16[128,1024]{1,0:T(8,128)(2,1)S(1)}, u32[]{:S(2)}, u32[]{:S(2)}) collective-permute-start(bf16[128,1024]{1,0:T(8,128)(2,1)} %get-tuple-element.53), channel_id=1, source_target_pairs={{124,0},{120,4},{116,8},{112,12},{108,16},{104,20},{100,24},{96,28... | collective-permute-start | bytes 786440 | tf_op jit(solution)/shard_map/ppermute | solution.py:497
  50.8 6.8 %copy-start.3 = (s32[256]{0:T(256)S(1)}, s32[256]{0:T(256)}, u32[]{:S(2)}) copy-start(s32[256]{0:T(256)} %text.1) | copy-start | bytes 3076
  55.9 4.4 %copy-start.7 = (bf16[136,1024]{1,0:T(8,128)(2,1)}, bf16[136,1024]{1,0:T(8,128)(2,1)S(1)}, u32[]{:S(2)}) copy-start(bf16[136,1024]{1,0:T(8,128)(2,1)S(1)} %get-tuple-element.61.q_hbm) | copy-start | bytes 835588
  57.6 2.7 %copy-start.8 = (bf16[128,1024]{1,0:T(8,128)(2,1)}, bf16[128,1024]{1,0:T(8,128)(2,1)S(1)}, u32[]{:S(2)}) copy-start(bf16[128,1024]{1,0:T(8,128)(2,1)S(1)} %collective-permute-done.8.far_ref) | copy-start | bytes 786436
  57.6 2.7 %copy-start.1 = (bf16[4096,256]{1,0:T(8,128)(2,1)}, bf16[4096,256]{1,0:T(8,128)(2,1)S(1)}, u32[]{:S(2)}) copy-start(bf16[4096,256]{1,0:T(8,128)(2,1)S(1)} %collective-permute-done.7.other_hbm.other_ref) | copy-start | bytes 6291460
  61.5 27.0 %all-to-all-start.1 = ((bf16[16,136,256]{2,1,0:T(8,128)(2,1)}), bf16[16,136,256]{2,1,0:T(8,128)(2,1)S(1)}, u32[]{:S(2)}, u32[]{:S(2)}) async-start(bf16[16,136,256]{2,1,0:T(8,128)(2,1)} %pad_maximum_fusion), calls=%async_computation.1 | async-start | bytes 2228224 | tf_op jit(solution)/shard_map/all_to_all | solution.py:485
  67.7 1.0 copy-start.9
  88.5 5.5 %collective-permute-start.9 = (bf16[16,136,256]{2,1,0:T(8,128)(2,1)S(1)}, bf16[16,136,256]{2,1,0:T(8,128)(2,1)S(1)}, u32[]{:S(2)}, u32[]{:S(2)}) collective-permute-start(bf16[16,136,256]{2,1,0:T(8,128)(2,1)S(1)} %all-to-all-done.1), channel_id=1, source_target_pairs={{4,0},{0,4},{12,8},{8,12},{20,16},{16,20},{28,24},{24,28},{36,32},... | collective-permute-start | bytes 3342344 | tf_op jit(solution)/shard_map/ppermute | solution.py:474
  88.6 19.5 %collective-permute-start.10 = (bf16[128,1024]{1,0:T(8,128)(2,1)}, bf16[128,1024]{1,0:T(8,128)(2,1)S(1)}, u32[]{:S(2)}, u32[]{:S(2)}) collective-permute-start(bf16[128,1024]{1,0:T(8,128)(2,1)} %get-tuple-element.64), channel_id=1, source_target_pairs={{124,0},{120,4},{116,8},{112,12},{108,16},{104,20},{100,24},{96,28... | collective-permute-start | bytes 786440 | tf_op jit(solution)/shard_map/ppermute | solution.py:497
  94.1 14.0 %collective-permute-start.11 = (f32[256]{0:T(256)S(1)}, f32[256]{0:T(256)S(1)}, u32[]{:S(2)}, u32[]{:S(2)}) collective-permute-start(f32[256]{0:T(256)S(1)} %bitcast.29), channel_id=1, source_target_pairs={{1,0},{0,1},{3,2},{2,3},{5,4},{4,5},{7,6},{6,7},{9,8},{8,9},{11,10... | collective-permute-start | bytes 3080 | tf_op jit(solution)/shard_map/ppermute | solution.py:491
  94.2 13.9 %collective-permute-start.12 = (f32[256]{0:T(256)S(1)}, f32[256]{0:T(256)S(1)}, u32[]{:S(2)}, u32[]{:S(2)}) collective-permute-start(f32[256]{0:T(256)S(1)} %bitcast.30), channel_id=1, source_target_pairs={{2,0},{3,1},{0,2},{1,3},{6,4},{7,5},{4,6},{5,7},{10,8},{11,9},{8,1... | collective-permute-start | bytes 3080 | tf_op jit(solution)/shard_map/ppermute | solution.py:491
  97.0 11.1 %collective-permute-start.13 = (f32[256]{0:T(256)S(1)}, f32[256]{0:T(256)S(1)}, u32[]{:S(2)}, u32[]{:S(2)}) collective-permute-start(f32[256]{0:T(256)S(1)} %bitcast.31), channel_id=1, source_target_pairs={{3,0},{2,1},{1,2},{0,3},{7,4},{6,5},{5,6},{4,7},{11,8},{10,9},{9,1... | collective-permute-start | bytes 3080 | tf_op jit(solution)/shard_map/ppermute | solution.py:491
  98.0 10.1 %copy-start.13 = (bf16[128,1024]{1,0:T(8,128)(2,1)S(1)}, bf16[128,1024]{1,0:T(8,128)(2,1)}, u32[]{:S(2)}) copy-start(bf16[128,1024]{1,0:T(8,128)(2,1)} %get-tuple-element.60) | copy-start | bytes 786436

commit v7 on v6

--- a/solution.py
+++ b/solution.py
@@ -299,7 +299,7 @@
     tokens = 2 * mine.shape[0]
     vmem = pl.BlockSpec(memory_space=pltpu.VMEM)
     hbm = pl.BlockSpec(memory_space=pl.ANY)
-    other = pltpu.with_memory_space_constraint(other, pltpu.HBM)
+    far, other = (pltpu.with_memory_space_constraint(x, pltpu.HBM) for x in (far, other))
     out = pltpu.HBM(own.shape, BF)
     return pl.pallas_call(
         attend_kernel,
@@ -535,6 +535,7 @@
 
     sums, marks, far = lax.optimization_barrier((partial[1], marks, q2[PART:]))
     partial = (partial[0], sums)
+    far = from_partner(far)
     positions = marks[:, 0] * 128 + marks[:, 1]
     lane = jnp.arange(HD, dtype=jnp.int32)
     freqs = 1000000.0 ** (-((lane % (HD // 2)).astype(F32) * 2.0) / HD)
@@ -554,9 +555,8 @@
     )
     partial = (partial[0], sums)
     other2 = from_core(mine2)
-    far = from_partner(far)
     q3, kv3 = project([(-2, 0), (2, 1)], last, weights, partial, (*biases, cosine, sine))
-    kv3, other2, far = lax.optimization_barrier((kv3, other2, far))
+    kv3, other2 = lax.optimization_barrier((kv3, other2))
     sums = text_sums(text_rows, q2, mine2, other2)
 
     sums = [part.reshape(2, chips, ROWS).swapaxes(0, 1) for part in sums]

time: 110 us -> 105 us (0.955)
  waiting for transfers between devices: 10.1 us -> 4.9 us
    ppermute x6, waiting for transfers between devices: 7.53 us -> 1.38 us  [from_head(): lax.ppermute(x, 'head', [((i + distance) % count, i) for i in range(count)])]
    ppermute x3, starting transfers between devices: 3.3 us -> 1.37 us  [from_core(): return lax.ppermute(x, 'seq', [(i ^ 1, i) for i in range(count)])]
    ppermute x2, starting transfers between devices: 10.3 us -> 12 us  [from_partner(): return lax.ppermute(x, 'seq', [(count - 1 - i, i) for i in range(count)])]
    unnamed x28 -> x26, local copies, waits for them, and re-layouts: 2.23 us -> 2.4 us
  transfers between devices with their start and end apart: 16 -> 16, of which waited for: 3 -> 3; matrix products, arithmetic and copies ran while one was open for 1% -> 1% of each run, Pallas kernels for 42% -> 45%
where the time goes in v7:
time: 105 us
  Pallas kernels  50 us (48%)
  starting transfers between devices  40.7 us (39%)
  waiting for transfers between devices  4.9 us (5%)
  other arithmetic  4.15 us (4%)
  local copies, waits for them, and re-layouts  4.11 us (4%)
    pallas_call x1, Pallas kernels, attend(): pl.pallas_call(attend_kernel, out_shape=(out, out), in_specs=[vmem, vmem,...  20.8 us
    pallas_call x3, Pallas kernels, project(): pl.pallas_call(kernel, out_shape=(*(jax.ShapeDtypeStruct(o, kind) if fini...  15.4 us
    all_to_all x2, starting transfers between devices, over_chips(): lax.all_to_all(many, 'seq', 0, 0, axis_index_groups=groups, tiled=True)  14.2 us
    ppermute x2, starting transfers between devices, from_partner(): return lax.ppermute(x, 'seq', [(count - 1 - i, i) for i in range(count)])  12 us
    pallas_call x1, Pallas kernels, attend3(): pl.pallas_call(attend3_kernel, out_shape=jax.ShapeDtypeStruct((SHARE, q3....  10 us
    ppermute x6, starting transfers between devices, from_head(): lax.ppermute(x, 'head', [((i + distance) % count, i) for i in range(count)])  9.21 us
    ppermute x3, starting transfers between devices, over_heads(): lax.ppermute(x, 'head', [(i ^ step, i) for i in range(count)])  3.93 us
    pallas_call x1, Pallas kernels, text_sums(): pl.pallas_call(text_kernel, out_shape=(jax.ShapeDtypeStruct((2, tokens //...  2.69 us
  transfers between devices with their start and end apart: 16, of which 3 were waited for; matrix products, arithmetic and copies ran while one was open for 1% of the time, Pallas kernels for 45%

profile of v7, /device:TPU:1, one launch (start us, length us, event | category | flops | bytes accessed | tf_op | source)
XLA Modules:
  0.0 104.8 jit_solution(18318228728820161137)
XLA Ops:
  0.6 0.9 pad_maximum_fusion.2
  1.5 1.5 %broadcast_in_dim.34 = bf16[16,256,256]{2,1,0:T(8,128)(2,1)} broadcast(bf16[256,256]{1,0:T(8,128)(2,1)S(1)} %pad_maximum_fusion.2), dimensions={1,2} | broadcast | bytes 2228224 | tf_op jit(solution)/shard_map/broadcast_in_dim | solution.py:521
  3.1 7.7 %all-to-all-start = ((bf16[16,256,256]{2,1,0:T(8,128)(2,1)}), bf16[16,256,256]{2,1,0:T(8,128)(2,1)S(1)}, u32[]{:S(2)}, u32[]{:S(2)}) async-start(bf16[16,256,256]{2,1,0:T(8,128)(2,1)} %broadcast_in_dim.34), calls=%async_computation | async-start | bytes 4194304 | tf_op jit(solution)/shard_map/all_to_all | solution.py:485
  10.8 0.0 copy-done.8
  10.8 0.0 copy-done.9
  10.8 0.0 copy-start.6
  10.8 1.2 %copy-done.6 = bf16[256,2048]{1,0:T(8,128)(2,1)S(1)} copy-done((bf16[256,2048]{1,0:T(8,128)(2,1)S(1)}, bf16[256,2048]{1,0:T(8,128)(2,1)}, u32[]{:S(2)}) %copy-start.6) | copy-done | bytes 1048600
  12.0 1.1 %pick_rows.1 = (bf16[136,2176]{1,0:T(8,128)(2,1)S(1)}, bf16[136,2176]{1,0:T(8,128)(2,1)S(1)}) custom-call(s32[2]{0:T(128)S(1)} %copy-done.9, s32[1,256]{1,0:T(1,128)S(1)} %bitcast.28, bf16[256,2048]{1,0:T(8,128)(2,1)S(1)} %copy-done.6), custom_call_target="tpu_custom_call" | custom-call | flops 303038464 | bytes 2228224 | tf_op jit(solution)/shard_map/pick_rows/pallas_call | solution.py:70
  13.1 1.0 collective-permute-start
  14.2 0.0 copy-done
  14.2 1.6 %collective-permute-done = bf16[136,2176]{1,0:T(8,128)(2,1)S(1)} collective-permute-done((bf16[136,2176]{1,0:T(8,128)(2,1)S(1)}, bf16[136,2176]{1,0:T(8,128)(2,1)S(1)}, u32[]{:S(2)}, u32[]{:S(2)}) %collective-permute-start) | collective-permute-done | bytes 591904 | tf_op jit(solution)/shard_map/ppermute | solution.py:474
  15.8 0.2 add.36
  16.0 0.1 fusion.6
  16.1 3.8 %collective-permute-start.2 = (bf16[136,1024]{1,0:T(8,128)(2,1)S(1)}, bf16[136,1024]{1,0:T(8,128)(2,1)S(1)}, u32[]{:S(2)}, u32[]{:S(2)}) collective-permute-start(bf16[136,1024]{1,0:T(8,128)(2,1)S(1)} %get-tuple-element.69.refs_1_), channel_id=1, source_target_pairs={{1,0},{2,1},{3,2},{0,3},{5,4},{6,5},{7,6},{4,7},{9,8},{10,9},{11,1... | collective-permute-start | bytes 835592 | tf_op jit(solution)/shard_map/ppermute | solution.py:479
  19.9 0.0 collective-permute-start.3
  19.9 0.0 collective-permute-start.1
  19.9 2.7 %collective-permute-start.4 = (bf16[136,1024]{1,0:T(8,128)(2,1)S(1)}, bf16[136,1024]{1,0:T(8,128)(2,1)S(1)}, u32[]{:S(2)}, u32[]{:S(2)}) collective-permute-start(bf16[136,1024]{1,0:T(8,128)(2,1)S(1)} %get-tuple-element.70.refs_0_), channel_id=1, source_target_pairs={{1,0},{2,1},{3,2},{0,3},{5,4},{6,5},{7,6},{4,7},{9,8},{10,9},{11,1... | collective-permute-start | bytes 835592 | tf_op jit(solution)/shard_map/ppermute | solution.py:479
  22.6 4.3 %project.3 = (f32[136,1024]{1,0:T(8,128)}, f32[136,256]{1,0:T(8,128)}) custom-call(bf16[136,1024]{1,0:T(8,128)(2,1)S(1)} %get-tuple-element.70.refs_0_, bf16[136,1024]{1,0:T(8,128)(2,1)S(1)} %get-tuple-element.69.refs_1_, bf16[8192,1024]{1,0:T(8,128)(2,1)} %refs_2_.3, bf16[8192,128]{1,0:T(8,128)(2,1)} %refs_3_.3, bf16[8192,128]{1,0:T(8,128)(2,1)} %refs_4_.5), custom_call_target="tpu_custom_call" | custom-call | flops 713031680 | bytes 5242880 | tf_op jit(solution)/shard_map/project/pallas_call | solution.py:180
  26.9 6.1 %collective-permute-start.5 = (bf16[128,1024]{1,0:T(8,128)(2,1)S(1)}, bf16[128,1024]{1,0:T(8,128)(2,1)S(1)}, u32[]{:S(2)}, u32[]{:S(2)}) collective-permute-start(bf16[128,1024]{1,0:T(8,128)(2,1)S(1)} %get-tuple-element.42), channel_id=1, source_target_pairs={{124,0},{120,4},{116,8},{112,12},{108,16},{104,20},{100,24},{96,28... | collective-permute-start | bytes 786440 | tf_op jit(solution)/shard_map/ppermute | solution.py:497
  33.1 0.2 convert_reduce_fusion
  33.2 1.4 %collective-permute-done.1.refs_0_ = bf16[136,1024]{1,0:T(8,128)(2,1)S(1)} collective-permute-done((bf16[136,1024]{1,0:T(8,128)(2,1)S(1)}, bf16[136,1024]{1,0:T(8,128)(2,1)S(1)}, u32[]{:S(2)}, u32[]{:S(2)}) %collective-permute-start.1) | collective-permute-done | bytes 278560 | tf_op jit(solution)/shard_map/ppermute | solution.py:479
  34.6 0.0 collective-permute-start.6
  34.6 0.0 collective-permute-done.2.refs_1_
  34.6 2.7 %collective-permute-start.7 = (bf16[136,1024]{1,0:T(8,128)(2,1)S(1)}, bf16[136,1024]{1,0:T(8,128)(2,1)}, u32[]{:S(2)}, u32[]{:S(2)}) collective-permute-start(bf16[136,1024]{1,0:T(8,128)(2,1)S(1)} %collective-permute-done.2.refs_1_), channel_id=1, source_target_pairs={{1,0},{2,1},{3,2},{0,3},{5,4},{6,5},{7,6},{4,7},{9,8},{10,9},{11,1... | collective-permute-start | bytes 835592 | tf_op jit(solution)/shard_map/ppermute | solution.py:479
  37.3 0.3 fusion
  37.6 0.0 collective-permute-done.3.refs_2_
  37.6 0.0 collective-permute-done.4.refs_3_
  37.6 0.0 copy-start.2
  37.7 0.0 copy-start.4
  37.7 0.0 copy-start.5
  37.7 6.0 %project.4 = (f32[136,1024]{1,0:T(8,128)}, f32[136,256]{1,0:T(8,128)}) custom-call(bf16[136,1024]{1,0:T(8,128)(2,1)S(1)} %collective-permute-done.1.refs_0_, bf16[136,1024]{1,0:T(8,128)(2,1)S(1)} %collective-permute-done.2.refs_1_, bf16[136,1024]{1,0:T(8,128)(2,1)S(1)} %collective-permute-done.3.refs_2_, ...), custom_call_target="tpu_custom_call" | custom-call | flops 1426063360 | bytes 10485760 | tf_op jit(solution)/shard_map/project/pallas_call | solution.py:180
  43.6 1.9 %collective-permute-done.5.far_ref = bf16[128,1024]{1,0:T(8,128)(2,1)S(1)} collective-permute-done((bf16[128,1024]{1,0:T(8,128)(2,1)S(1)}, bf16[128,1024]{1,0:T(8,128)(2,1)S(1)}, u32[]{:S(2)}, u32[]{:S(2)}) %collective-permute-start.5) | collective-permute-done | bytes 262176 | tf_op jit(solution)/shard_map/ppermute | solution.py:497
  45.6 0.0 collective-permute-done.6.refs_0_
  45.6 0.7 copy-done.12
  46.3 0.0 collective-permute-done.7.refs_1_
  46.3 0.0 all-to-all-done
  46.3 0.3 collective-permute-start.8
  46.5 0.4 copy-done.10
  47.0 0.0 copy-done.2
  47.0 0.0 copy-done.4
  47.0 0.0 copy-done.5
  47.0 5.1 %project.5 = (bf16[136,1024]{1,0:T(8,128)(2,1)S(1)}, bf16[136,256]{1,0:T(8,128)(2,1)S(1)}) custom-call(bf16[136,1024]{1,0:T(8,128)(2,1)} %copy-done.10, bf16[136,1024]{1,0:T(8,128)(2,1)} %collective-permute-done.7.refs_1_, bf16[8192,1024]{1,0:T(8,128)(2,1)} %refs_2_.3, bf16[8192,128]{1,0:T(8,128)(2,1)} %refs_3_.3, bf16[8192,128]{1,0:T(8,128)(2,1)} %refs_4_.5, ...), custom_call_target="tpu_custom_call" | custom-call | flops 713031680 | bytes 5242880 | tf_op jit(solution)/shard_map/project/pallas_call | solution.py:180
  52.1 0.0 copy-start.7
  52.1 0.0 collective-permute-done.8.other_hbm.other_ref
  52.1 0.0 copy-start.1
  52.1 2.7 %text_sums.1 = (bf16[2,4096]{1,0:T(2,128)(2,1)S(1)}, bf16[2,4096]{1,0:T(2,128)(2,1)S(1)}) custom-call(s32[256]{0:T(256)S(1)} %copy-done.3, s32[1,256]{1,0:T(1,128)S(1)} %bitcast.24, bf16[256,1024]{1,0:T(8,128)(2,1)S(1)} %copy-done, bf16[4096,256]{1,0:T(8,128)(2,1)S(1)} %bitcast.17, bf16[4096,256]{1,0:T(8,128)(2,1)S(1)} %collective-permute-done.8.other_hbm.other_ref), custom_call_target="tpu_custom_call" | custom-call | flops 134217728 | bytes 4194304 | tf_op jit(solution)/shard_map/text_sums/pallas_call | solution.py:387
  54.8 0.1 broadcast_in_dim.38
  54.9 1.1 %pad_maximum_fusion = bf16[16,136,256]{2,1,0:T(8,128)(2,1)} fusion(bf16[16,2,256]{2,1,0:T(2,128)(2,1)S(1)} %bitcast.22, bf16[16,2,256]{2,1,0:T(2,128)(2,1)S(1)} %bitcast.21, bf16[16,132,256]{2,1,0:T(8,128)(2,1)S(1)} %broadcast_in_dim.38), kind=kLoop, calls=%fused_computation | loop fusion | flops 3342336 | bytes 2228224 | tf_op jit(solution)/shard_map/concatenate | solution.py:564
  56.0 6.5 %all-to-all-start.1 = ((bf16[16,136,256]{2,1,0:T(8,128)(2,1)}), bf16[16,136,256]{2,1,0:T(8,128)(2,1)S(1)}, u32[]{:S(2)}, u32[]{:S(2)}) async-start(bf16[16,136,256]{2,1,0:T(8,128)(2,1)} %pad_maximum_fusion), calls=%async_computation.1 | async-start | bytes 2228224 | tf_op jit(solution)/shard_map/all_to_all | solution.py:485
  62.5 20.8 %attend2.1 = (bf16[128,1024]{1,0:T(8,128)(2,1)}, bf16[128,1024]{1,0:T(8,128)(2,1)}) custom-call(bf16[128,1024]{1,0:T(8,128)(2,1)S(1)} %get-tuple-element.71.own_ref, bf16[128,1024]{1,0:T(8,128)(2,1)} %copy-done.12, bf16[4096,256]{1,0:T(8,128)(2,1)S(1)} %bitcast.18, bf16[4096,256]{1,0:T(8,128)(2,1)} %copy-done.1), custom_call_target="tpu_custom_call" | custom-call | flops 4294967296 | bytes 4194304 | tf_op jit(solution)/shard_map/attend2/pallas_call | solution.py:304
  83.3 0.0 all-to-all-done.1
  83.3 0.1 collective-permute-start.9
  83.4 5.8 %collective-permute-start.10 = (bf16[128,1024]{1,0:T(8,128)(2,1)}, bf16[128,1024]{1,0:T(8,128)(2,1)S(1)}, u32[]{:S(2)}, u32[]{:S(2)}) collective-permute-start(bf16[128,1024]{1,0:T(8,128)(2,1)} %get-tuple-element.62), channel_id=1, source_target_pairs={{124,0},{120,4},{116,8},{112,12},{108,16},{104,20},{100,24},{96,28... | collective-permute-start | bytes 786440 | tf_op jit(solution)/shard_map/ppermute | solution.py:497
  89.3 0.0 collective-permute-done.9
  89.4 0.1 collective-permute-start.11
  89.4 2.7 %collective-permute-start.12 = (f32[256]{0:T(256)S(1)}, f32[256]{0:T(256)S(1)}, u32[]{:S(2)}, u32[]{:S(2)}) collective-permute-start(f32[256]{0:T(256)S(1)} %bitcast.30), channel_id=1, source_target_pairs={{2,0},{3,1},{0,2},{1,3},{6,4},{7,5},{4,6},{5,7},{10,8},{11,9},{8,1... | collective-permute-start | bytes 3080 | tf_op jit(solution)/shard_map/ppermute | solution.py:491
  92.1 1.2 %collective-permute-start.13 = (f32[256]{0:T(256)S(1)}, f32[256]{0:T(256)S(1)}, u32[]{:S(2)}, u32[]{:S(2)}) collective-permute-start(f32[256]{0:T(256)S(1)} %bitcast.31), channel_id=1, source_target_pairs={{3,0},{2,1},{1,2},{0,3},{7,4},{6,5},{5,6},{4,7},{11,8},{10,9},{9,1... | collective-permute-start | bytes 3080 | tf_op jit(solution)/shard_map/ppermute | solution.py:491
  93.3 10.0 %attend3.1 = bf16[132,1024]{1,0:T(8,128)(2,1)} custom-call(bf16[136,1024]{1,0:T(8,128)(2,1)} %copy-done.7, bf16[2176,256]{1,0:T(8,128)(2,1)S(1)} %bitcast.19, bf16[2176,256]{1,0:T(8,128)(2,1)S(1)} %bitcast.25), custom_call_target="tpu_custom_call" | custom-call | flops 3636461568 | bytes 2228224 | tf_op jit(solution)/shard_map/attend3/pallas_call | solution.py:451
  103.3 0.0 collective-permute-done.10
  103.4 0.0 collective-permute-done.11
  103.4 0.0 collective-permute-done.12
  103.4 0.0 collective-permute-done.13
  103.4 0.8 pad_maximum_fusion.1
  104.2 0.6 add_add_fusion
  (19 shorter events, 0.2 us)
Async XLA Ops:
  3.1 7.7 %copy-start.8 = (s32[256]{0:T(256)S(1)}, s32[256]{0:T(256)}, u32[]{:S(2)}) copy-start(s32[256]{0:T(256)} %param.23) | copy-start | bytes 3076
  3.1 7.7 %copy-start.9 = (s32[2]{0:T(128)S(1)}, s32[2]{0:T(128)}, u32[]{:S(2)}) copy-start(s32[2]{0:T(128)} %counts.1) | copy-start | bytes 28
  3.1 11.1 %copy-start = (bf16[256,1024]{1,0:T(8,128)(2,1)S(1)}, bf16[256,1024]{1,0:T(8,128)(2,1)}, u32[]{:S(2)}) copy-start(bf16[256,1024]{1,0:T(8,128)(2,1)} %q_ref.1) | copy-start | bytes 1572868
  3.1 43.2 %all-to-all-start = ((bf16[16,256,256]{2,1,0:T(8,128)(2,1)}), bf16[16,256,256]{2,1,0:T(8,128)(2,1)S(1)}, u32[]{:S(2)}, u32[]{:S(2)}) async-start(bf16[16,256,256]{2,1,0:T(8,128)(2,1)} %broadcast_in_dim.34), calls=%async_computation | async-start | bytes 4194304 | tf_op jit(solution)/shard_map/all_to_all | solution.py:485
  10.8 1.2 %copy-start.6 = (bf16[256,2048]{1,0:T(8,128)(2,1)S(1)}, bf16[256,2048]{1,0:T(8,128)(2,1)}, u32[]{:S(2)}) copy-start(bf16[256,2048]{1,0:T(8,128)(2,1)} %hidden_ref.1) | copy-start | bytes 3145732
  13.1 2.7 %collective-permute-start = (bf16[136,2176]{1,0:T(8,128)(2,1)S(1)}, bf16[136,2176]{1,0:T(8,128)(2,1)S(1)}, u32[]{:S(2)}, u32[]{:S(2)}) collective-permute-start(bf16[136,2176]{1,0:T(8,128)(2,1)S(1)} %get-tuple-element.37), channel_id=1, source_target_pairs={{4,0},{0,4},{12,8},{8,12},{20,16},{16,20},{28,24},{24,28},{36,32},... | collective-permute-start | bytes 1775624 | tf_op jit(solution)/shard_map/ppermute | solution.py:474
  16.1 18.6 %collective-permute-start.2 = (bf16[136,1024]{1,0:T(8,128)(2,1)S(1)}, bf16[136,1024]{1,0:T(8,128)(2,1)S(1)}, u32[]{:S(2)}, u32[]{:S(2)}) collective-permute-start(bf16[136,1024]{1,0:T(8,128)(2,1)S(1)} %get-tuple-element.69.refs_1_), channel_id=1, source_target_pairs={{1,0},{2,1},{3,2},{0,3},{5,4},{6,5},{7,6},{4,7},{9,8},{10,9},{11,1... | collective-permute-start | bytes 835592 | tf_op jit(solution)/shard_map/ppermute | solution.py:479
  19.9 17.7 %collective-permute-start.3 = (bf16[136,1024]{1,0:T(8,128)(2,1)S(1)}, bf16[136,1024]{1,0:T(8,128)(2,1)S(1)}, u32[]{:S(2)}, u32[]{:S(2)}) collective-permute-start(bf16[136,1024]{1,0:T(8,128)(2,1)S(1)} %get-tuple-element.69.refs_1_), channel_id=1, source_target_pairs={{3,0},{0,1},{1,2},{2,3},{7,4},{4,5},{5,6},{6,7},{11,8},{8,9},{9,10... | collective-permute-start | bytes 835592 | tf_op jit(solution)/shard_map/ppermute | solution.py:479
  19.9 14.7 %collective-permute-start.1 = (bf16[136,1024]{1,0:T(8,128)(2,1)S(1)}, bf16[136,1024]{1,0:T(8,128)(2,1)S(1)}, u32[]{:S(2)}, u32[]{:S(2)}) collective-permute-start(bf16[136,1024]{1,0:T(8,128)(2,1)S(1)} %get-tuple-element.70.refs_0_), channel_id=1, source_target_pairs={{3,0},{0,1},{1,2},{2,3},{7,4},{4,5},{5,6},{6,7},{11,8},{8,9},{9,10... | collective-permute-start | bytes 835592 | tf_op jit(solution)/shard_map/ppermute | solution.py:479
  19.9 17.7 %collective-permute-start.4 = (bf16[136,1024]{1,0:T(8,128)(2,1)S(1)}, bf16[136,1024]{1,0:T(8,128)(2,1)S(1)}, u32[]{:S(2)}, u32[]{:S(2)}) collective-permute-start(bf16[136,1024]{1,0:T(8,128)(2,1)S(1)} %get-tuple-element.70.refs_0_), channel_id=1, source_target_pairs={{1,0},{2,1},{3,2},{0,3},{5,4},{6,5},{7,6},{4,7},{9,8},{10,9},{11,1... | collective-permute-start | bytes 835592 | tf_op jit(solution)/shard_map/ppermute | solution.py:479
  26.9 18.6 %collective-permute-start.5 = (bf16[128,1024]{1,0:T(8,128)(2,1)S(1)}, bf16[128,1024]{1,0:T(8,128)(2,1)S(1)}, u32[]{:S(2)}, u32[]{:S(2)}) collective-permute-start(bf16[128,1024]{1,0:T(8,128)(2,1)S(1)} %get-tuple-element.42), channel_id=1, source_target_pairs={{124,0},{120,4},{116,8},{112,12},{108,16},{104,20},{100,24},{96,28... | collective-permute-start | bytes 786440 | tf_op jit(solution)/shard_map/ppermute | solution.py:497
  34.6 11.0 %collective-permute-start.6 = (bf16[136,1024]{1,0:T(8,128)(2,1)S(1)}, bf16[136,1024]{1,0:T(8,128)(2,1)S(1)}, u32[]{:S(2)}, u32[]{:S(2)}) collective-permute-start(bf16[136,1024]{1,0:T(8,128)(2,1)S(1)} %collective-permute-done.1.refs_0_), channel_id=1, source_target_pairs={{3,0},{0,1},{1,2},{2,3},{7,4},{4,5},{5,6},{6,7},{11,8},{8,9},{9,10... | collective-permute-start | bytes 835592 | tf_op jit(solution)/shard_map/ppermute | solution.py:479
  34.6 11.6 %collective-permute-start.7 = (bf16[136,1024]{1,0:T(8,128)(2,1)S(1)}, bf16[136,1024]{1,0:T(8,128)(2,1)}, u32[]{:S(2)}, u32[]{:S(2)}) collective-permute-start(bf16[136,1024]{1,0:T(8,128)(2,1)S(1)} %collective-permute-done.2.refs_1_), channel_id=1, source_target_pairs={{1,0},{2,1},{3,2},{0,3},{5,4},{6,5},{7,6},{4,7},{9,8},{10,9},{11,1... | collective-permute-start | bytes 835592 | tf_op jit(solution)/shard_map/ppermute | solution.py:479
  37.6 9.3 %copy-start.2 = (f32[1024]{0:T(1024)S(1)}, f32[1024]{0:T(1024)}, u32[]{:S(2)}) copy-start(f32[1024]{0:T(1024)} %param.18) | copy-start | bytes 12292
  37.7 9.3 %copy-start.4 = (f32[128]{0:T(128)S(1)}, f32[128]{0:T(128)}, u32[]{:S(2)}) copy-start(f32[128]{0:T(128)} %param.20) | copy-start | bytes 1540
  37.7 9.3 %copy-start.5 = (f32[128]{0:T(128)S(1)}, f32[128]{0:T(128)}, u32[]{:S(2)}) copy-start(f32[128]{0:T(128)} %param.22) | copy-start | bytes 1540
  45.6 0.7 copy-start.12
  46.3 0.7 copy-start.10
  46.3 5.8 %collective-permute-start.8 = (bf16[4096,256]{1,0:T(8,128)(2,1)S(1)}, bf16[4096,256]{1,0:T(8,128)(2,1)S(1)}, u32[]{:S(2)}, u32[]{:S(2)}) collective-permute-start(bf16[4096,256]{1,0:T(8,128)(2,1)S(1)} %bitcast.16), channel_id=1, source_target_pairs={{4,0},{0,4},{12,8},{8,12},{20,16},{16,20},{28,24},{24,28},{36,32},... | collective-permute-start | bytes 6291464 | tf_op jit(solution)/shard_map/ppermute | solution.py:474
  47.0 5.2 %copy-start.3 = (s32[256]{0:T(256)S(1)}, s32[256]{0:T(256)}, u32[]{:S(2)}) copy-start(s32[256]{0:T(256)} %text.1) | copy-start | bytes 3076
  52.1 2.7 %copy-start.7 = (bf16[136,1024]{1,0:T(8,128)(2,1)}, bf16[136,1024]{1,0:T(8,128)(2,1)S(1)}, u32[]{:S(2)}) copy-start(bf16[136,1024]{1,0:T(8,128)(2,1)S(1)} %get-tuple-element.59.q_hbm) | copy-start | bytes 835588
  52.1 2.7 %copy-start.1 = (bf16[4096,256]{1,0:T(8,128)(2,1)}, bf16[4096,256]{1,0:T(8,128)(2,1)S(1)}, u32[]{:S(2)}) copy-start(bf16[4096,256]{1,0:T(8,128)(2,1)S(1)} %collective-permute-done.8.other_hbm.other_ref) | copy-start | bytes 6291460
  56.0 27.3 %all-to-all-start.1 = ((bf16[16,136,256]{2,1,0:T(8,128)(2,1)}), bf16[16,136,256]{2,1,0:T(8,128)(2,1)S(1)}, u32[]{:S(2)}, u32[]{:S(2)}) async-start(bf16[16,136,256]{2,1,0:T(8,128)(2,1)} %pad_maximum_fusion), calls=%async_computation.1 | async-start | bytes 2228224 | tf_op jit(solution)/shard_map/all_to_all | solution.py:485
  83.3 6.0 %collective-permute-start.9 = (bf16[16,136,256]{2,1,0:T(8,128)(2,1)S(1)}, bf16[16,136,256]{2,1,0:T(8,128)(2,1)S(1)}, u32[]{:S(2)}, u32[]{:S(2)}) collective-permute-start(bf16[16,136,256]{2,1,0:T(8,128)(2,1)S(1)} %all-to-all-done.1), channel_id=1, source_target_pairs={{4,0},{0,4},{12,8},{8,12},{20,16},{16,20},{28,24},{24,28},{36,32},... | collective-permute-start | bytes 3342344 | tf_op jit(solution)/shard_map/ppermute | solution.py:474
  83.4 19.9 %collective-permute-start.10 = (bf16[128,1024]{1,0:T(8,128)(2,1)}, bf16[128,1024]{1,0:T(8,128)(2,1)S(1)}, u32[]{:S(2)}, u32[]{:S(2)}) collective-permute-start(bf16[128,1024]{1,0:T(8,128)(2,1)} %get-tuple-element.62), channel_id=1, source_target_pairs={{124,0},{120,4},{116,8},{112,12},{108,16},{104,20},{100,24},{96,28... | collective-permute-start | bytes 786440 | tf_op jit(solution)/shard_map/ppermute | solution.py:497
  89.4 14.0 %collective-permute-start.11 = (f32[256]{0:T(256)S(1)}, f32[256]{0:T(256)S(1)}, u32[]{:S(2)}, u32[]{:S(2)}) collective-permute-start(f32[256]{0:T(256)S(1)} %bitcast.29), channel_id=1, source_target_pairs={{1,0},{0,1},{3,2},{2,3},{5,4},{4,5},{7,6},{6,7},{9,8},{8,9},{11,10... | collective-permute-start | bytes 3080 | tf_op jit(solution)/shard_map/ppermute | solution.py:491
  89.4 13.9 %collective-permute-start.12 = (f32[256]{0:T(256)S(1)}, f32[256]{0:T(256)S(1)}, u32[]{:S(2)}, u32[]{:S(2)}) collective-permute-start(f32[256]{0:T(256)S(1)} %bitcast.30), channel_id=1, source_target_pairs={{2,0},{3,1},{0,2},{1,3},{6,4},{7,5},{4,6},{5,7},{10,8},{11,9},{8,1... | collective-permute-start | bytes 3080 | tf_op jit(solution)/shard_map/ppermute | solution.py:491
  92.1 11.3 %collective-permute-start.13 = (f32[256]{0:T(256)S(1)}, f32[256]{0:T(256)S(1)}, u32[]{:S(2)}, u32[]{:S(2)}) collective-permute-start(f32[256]{0:T(256)S(1)} %bitcast.31), channel_id=1, source_target_pairs={{3,0},{2,1},{1,2},{0,3},{7,4},{6,5},{5,6},{4,7},{11,8},{10,9},{9,1... | collective-permute-start | bytes 3080 | tf_op jit(solution)/shard_map/ppermute | solution.py:491
  93.3 10.1 %copy-start.11 = (bf16[128,1024]{1,0:T(8,128)(2,1)S(1)}, bf16[128,1024]{1,0:T(8,128)(2,1)}, u32[]{:S(2)}) copy-start(bf16[128,1024]{1,0:T(8,128)(2,1)} %get-tuple-element.58) | copy-start | bytes 786436

commit v8 on v7

--- a/solution.py
+++ b/solution.py
@@ -233,20 +233,20 @@
     fetch.wait()
     v_s[1, :, :HD] = other_s[:, HD:]
 
-    def step(g, p, ref, b, bound):
-        at = pl.ds(pl.multiple_of(b * WIDE, WIDE), WIDE)
+    def step(g, p, ref, b, bound, width=WIDE):
+        at = pl.ds(pl.multiple_of(b * WIDE, WIDE), width)
         keys = ref[at, :HD]
         values = v_s[p, at, :]
         if bound is not None:
-            key = lax.broadcasted_iota(jnp.int32, (PART, WIDE), 1)
-            query = lax.broadcasted_iota(jnp.int32, (PART, WIDE), 0)
+            key = lax.broadcasted_iota(jnp.int32, (PART, width), 1)
+            query = lax.broadcasted_iota(jnp.int32, (PART, width), 0)
             bias = jnp.where(key + b * WIDE < bound[0] + bound[1] * query, 0.0, LOW)
-            bias_s[:PART] = bias
-            bias_s[PART:] = bias
+            bias_s[:PART, :width] = bias
+            bias_s[PART:, :width] = bias
 
         def scored(h):
             scores = dot_t(q_s[g, h], keys)
-            return scores if bound is None else scores + bias_s[...]
+            return scores if bound is None else scores + bias_s[:, :width]
 
         def weighed(h, scores):
             before = top_s[g, h]
@@ -274,9 +274,16 @@
 
             lax.fori_loop(0, whole_steps, plain, 0)
 
-            @pl.when((before % WIDE > 0) | (same > 0))
-            def _(p=p, ref=ref):
-                step(g, p, ref, whole_steps, (before + same * (PART * g + 1), same))
+            rest = before % WIDE + same * ROWS
+            bound = (before + same * (PART * g + 1), same)
+
+            @pl.when((rest > 0) & (rest <= WIDE // 2))
+            def _(p=p, ref=ref, whole_steps=whole_steps, bound=bound):
+                step(g, p, ref, whole_steps, bound, WIDE // 2)
+
+            @pl.when(rest > WIDE // 2)
+            def _(p=p, ref=ref, whole_steps=whole_steps, bound=bound):
+                step(g, p, ref, whole_steps, bound)
 
         return carry
 

time: 105 us -> 104 us (level)
  Pallas kernels: 50 us -> 48.8 us
    pallas_call x1, Pallas kernels: 20.8 us -> 19.6 us  [attend(): pl.pallas_call(attend_kernel, out_shape=(out, out), in_specs=[vmem, vmem,...]
where the time goes in v8:
time: 104 us
  Pallas kernels  48.8 us (47%)
  starting transfers between devices  40.7 us (39%)
  waiting for transfers between devices  4.9 us (5%)
  other arithmetic  4.15 us (4%)
  local copies, waits for them, and re-layouts  4.11 us (4%)
    pallas_call x1, Pallas kernels, attend(): pl.pallas_call(attend_kernel, out_shape=(out, out), in_specs=[vmem, vmem,...  19.6 us
    pallas_call x3, Pallas kernels, project(): pl.pallas_call(kernel, out_shape=(*(jax.ShapeDtypeStruct(o, kind) if fini...  15.4 us
    all_to_all x2, starting transfers between devices, over_chips(): lax.all_to_all(many, 'seq', 0, 0, axis_index_groups=groups, tiled=True)  14.2 us
    ppermute x2, starting transfers between devices, from_partner(): return lax.ppermute(x, 'seq', [(count - 1 - i, i) for i in range(count)])  12 us
    pallas_call x1, Pallas kernels, attend3(): pl.pallas_call(attend3_kernel, out_shape=jax.ShapeDtypeStruct((SHARE, q3....  10 us
    ppermute x6, starting transfers between devices, from_head(): lax.ppermute(x, 'head', [((i + distance) % count, i) for i in range(count)])  9.21 us
    ppermute x3, starting transfers between devices, over_heads(): lax.ppermute(x, 'head', [(i ^ step, i) for i in range(count)])  3.93 us
    pallas_call x1, Pallas kernels, text_sums(): pl.pallas_call(text_kernel, out_shape=(jax.ShapeDtypeStruct((2, tokens //...  2.69 us
  transfers between devices with their start and end apart: 16, of which 3 were waited for; matrix products, arithmetic and copies ran while one was open for 1% of the time, Pallas kernels for 45%

profile of v8, /device:TPU:1, one launch (start us, length us, event | category | flops | bytes accessed | tf_op | source)
XLA Modules:
  0.0 103.6 jit_solution(14600677176184831986)
XLA Ops:
  0.6 0.9 pad_maximum_fusion.2
  1.5 1.5 %broadcast_in_dim.34 = bf16[16,256,256]{2,1,0:T(8,128)(2,1)} broadcast(bf16[256,256]{1,0:T(8,128)(2,1)S(1)} %pad_maximum_fusion.2), dimensions={1,2} | broadcast | bytes 2228224 | tf_op jit(solution)/shard_map/broadcast_in_dim | solution.py:528
  3.1 7.7 %all-to-all-start = ((bf16[16,256,256]{2,1,0:T(8,128)(2,1)}), bf16[16,256,256]{2,1,0:T(8,128)(2,1)S(1)}, u32[]{:S(2)}, u32[]{:S(2)}) async-start(bf16[16,256,256]{2,1,0:T(8,128)(2,1)} %broadcast_in_dim.34), calls=%async_computation | async-start | bytes 4194304 | tf_op jit(solution)/shard_map/all_to_all | solution.py:492
  10.8 0.0 copy-done.8
  10.8 0.0 copy-done.9
  10.8 0.0 copy-start.6
  10.8 1.2 %copy-done.6 = bf16[256,2048]{1,0:T(8,128)(2,1)S(1)} copy-done((bf16[256,2048]{1,0:T(8,128)(2,1)S(1)}, bf16[256,2048]{1,0:T(8,128)(2,1)}, u32[]{:S(2)}) %copy-start.6) | copy-done | bytes 1048600
  12.0 1.1 %pick_rows.1 = (bf16[136,2176]{1,0:T(8,128)(2,1)S(1)}, bf16[136,2176]{1,0:T(8,128)(2,1)S(1)}) custom-call(s32[2]{0:T(128)S(1)} %copy-done.9, s32[1,256]{1,0:T(1,128)S(1)} %bitcast.28, bf16[256,2048]{1,0:T(8,128)(2,1)S(1)} %copy-done.6), custom_call_target="tpu_custom_call" | custom-call | flops 303038464 | bytes 2228224 | tf_op jit(solution)/shard_map/pick_rows/pallas_call | solution.py:70
  13.1 1.0 collective-permute-start
  14.2 0.0 copy-done
  14.2 1.6 %collective-permute-done = bf16[136,2176]{1,0:T(8,128)(2,1)S(1)} collective-permute-done((bf16[136,2176]{1,0:T(8,128)(2,1)S(1)}, bf16[136,2176]{1,0:T(8,128)(2,1)S(1)}, u32[]{:S(2)}, u32[]{:S(2)}) %collective-permute-start) | collective-permute-done | bytes 591904 | tf_op jit(solution)/shard_map/ppermute | solution.py:481
  15.8 0.2 add.36
  16.0 0.1 fusion.6
  16.1 3.8 %collective-permute-start.2 = (bf16[136,1024]{1,0:T(8,128)(2,1)S(1)}, bf16[136,1024]{1,0:T(8,128)(2,1)S(1)}, u32[]{:S(2)}, u32[]{:S(2)}) collective-permute-start(bf16[136,1024]{1,0:T(8,128)(2,1)S(1)} %get-tuple-element.69.refs_1_), channel_id=1, source_target_pairs={{1,0},{2,1},{3,2},{0,3},{5,4},{6,5},{7,6},{4,7},{9,8},{10,9},{11,1... | collective-permute-start | bytes 835592 | tf_op jit(solution)/shard_map/ppermute | solution.py:486
  19.9 0.0 collective-permute-start.3
  19.9 0.0 collective-permute-start.1
  19.9 2.7 %collective-permute-start.4 = (bf16[136,1024]{1,0:T(8,128)(2,1)S(1)}, bf16[136,1024]{1,0:T(8,128)(2,1)S(1)}, u32[]{:S(2)}, u32[]{:S(2)}) collective-permute-start(bf16[136,1024]{1,0:T(8,128)(2,1)S(1)} %get-tuple-element.70.refs_0_), channel_id=1, source_target_pairs={{1,0},{2,1},{3,2},{0,3},{5,4},{6,5},{7,6},{4,7},{9,8},{10,9},{11,1... | collective-permute-start | bytes 835592 | tf_op jit(solution)/shard_map/ppermute | solution.py:486
  22.6 4.3 %project.3 = (f32[136,1024]{1,0:T(8,128)}, f32[136,256]{1,0:T(8,128)}) custom-call(bf16[136,1024]{1,0:T(8,128)(2,1)S(1)} %get-tuple-element.70.refs_0_, bf16[136,1024]{1,0:T(8,128)(2,1)S(1)} %get-tuple-element.69.refs_1_, bf16[8192,1024]{1,0:T(8,128)(2,1)} %refs_2_.3, bf16[8192,128]{1,0:T(8,128)(2,1)} %refs_3_.3, bf16[8192,128]{1,0:T(8,128)(2,1)} %refs_4_.5), custom_call_target="tpu_custom_call" | custom-call | flops 713031680 | bytes 5242880 | tf_op jit(solution)/shard_map/project/pallas_call | solution.py:180
  26.9 6.1 %collective-permute-start.5 = (bf16[128,1024]{1,0:T(8,128)(2,1)S(1)}, bf16[128,1024]{1,0:T(8,128)(2,1)S(1)}, u32[]{:S(2)}, u32[]{:S(2)}) collective-permute-start(bf16[128,1024]{1,0:T(8,128)(2,1)S(1)} %get-tuple-element.42), channel_id=1, source_target_pairs={{124,0},{120,4},{116,8},{112,12},{108,16},{104,20},{100,24},{96,28... | collective-permute-start | bytes 786440 | tf_op jit(solution)/shard_map/ppermute | solution.py:504
  33.1 0.2 convert_reduce_fusion
  33.2 1.4 %collective-permute-done.1.refs_0_ = bf16[136,1024]{1,0:T(8,128)(2,1)S(1)} collective-permute-done((bf16[136,1024]{1,0:T(8,128)(2,1)S(1)}, bf16[136,1024]{1,0:T(8,128)(2,1)S(1)}, u32[]{:S(2)}, u32[]{:S(2)}) %collective-permute-start.1) | collective-permute-done | bytes 278560 | tf_op jit(solution)/shard_map/ppermute | solution.py:486
  34.6 0.0 collective-permute-start.6
  34.6 0.0 collective-permute-done.2.refs_1_
  34.6 2.7 %collective-permute-start.7 = (bf16[136,1024]{1,0:T(8,128)(2,1)S(1)}, bf16[136,1024]{1,0:T(8,128)(2,1)}, u32[]{:S(2)}, u32[]{:S(2)}) collective-permute-start(bf16[136,1024]{1,0:T(8,128)(2,1)S(1)} %collective-permute-done.2.refs_1_), channel_id=1, source_target_pairs={{1,0},{2,1},{3,2},{0,3},{5,4},{6,5},{7,6},{4,7},{9,8},{10,9},{11,1... | collective-permute-start | bytes 835592 | tf_op jit(solution)/shard_map/ppermute | solution.py:486
  37.3 0.3 fusion
  37.6 0.0 collective-permute-done.3.refs_2_
  37.6 0.0 collective-permute-done.4.refs_3_
  37.6 0.0 copy-start.2
  37.7 0.0 copy-start.4
  37.7 0.0 copy-start.5
  37.7 6.0 %project.4 = (f32[136,1024]{1,0:T(8,128)}, f32[136,256]{1,0:T(8,128)}) custom-call(bf16[136,1024]{1,0:T(8,128)(2,1)S(1)} %collective-permute-done.1.refs_0_, bf16[136,1024]{1,0:T(8,128)(2,1)S(1)} %collective-permute-done.2.refs_1_, bf16[136,1024]{1,0:T(8,128)(2,1)S(1)} %collective-permute-done.3.refs_2_, ...), custom_call_target="tpu_custom_call" | custom-call | flops 1426063360 | bytes 10485760 | tf_op jit(solution)/shard_map/project/pallas_call | solution.py:180
  43.6 1.9 %collective-permute-done.5.far_ref = bf16[128,1024]{1,0:T(8,128)(2,1)S(1)} collective-permute-done((bf16[128,1024]{1,0:T(8,128)(2,1)S(1)}, bf16[128,1024]{1,0:T(8,128)(2,1)S(1)}, u32[]{:S(2)}, u32[]{:S(2)}) %collective-permute-start.5) | collective-permute-done | bytes 262176 | tf_op jit(solution)/shard_map/ppermute | solution.py:504
  45.6 0.0 collective-permute-done.6.refs_0_
  45.6 0.7 copy-done.12
  46.3 0.0 collective-permute-done.7.refs_1_
  46.3 0.0 all-to-all-done
  46.3 0.3 collective-permute-start.8
  46.5 0.4 copy-done.10
  47.0 0.0 copy-done.2
  47.0 0.0 copy-done.4
  47.0 0.0 copy-done.5
  47.0 5.1 %project.5 = (bf16[136,1024]{1,0:T(8,128)(2,1)S(1)}, bf16[136,256]{1,0:T(8,128)(2,1)S(1)}) custom-call(bf16[136,1024]{1,0:T(8,128)(2,1)} %copy-done.10, bf16[136,1024]{1,0:T(8,128)(2,1)} %collective-permute-done.7.refs_1_, bf16[8192,1024]{1,0:T(8,128)(2,1)} %refs_2_.3, bf16[8192,128]{1,0:T(8,128)(2,1)} %refs_3_.3, bf16[8192,128]{1,0:T(8,128)(2,1)} %refs_4_.5, ...), custom_call_target="tpu_custom_call" | custom-call | flops 713031680 | bytes 5242880 | tf_op jit(solution)/shard_map/project/pallas_call | solution.py:180
  52.1 0.0 copy-start.7
  52.1 0.0 collective-permute-done.8.other_hbm.other_ref
  52.1 0.0 copy-start.1
  52.1 2.7 %text_sums.1 = (bf16[2,4096]{1,0:T(2,128)(2,1)S(1)}, bf16[2,4096]{1,0:T(2,128)(2,1)S(1)}) custom-call(s32[256]{0:T(256)S(1)} %copy-done.3, s32[1,256]{1,0:T(1,128)S(1)} %bitcast.24, bf16[256,1024]{1,0:T(8,128)(2,1)S(1)} %copy-done, bf16[4096,256]{1,0:T(8,128)(2,1)S(1)} %bitcast.17, bf16[4096,256]{1,0:T(8,128)(2,1)S(1)} %collective-permute-done.8.other_hbm.other_ref), custom_call_target="tpu_custom_call" | custom-call | flops 134217728 | bytes 4194304 | tf_op jit(solution)/shard_map/text_sums/pallas_call | solution.py:394
  54.8 0.1 broadcast_in_dim.38
  54.9 1.1 %pad_maximum_fusion = bf16[16,136,256]{2,1,0:T(8,128)(2,1)} fusion(bf16[16,2,256]{2,1,0:T(2,128)(2,1)S(1)} %bitcast.22, bf16[16,2,256]{2,1,0:T(2,128)(2,1)S(1)} %bitcast.21, bf16[16,132,256]{2,1,0:T(8,128)(2,1)S(1)} %broadcast_in_dim.38), kind=kLoop, calls=%fused_computation | loop fusion | flops 3342336 | bytes 2228224 | tf_op jit(solution)/shard_map/concatenate | solution.py:571
  56.0 6.5 %all-to-all-start.1 = ((bf16[16,136,256]{2,1,0:T(8,128)(2,1)}), bf16[16,136,256]{2,1,0:T(8,128)(2,1)S(1)}, u32[]{:S(2)}, u32[]{:S(2)}) async-start(bf16[16,136,256]{2,1,0:T(8,128)(2,1)} %pad_maximum_fusion), calls=%async_computation.1 | async-start | bytes 2228224 | tf_op jit(solution)/shard_map/all_to_all | solution.py:492
  62.5 19.6 %attend2.1 = (bf16[128,1024]{1,0:T(8,128)(2,1)}, bf16[128,1024]{1,0:T(8,128)(2,1)}) custom-call(bf16[128,1024]{1,0:T(8,128)(2,1)S(1)} %get-tuple-element.71.own_ref, bf16[128,1024]{1,0:T(8,128)(2,1)} %copy-done.12, bf16[4096,256]{1,0:T(8,128)(2,1)S(1)} %bitcast.18, bf16[4096,256]{1,0:T(8,128)(2,1)} %copy-done.1), custom_call_target="tpu_custom_call" | custom-call | flops 4294967296 | bytes 4194304 | tf_op jit(solution)/shard_map/attend2/pallas_call | solution.py:311
  82.1 0.0 all-to-all-done.1
  82.2 0.1 collective-permute-start.9
  82.3 5.8 %collective-permute-start.10 = (bf16[128,1024]{1,0:T(8,128)(2,1)}, bf16[128,1024]{1,0:T(8,128)(2,1)S(1)}, u32[]{:S(2)}, u32[]{:S(2)}) collective-permute-start(bf16[128,1024]{1,0:T(8,128)(2,1)} %get-tuple-element.62), channel_id=1, source_target_pairs={{124,0},{120,4},{116,8},{112,12},{108,16},{104,20},{100,24},{96,28... | collective-permute-start | bytes 786440 | tf_op jit(solution)/shard_map/ppermute | solution.py:504
  88.1 0.0 collective-permute-done.9
  88.2 0.1 collective-permute-start.11
  88.3 2.7 %collective-permute-start.12 = (f32[256]{0:T(256)S(1)}, f32[256]{0:T(256)S(1)}, u32[]{:S(2)}, u32[]{:S(2)}) collective-permute-start(f32[256]{0:T(256)S(1)} %bitcast.30), channel_id=1, source_target_pairs={{2,0},{3,1},{0,2},{1,3},{6,4},{7,5},{4,6},{5,7},{10,8},{11,9},{8,1... | collective-permute-start | bytes 3080 | tf_op jit(solution)/shard_map/ppermute | solution.py:498
  91.0 1.2 %collective-permute-start.13 = (f32[256]{0:T(256)S(1)}, f32[256]{0:T(256)S(1)}, u32[]{:S(2)}, u32[]{:S(2)}) collective-permute-start(f32[256]{0:T(256)S(1)} %bitcast.31), channel_id=1, source_target_pairs={{3,0},{2,1},{1,2},{0,3},{7,4},{6,5},{5,6},{4,7},{11,8},{10,9},{9,1... | collective-permute-start | bytes 3080 | tf_op jit(solution)/shard_map/ppermute | solution.py:498
  92.1 10.0 %attend3.1 = bf16[132,1024]{1,0:T(8,128)(2,1)} custom-call(bf16[136,1024]{1,0:T(8,128)(2,1)} %copy-done.7, bf16[2176,256]{1,0:T(8,128)(2,1)S(1)} %bitcast.19, bf16[2176,256]{1,0:T(8,128)(2,1)S(1)} %bitcast.25), custom_call_target="tpu_custom_call" | custom-call | flops 3636461568 | bytes 2228224 | tf_op jit(solution)/shard_map/attend3/pallas_call | solution.py:458
  102.2 0.0 collective-permute-done.10
  102.2 0.0 collective-permute-done.11
  102.2 0.0 collective-permute-done.12
  102.2 0.0 collective-permute-done.13
  102.2 0.8 pad_maximum_fusion.1
  103.1 0.6 add_add_fusion
  (19 shorter events, 0.2 us)
Async XLA Ops:
  3.1 7.7 %copy-start.8 = (s32[256]{0:T(256)S(1)}, s32[256]{0:T(256)}, u32[]{:S(2)}) copy-start(s32[256]{0:T(256)} %param.23) | copy-start | bytes 3076
  3.1 7.7 %copy-start.9 = (s32[2]{0:T(128)S(1)}, s32[2]{0:T(128)}, u32[]{:S(2)}) copy-start(s32[2]{0:T(128)} %counts.1) | copy-start | bytes 28
  3.1 11.1 %copy-start = (bf16[256,1024]{1,0:T(8,128)(2,1)S(1)}, bf16[256,1024]{1,0:T(8,128)(2,1)}, u32[]{:S(2)}) copy-start(bf16[256,1024]{1,0:T(8,128)(2,1)} %q_ref.1) | copy-start | bytes 1572868
  3.1 43.2 %all-to-all-start = ((bf16[16,256,256]{2,1,0:T(8,128)(2,1)}), bf16[16,256,256]{2,1,0:T(8,128)(2,1)S(1)}, u32[]{:S(2)}, u32[]{:S(2)}) async-start(bf16[16,256,256]{2,1,0:T(8,128)(2,1)} %broadcast_in_dim.34), calls=%async_computation | async-start | bytes 4194304 | tf_op jit(solution)/shard_map/all_to_all | solution.py:492
  10.8 1.2 %copy-start.6 = (bf16[256,2048]{1,0:T(8,128)(2,1)S(1)}, bf16[256,2048]{1,0:T(8,128)(2,1)}, u32[]{:S(2)}) copy-start(bf16[256,2048]{1,0:T(8,128)(2,1)} %hidden_ref.1) | copy-start | bytes 3145732
  13.1 2.7 %collective-permute-start = (bf16[136,2176]{1,0:T(8,128)(2,1)S(1)}, bf16[136,2176]{1,0:T(8,128)(2,1)S(1)}, u32[]{:S(2)}, u32[]{:S(2)}) collective-permute-start(bf16[136,2176]{1,0:T(8,128)(2,1)S(1)} %get-tuple-element.37), channel_id=1, source_target_pairs={{4,0},{0,4},{12,8},{8,12},{20,16},{16,20},{28,24},{24,28},{36,32},... | collective-permute-start | bytes 1775624 | tf_op jit(solution)/shard_map/ppermute | solution.py:481
  16.1 18.6 %collective-permute-start.2 = (bf16[136,1024]{1,0:T(8,128)(2,1)S(1)}, bf16[136,1024]{1,0:T(8,128)(2,1)S(1)}, u32[]{:S(2)}, u32[]{:S(2)}) collective-permute-start(bf16[136,1024]{1,0:T(8,128)(2,1)S(1)} %get-tuple-element.69.refs_1_), channel_id=1, source_target_pairs={{1,0},{2,1},{3,2},{0,3},{5,4},{6,5},{7,6},{4,7},{9,8},{10,9},{11,1... | collective-permute-start | bytes 835592 | tf_op jit(solution)/shard_map/ppermute | solution.py:486
  19.9 17.7 %collective-permute-start.3 = (bf16[136,1024]{1,0:T(8,128)(2,1)S(1)}, bf16[136,1024]{1,0:T(8,128)(2,1)S(1)}, u32[]{:S(2)}, u32[]{:S(2)}) collective-permute-start(bf16[136,1024]{1,0:T(8,128)(2,1)S(1)} %get-tuple-element.69.refs_1_), channel_id=1, source_target_pairs={{3,0},{0,1},{1,2},{2,3},{7,4},{4,5},{5,6},{6,7},{11,8},{8,9},{9,10... | collective-permute-start | bytes 835592 | tf_op jit(solution)/shard_map/ppermute | solution.py:486
  19.9 14.7 %collective-permute-start.1 = (bf16[136,1024]{1,0:T(8,128)(2,1)S(1)}, bf16[136,1024]{1,0:T(8,128)(2,1)S(1)}, u32[]{:S(2)}, u32[]{:S(2)}) collective-permute-start(bf16[136,1024]{1,0:T(8,128)(2,1)S(1)} %get-tuple-element.70.refs_0_), channel_id=1, source_target_pairs={{3,0},{0,1},{1,2},{2,3},{7,4},{4,5},{5,6},{6,7},{11,8},{8,9},{9,10... | collective-permute-start | bytes 835592 | tf_op jit(solution)/shard_map/ppermute | solution.py:486
  19.9 17.7 %collective-permute-start.4 = (bf16[136,1024]{1,0:T(8,128)(2,1)S(1)}, bf16[136,1024]{1,0:T(8,128)(2,1)S(1)}, u32[]{:S(2)}, u32[]{:S(2)}) collective-permute-start(bf16[136,1024]{1,0:T(8,128)(2,1)S(1)} %get-tuple-element.70.refs_0_), channel_id=1, source_target_pairs={{1,0},{2,1},{3,2},{0,3},{5,4},{6,5},{7,6},{4,7},{9,8},{10,9},{11,1... | collective-permute-start | bytes 835592 | tf_op jit(solution)/shard_map/ppermute | solution.py:486
  26.9 18.6 %collective-permute-start.5 = (bf16[128,1024]{1,0:T(8,128)(2,1)S(1)}, bf16[128,1024]{1,0:T(8,128)(2,1)S(1)}, u32[]{:S(2)}, u32[]{:S(2)}) collective-permute-start(bf16[128,1024]{1,0:T(8,128)(2,1)S(1)} %get-tuple-element.42), channel_id=1, source_target_pairs={{124,0},{120,4},{116,8},{112,12},{108,16},{104,20},{100,24},{96,28... | collective-permute-start | bytes 786440 | tf_op jit(solution)/shard_map/ppermute | solution.py:504
  34.6 11.0 %collective-permute-start.6 = (bf16[136,1024]{1,0:T(8,128)(2,1)S(1)}, bf16[136,1024]{1,0:T(8,128)(2,1)S(1)}, u32[]{:S(2)}, u32[]{:S(2)}) collective-permute-start(bf16[136,1024]{1,0:T(8,128)(2,1)S(1)} %collective-permute-done.1.refs_0_), channel_id=1, source_target_pairs={{3,0},{0,1},{1,2},{2,3},{7,4},{4,5},{5,6},{6,7},{11,8},{8,9},{9,10... | collective-permute-start | bytes 835592 | tf_op jit(solution)/shard_map/ppermute | solution.py:486
  34.6 11.6 %collective-permute-start.7 = (bf16[136,1024]{1,0:T(8,128)(2,1)S(1)}, bf16[136,1024]{1,0:T(8,128)(2,1)}, u32[]{:S(2)}, u32[]{:S(2)}) collective-permute-start(bf16[136,1024]{1,0:T(8,128)(2,1)S(1)} %collective-permute-done.2.refs_1_), channel_id=1, source_target_pairs={{1,0},{2,1},{3,2},{0,3},{5,4},{6,5},{7,6},{4,7},{9,8},{10,9},{11,1... | collective-permute-start | bytes 835592 | tf_op jit(solution)/shard_map/ppermute | solution.py:486
  37.6 9.3 %copy-start.2 = (f32[1024]{0:T(1024)S(1)}, f32[1024]{0:T(1024)}, u32[]{:S(2)}) copy-start(f32[1024]{0:T(1024)} %param.18) | copy-start | bytes 12292
  37.7 9.3 %copy-start.4 = (f32[128]{0:T(128)S(1)}, f32[128]{0:T(128)}, u32[]{:S(2)}) copy-start(f32[128]{0:T(128)} %param.20) | copy-start | bytes 1540
  37.7 9.3 %copy-start.5 = (f32[128]{0:T(128)S(1)}, f32[128]{0:T(128)}, u32[]{:S(2)}) copy-start(f32[128]{0:T(128)} %param.22) | copy-start | bytes 1540
  45.6 0.7 copy-start.12
  46.3 0.7 copy-start.10
  46.3 5.8 %collective-permute-start.8 = (bf16[4096,256]{1,0:T(8,128)(2,1)S(1)}, bf16[4096,256]{1,0:T(8,128)(2,1)S(1)}, u32[]{:S(2)}, u32[]{:S(2)}) collective-permute-start(bf16[4096,256]{1,0:T(8,128)(2,1)S(1)} %bitcast.16), channel_id=1, source_target_pairs={{4,0},{0,4},{12,8},{8,12},{20,16},{16,20},{28,24},{24,28},{36,32},... | collective-permute-start | bytes 6291464 | tf_op jit(solution)/shard_map/ppermute | solution.py:481
  47.0 5.2 %copy-start.3 = (s32[256]{0:T(256)S(1)}, s32[256]{0:T(256)}, u32[]{:S(2)}) copy-start(s32[256]{0:T(256)} %text.1) | copy-start | bytes 3076
  52.1 2.7 %copy-start.7 = (bf16[136,1024]{1,0:T(8,128)(2,1)}, bf16[136,1024]{1,0:T(8,128)(2,1)S(1)}, u32[]{:S(2)}) copy-start(bf16[136,1024]{1,0:T(8,128)(2,1)S(1)} %get-tuple-element.59.q_hbm) | copy-start | bytes 835588
  52.1 2.7 %copy-start.1 = (bf16[4096,256]{1,0:T(8,128)(2,1)}, bf16[4096,256]{1,0:T(8,128)(2,1)S(1)}, u32[]{:S(2)}) copy-start(bf16[4096,256]{1,0:T(8,128)(2,1)S(1)} %collective-permute-done.8.other_hbm.other_ref) | copy-start | bytes 6291460
  56.0 26.1 %all-to-all-start.1 = ((bf16[16,136,256]{2,1,0:T(8,128)(2,1)}), bf16[16,136,256]{2,1,0:T(8,128)(2,1)S(1)}, u32[]{:S(2)}, u32[]{:S(2)}) async-start(bf16[16,136,256]{2,1,0:T(8,128)(2,1)} %pad_maximum_fusion), calls=%async_computation.1 | async-start | bytes 2228224 | tf_op jit(solution)/shard_map/all_to_all | solution.py:492
  82.2 6.0 %collective-permute-start.9 = (bf16[16,136,256]{2,1,0:T(8,128)(2,1)S(1)}, bf16[16,136,256]{2,1,0:T(8,128)(2,1)S(1)}, u32[]{:S(2)}, u32[]{:S(2)}) collective-permute-start(bf16[16,136,256]{2,1,0:T(8,128)(2,1)S(1)} %all-to-all-done.1), channel_id=1, source_target_pairs={{4,0},{0,4},{12,8},{8,12},{20,16},{16,20},{28,24},{24,28},{36,32},... | collective-permute-start | bytes 3342344 | tf_op jit(solution)/shard_map/ppermute | solution.py:481
  82.3 19.9 %collective-permute-start.10 = (bf16[128,1024]{1,0:T(8,128)(2,1)}, bf16[128,1024]{1,0:T(8,128)(2,1)S(1)}, u32[]{:S(2)}, u32[]{:S(2)}) collective-permute-start(bf16[128,1024]{1,0:T(8,128)(2,1)} %get-tuple-element.62), channel_id=1, source_target_pairs={{124,0},{120,4},{116,8},{112,12},{108,16},{104,20},{100,24},{96,28... | collective-permute-start | bytes 786440 | tf_op jit(solution)/shard_map/ppermute | solution.py:504
  88.2 14.0 %collective-permute-start.11 = (f32[256]{0:T(256)S(1)}, f32[256]{0:T(256)S(1)}, u32[]{:S(2)}, u32[]{:S(2)}) collective-permute-start(f32[256]{0:T(256)S(1)} %bitcast.29), channel_id=1, source_target_pairs={{1,0},{0,1},{3,2},{2,3},{5,4},{4,5},{7,6},{6,7},{9,8},{8,9},{11,10... | collective-permute-start | bytes 3080 | tf_op jit(solution)/shard_map/ppermute | solution.py:498
  88.3 13.9 %collective-permute-start.12 = (f32[256]{0:T(256)S(1)}, f32[256]{0:T(256)S(1)}, u32[]{:S(2)}, u32[]{:S(2)}) collective-permute-start(f32[256]{0:T(256)S(1)} %bitcast.30), channel_id=1, source_target_pairs={{2,0},{3,1},{0,2},{1,3},{6,4},{7,5},{4,6},{5,7},{10,8},{11,9},{8,1... | collective-permute-start | bytes 3080 | tf_op jit(solution)/shard_map/ppermute | solution.py:498
  91.0 11.3 %collective-permute-start.13 = (f32[256]{0:T(256)S(1)}, f32[256]{0:T(256)S(1)}, u32[]{:S(2)}, u32[]{:S(2)}) collective-permute-start(f32[256]{0:T(256)S(1)} %bitcast.31), channel_id=1, source_target_pairs={{3,0},{2,1},{1,2},{0,3},{7,4},{6,5},{5,6},{4,7},{11,8},{10,9},{9,1... | collective-permute-start | bytes 3080 | tf_op jit(solution)/shard_map/ppermute | solution.py:498
  92.1 10.1 %copy-start.11 = (bf16[128,1024]{1,0:T(8,128)(2,1)S(1)}, bf16[128,1024]{1,0:T(8,128)(2,1)}, u32[]{:S(2)}) copy-start(bf16[128,1024]{1,0:T(8,128)(2,1)} %get-tuple-element.58) | copy-start | bytes 786436
